TPU v7x, 32 devices: a whole 2x2x4 slice. The times are simulated.
32 devices in a mesh: dp: 4 (over z), seq: 8 (over y, x, core).
Axes of the slice: x: 2, y: 2, z: 4, core: 2. Of those that a mesh axis runs over, the one named last changes fastest.
Arguments:
- query_rows: bfloat16 [4, 3072, 1024], P('dp', 'seq'), may hold values from -48 to 48
- key_rows: bfloat16 [4, 3072, 1024], P('dp', 'seq'), may hold values from -8 to 8
- value_rows: bfloat16 [4, 3072, 1024], P('dp', 'seq'), may hold values from -6 to 6
- scale_end: int32 [3072], P('seq'), may hold values from 1 to 3072, as said below
- out_weight: bfloat16 [1024, 2048], replicated, may hold values from -0.8984375 to 0.8984375
- grad_out: bfloat16 [4, 3072, 2048], P('dp', 'seq'), may hold values from -1.5 to 1.5
Outputs:
- mixed_out: bfloat16 [4, 3072, 2048], P('dp', 'seq')
- out_grad: float32 [1024, 2048], P(('dp', 'seq'))
Inputs may be any that keep to these rules, and one draw needn't show every extreme that they name: scale_end is constant over each of 4 scales of consecutive tokens, equals the index one past the scale's last token (so scale_end[t] > t), never falls, and is 3072 on the last scale; the same for every image.
All inputs are finite; a program needn't handle non-finite values.
Results may differ from a plain program's by a relative error of at most 0.014.
Values may be sent and summed in bfloat16 or wider, within the bound.
No kernel may reach another device: no remote copies, remote signals or barrier semaphores. Data moves between devices by JAX's collectives and lax.ppermute only.
A program may use at most 256 MiB of HBM per device.

v0:
```python
import functools

import jax
import jax.numpy as jnp
from jax import lax
from jax.experimental import pallas as pl
from jax.experimental.pallas import tpu as pltpu
from jax.sharding import PartitionSpec as P


HEAD = 128
FLOOR = -1e30
SCALES = 4
LOG2E = 1.4426950408889634


HBM = pl.BlockSpec(memory_space=pltpu.HBM)
VMEM = pl.BlockSpec(memory_space=pltpu.VMEM)
SMEM = pl.BlockSpec(memory_space=pltpu.SMEM)


def place():
    index = lax.axis_index("seq")
    return index // 2, index % 2


def params(mebibytes):
    return pltpu.CompilerParams(vmem_limit_bytes=mebibytes * 1024 * 1024)


def cut(sources, chips, width):
    row_count = sources[0].shape[0]
    count = len(sources)

    def kernel(*refs):
        ins, outs, sems = refs[:count], refs[count:-1], refs[-1]
        chip, _ = place()
        copies = []
        for away in reversed(range(chips)):
            columns = pl.ds(pl.multiple_of((chip ^ away) * width, width), width)
            for at, source in enumerate(ins):
                copies.append(
                    pltpu.make_async_copy(
                        source.at[:, columns],
                        outs[away].at[:, at * width : (at + 1) * width],
                        sems.at[len(copies)],
                    )
                )
        for copy in copies:
            copy.start()
        for copy in copies:
            copy.wait()

    shape = jax.ShapeDtypeStruct((row_count, count * width), sources[0].dtype)
    return pl.pallas_call(
        kernel,
        out_shape=[shape] * chips,
        in_specs=[HBM] * count,
        out_specs=[VMEM] * chips,
        scratch_shapes=[pltpu.SemaphoreType.DMA((count * chips,))],
        compiler_params=params(16),
        name="cut",
    )(*(pltpu.with_memory_space_constraint(source, pltpu.HBM) for source in sources))


def assemble(near, far, chips):
    row_count, wide = near[0].shape

    def kernel(*refs):
        pieces, out = (refs[:chips], refs[chips : 2 * chips]), refs[2 * chips]
        chip, core = place()
        for away in range(chips):
            for side in range(2):
                at = (chip ^ away) * 2 + (core ^ side)
                rows = pl.ds(pl.multiple_of(at * row_count, row_count), row_count)
                out[rows, :] = pieces[side][away][...]

    return pl.pallas_call(
        kernel,
        out_shape=jax.ShapeDtypeStruct((2 * chips * row_count, wide), near[0].dtype),
        in_specs=[VMEM] * (2 * chips),
        out_specs=VMEM,
        compiler_params=params(16),
        name="assemble",
    )(*near, *far)


def attend(queries, ends, aways, both, width):
    row_count = queries[0].shape[0]
    total = both.shape[0]
    heads = width // HEAD
    count = len(queries)
    step_k = total // 4
    scale = float(HEAD) ** -0.5 * LOG2E

    def kernel(*refs):
        ends_in = refs[:count]
        q_in = refs[count : 2 * count]
        both_ref = refs[2 * count]
        outs = refs[2 * count + 1 : 3 * count + 1]
        qbuf, obuf, sbuf, sums, tallies, tops = refs[3 * count + 1 :]
        chip, core = place()

        def part(index, room, base, steps):
            shifts, factors = [], []
            for head in range(heads):
                columns = slice(head * HEAD, (head + 1) * HEAD)
                query = qbuf[index, :, columns]
                top = None
                for at in range(base, base + steps * step_k, step_k):
                    score = lax.dot_general(
                        query,
                        both_ref[at : at + step_k, columns],
                        (((1,), (1,)), ((), ())),
                        preferred_element_type=jnp.float32,
                    )
                    for key in range(0, step_k, HEAD):
                        piece = jnp.where(room > at + key, score[:, key : key + HEAD], FLOOR)
                        sbuf[head, :, at - base + key : at - base + key + HEAD] = piece
                        top = piece if top is None else jnp.maximum(top, piece)
                shift = jnp.broadcast_to(jnp.max(top, axis=1, keepdims=True), top.shape) * scale
                if base:
                    before = tops[head]
                    shift = jnp.maximum(before, shift)
                    factors.append(jnp.exp2(before - shift))
                shifts.append(shift)
            for head in range(heads):
                tally = acc = None
                for at in range(base, base + steps * step_k, step_k):
                    weights = []
                    for key in range(0, step_k, HEAD):
                        piece = sbuf[head, :, at - base + key : at - base + key + HEAD]
                        piece = jnp.exp2(piece * scale - shifts[head])
                        tally = piece if tally is None else tally + piece
                        weights.append(piece.astype(jnp.bfloat16))
                    product = jnp.dot(
                        jnp.concatenate(weights, axis=1),
                        both_ref[at : at + step_k, width + head * HEAD : width + (head + 1) * HEAD],
                        preferred_element_type=jnp.float32,
                    )
                    acc = product if acc is None else acc + product
                if base:
                    acc = acc + sums[head] * factors[head]
                    tally = tally + tallies[head] * factors[head]
                sums[head], tallies[head], tops[head] = acc, tally, shifts[head]

        starts, limits = [], []
        for index, away in enumerate(aways):
            qbuf[index] = q_in[index][...]
            start = ((chip ^ away) * 2 + core) * row_count
            limit = [ends_in[index][0]]
            for _ in range(SCALES - 1):
                limit.append(ends_in[index][jnp.minimum(limit[-1] - start, row_count - 1)])
            starts.append(start)
            limits.append(limit)

        def turn(index, carry):
            def pick(values):
                value = values[0]
                for at in range(1, count):
                    value = jnp.where(index == at, values[at], value)
                return value

            limit = [pick([one[at] for one in limits]) for at in range(SCALES)]
            needed = (limit[-1] + step_k - 1) // step_k
            token = pick(starts) + lax.broadcasted_iota(jnp.int32, (row_count, HEAD), 0)
            bound = jnp.full((row_count, HEAD), limit[-1], jnp.int32)
            for value in reversed(limit[:-1]):
                bound = jnp.where(token < value, value, bound)
            room = bound - lax.broadcasted_iota(jnp.int32, (row_count, HEAD), 1)
            for test, base, steps in (
                (needed == 1, 0, 1),
                (needed >= 2, 0, 2),
                (needed == 3, 2 * step_k, 1),
                (needed == 4, 2 * step_k, 2),
            ):

                @pl.when(test)
                def _(base=base, steps=steps):
                    part(index, room, base, steps)

            for head in range(heads):
                obuf[index, :, head * HEAD : (head + 1) * HEAD] = (
                    sums[head] / jnp.sum(tallies[head], axis=1, keepdims=True)
                ).astype(obuf.dtype)
            return carry

        lax.fori_loop(0, count, turn, 0)
        for index in range(count):
            outs[index][...] = obuf[index]

    state = pltpu.VMEM((heads, row_count, HEAD), jnp.float32)
    return pl.pallas_call(
        kernel,
        out_shape=[jax.ShapeDtypeStruct((row_count, width), jnp.bfloat16)] * count,
        in_specs=[SMEM] * count + [VMEM] * (count + 1),
        out_specs=[VMEM] * count,
        scratch_shapes=[
            pltpu.VMEM((count, row_count, width), jnp.bfloat16),
            pltpu.VMEM((count, row_count, width), jnp.bfloat16),
            pltpu.VMEM((heads, row_count, total // 2), jnp.float32),
            state,
            state,
            state,
        ],
        compiler_params=params(30),
        cost_estimate=pl.CostEstimate(
            flops=4 * count * row_count * total * width,
            bytes_accessed=4 * total * width,
            transcendentals=count * row_count * total * heads,
        ),
        name="attend",
    )(*ends, *queries, both)


def weight_gradient(near, far, grad_near, grad_far, chips, width, planes, split):
    row_count = near[0].shape[0]
    full = chips * width
    out_width = grad_near.shape[1]
    group = full // (planes * chips * 2)

    def kernel(*refs):
        pieces = (refs[0:chips], refs[chips : 2 * chips])
        grads = refs[2 * chips : 2 * chips + 2]
        by_plane = refs[2 * chips + 2 : 2 * chips + 2 + planes]
        by_chip = refs[2 * chips + 2 + planes : 3 * chips + 2 + planes]
        turned, left = refs[3 * chips + 2 + planes :]
        chip, core = place()
        here = lax.axis_index("dp")
        for side in range(2):
            for away in range(chips):
                start = pl.multiple_of((chip ^ away) * width, width)
                turned[pl.ds(start, width), side * row_count : (side + 1) * row_count] = (
                    pieces[side][away][...].T
                )

        def product(outs, columns, picks):
            for out, starts in zip(outs, picks):
                for at, start in enumerate(starts):
                    rows = pl.ds(pl.multiple_of((start * 2 + core) * group, group), group)
                    left[at * group : (at + 1) * group, :] = turned[rows, :]
                size = len(starts) * group
                value = jnp.dot(
                    left[:size, :row_count], grads[0][:, columns], preferred_element_type=jnp.float32
                ) + jnp.dot(
                    left[:size, row_count:], grads[1][:, columns], preferred_element_type=jnp.float32
                )
                out[...] = value.astype(out.dtype)

        product(
            by_plane,
            slice(split, out_width),
            [[(here ^ far_) * chips + at for at in range(chips)] for far_ in range(planes)],
        )
        product(
            by_chip,
            slice(0, split),
            [[at * chips + (chip ^ far_) for at in range(planes)] for far_ in range(chips)],
        )

    def shape(rows, columns, away):
        return jax.ShapeDtypeStruct((rows, columns), jnp.float32 if away == 0 else jnp.bfloat16)

    outs = pl.pallas_call(
        kernel,
        out_shape=[shape(chips * group, out_width - split, away) for away in range(planes)]
        + [shape(planes * group, split, away) for away in range(chips)],
        in_specs=[VMEM] * (2 * chips + 2),
        out_specs=[VMEM] * (planes + chips),
        scratch_shapes=[
            pltpu.VMEM((full, 2 * row_count), jnp.bfloat16),
            pltpu.VMEM((max(planes, chips) * group, 2 * row_count), jnp.bfloat16),
        ],
        compiler_params=params(32),
        cost_estimate=pl.CostEstimate(
            flops=2 * full * row_count * out_width,
            bytes_accessed=4 * row_count * out_width,
            transcendentals=0,
        ),
        name="weight_gradient",
    )(*near, *far, grad_near, grad_far)
    return outs[:planes], outs[planes:]


def project(pieces, out_weight, chips, width):
    row_count = pieces[0].shape[0]
    out_width = out_weight.shape[1]

    def kernel(*refs):
        ins, weight, out = refs[:chips], refs[chips], refs[chips + 1]
        chip, _ = place()
        step = min(out_width, 512)
        for column in range(0, out_width, step):
            value = None
            for away in range(chips):
                start = pl.multiple_of((chip ^ away) * width, width)
                part = jnp.dot(
                    ins[away][...],
                    weight[pl.ds(start, width), column : column + step],
                    preferred_element_type=jnp.float32,
                )
                value = part if value is None else value + part
            out[:, column : column + step] = value.astype(out.dtype)

    return pl.pallas_call(
        kernel,
        out_shape=jax.ShapeDtypeStruct((row_count, out_width), jnp.bfloat16),
        in_specs=[VMEM] * (chips + 1),
        out_specs=VMEM,
        compiler_params=params(24),
        cost_estimate=pl.CostEstimate(
            flops=2 * row_count * out_weight.size,
            bytes_accessed=2 * out_weight.size,
            transcendentals=0,
        ),
        name="project",
    )(*pieces, out_weight)


def add_up(own, others, axis, size):
    group = own.shape[0] // size

    def kernel(*refs):
        ins, outs = refs[: 1 + len(others)], refs[1 + len(others) :]
        here = lax.axis_index("dp") if axis == "dp" else place()[0]
        for away in range(size):
            rows = pl.ds(pl.multiple_of((here ^ away) * group, group), group)
            value = ins[0][rows, :]
            for ref in ins[1:]:
                value = value + ref[rows, :].astype(jnp.float32)
            outs[away][...] = value.astype(outs[away].dtype)

    return pl.pallas_call(
        kernel,
        out_shape=[
            jax.ShapeDtypeStruct(
                (group, own.shape[1]), jnp.float32 if away == 0 else jnp.bfloat16
            )
            for away in range(size)
        ],
        in_specs=[VMEM] * (1 + len(others)),
        out_specs=[VMEM] * size,
        compiler_params=params(16),
        name="add_up",
    )(own, *others)


def finish(lefts, rights):
    rows, split = lefts[0].shape
    width = split + rights[0].shape[1]

    def kernel(*refs):
        ins, out = refs[:-1], refs[-1]
        for group, columns in (
            (ins[: len(lefts)], slice(0, split)),
            (ins[len(lefts) :], slice(split, width)),
        ):
            value = group[0][...]
            for ref in group[1:]:
                value = value + ref[...].astype(jnp.float32)
            out[:, columns] = value

    return pl.pallas_call(
        kernel,
        out_shape=jax.ShapeDtypeStruct((rows, width), jnp.float32),
        in_specs=[VMEM] * (len(lefts) + len(rights)),
        out_specs=VMEM,
        compiler_params=params(16),
        name="finish",
    )(*lefts, *rights)


def body(seq, planes, query_rows, key_rows, value_rows, scale_end, out_weight, grad_out):
    chips = seq // 2
    full = query_rows.shape[2]
    width = full // chips

    def over(axis, size, value, mask):
        return lax.ppermute(value, axis, [(i, i ^ mask) for i in range(size)])

    def other_core(value):
        return over("seq", seq, value, 1)

    def spread(pieces):
        return [pieces[0]] + [over("seq", seq, pieces[away], 2 * away) for away in range(1, chips)]

    def meet(pieces):
        return [pieces[0]] + [over("dp", planes, pieces[away], away) for away in range(1, planes)]

    near = spread(cut([key_rows[0], value_rows[0]], chips, width))
    queries = spread(cut([query_rows[0]], chips, width))
    ends = spread([scale_end] * chips)
    far = [other_core(piece) for piece in near]
    grad_near = grad_out[0]
    grad_far = other_core(grad_near)
    both = assemble(near, far, chips)
    mine = [None] * chips
    for aways in ([chips - 1], list(range(1, chips - 1)), [0]):
        results = attend(
            [queries[i] for i in aways], [ends[i] for i in aways], aways, both, width
        )
        for away, piece in zip(aways, results):
            mine[away] = over("seq", seq, piece, 2 * away) if away else piece
    others = [other_core(piece) for piece in mine]
    out_width = out_weight.shape[1]
    split = out_width * 11 // 16
    by_plane, by_chip = weight_gradient(
        mine, others, grad_near, grad_far, chips, width, planes, split
    )
    met = meet(by_plane)
    gathered = spread(by_chip)
    mixed_out = project(mine, out_weight, chips, width)[None]
    lefts = meet(add_up(gathered[0], gathered[1:], "dp", planes))
    rights = spread(add_up(met[0], met[1:], "seq", chips))
    return mixed_out, finish(lefts, rights)


def solution(mesh):
    placed = (
        P("dp", "seq", None),
        P("dp", "seq", None),
        P("dp", "seq", None),
        P("seq"),
        P(),
        P("dp", "seq", None),
    )
    seq, planes = mesh.shape["seq"], mesh.shape["dp"]
    return jax.shard_map(
        functools.partial(body, seq, planes),
        mesh=mesh,
        in_specs=placed,
        out_specs=(P("dp", "seq", None), P(("dp", "seq"), None)),
        check_vma=False,
    )
```

profile of v0, /device:TPU:0, one launch (start us, length us, event | category | flops | bytes accessed | tf_op | source)
XLA Modules:
  0.0 98.7 jit_solution(6690079686444824073)
XLA Ops:
  0.7 1.7 %cut.3 = (bf16[384,512]{1,0:T(8,128)(2,1)S(1)}, bf16[384,512]{1,0:T(8,128)(2,1)S(1)}, bf16[384,512]{1,0:T(8,128)(2,1)S(1)}, bf16[384,512]{1,0:T(8,128)(2,1)S(1)}) custom-call(bf16[384,1024]{1,0:T(8,128)(2,1)} %bitcast.8, bf16[384,1024]{1,0:T(8,128)(2,1)} %bitcast.9), custom_call_target="tpu_custom_call" | custom-call | tf_op jit(solution)/shard_map/cut/pallas_call | solution.py:55
  2.3 3.0 %collective-permute-start = (bf16[384,512]{1,0:T(8,128)(2,1)S(1)}, bf16[384,512]{1,0:T(8,128)(2,1)S(1)}, u32[]{:S(2)}, u32[]{:S(2)}) collective-permute-start(bf16[384,512]{1,0:T(8,128)(2,1)S(1)} %get-tuple-element.30), channel_id=1, source_target_pairs={{0,2},{1,3},{2,0},{3,1},{4,6},{5,7},{6,4},{7,5},{8,10},{9,11},{10,... | collective-permute-start | bytes 1179656 | tf_op jit(solution)/shard_map/ppermute | solution.py:379
  5.4 1.5 %collective-permute-start.1 = (bf16[384,512]{1,0:T(8,128)(2,1)S(1)}, bf16[384,512]{1,0:T(8,128)(2,1)S(1)}, u32[]{:S(2)}, u32[]{:S(2)}) collective-permute-start(bf16[384,512]{1,0:T(8,128)(2,1)S(1)} %get-tuple-element.31), channel_id=1, source_target_pairs={{0,4},{1,5},{2,6},{3,7},{4,0},{5,1},{6,2},{7,3},{8,12},{9,13},{10,... | collective-permute-start | bytes 1179656 | tf_op jit(solution)/shard_map/ppermute | solution.py:379
  7.1 8.2 %collective-permute-done.refs_1_ = bf16[384,512]{1,0:T(8,128)(2,1)S(1)} collective-permute-done((bf16[384,512]{1,0:T(8,128)(2,1)S(1)}, bf16[384,512]{1,0:T(8,128)(2,1)S(1)}, u32[]{:S(2)}, u32[]{:S(2)}) %collective-permute-start) | collective-permute-done | bytes 393248 | tf_op jit(solution)/shard_map/ppermute | solution.py:379
  15.3 10.0 %collective-permute-done.1.refs_2_ = bf16[384,512]{1,0:T(8,128)(2,1)S(1)} collective-permute-done((bf16[384,512]{1,0:T(8,128)(2,1)S(1)}, bf16[384,512]{1,0:T(8,128)(2,1)S(1)}, u32[]{:S(2)}, u32[]{:S(2)}) %collective-permute-start.1) | collective-permute-done | bytes 393248 | tf_op jit(solution)/shard_map/ppermute | solution.py:379
  25.8 1.3 %cut.2 = (bf16[384,256]{1,0:T(8,128)(2,1)S(1)}, bf16[384,256]{1,0:T(8,128)(2,1)S(1)}, bf16[384,256]{1,0:T(8,128)(2,1)S(1)}, bf16[384,256]{1,0:T(8,128)(2,1)S(1)}) custom-call(bf16[384,1024]{1,0:T(8,128)(2,1)} %bitcast.10), custom_call_target="tpu_custom_call" | custom-call | tf_op jit(solution)/shard_map/cut/pallas_call | solution.py:55
  27.1 1.6 %collective-permute-start.10 = (bf16[384,256]{1,0:T(8,128)(2,1)S(1)}, bf16[384,256]{1,0:T(8,128)(2,1)S(1)}, u32[]{:S(2)}, u32[]{:S(2)}) collective-permute-start(bf16[384,256]{1,0:T(8,128)(2,1)S(1)} %get-tuple-element.34), channel_id=1, source_target_pairs={{0,4},{1,5},{2,6},{3,7},{4,0},{5,1},{6,2},{7,3},{8,12},{9,13},{10,... | collective-permute-start | bytes 589832 | tf_op jit(solution)/shard_map/ppermute | solution.py:379
  29.2 1.5 %collective-permute-start.7 = (s32[384]{0:T(512)S(1)}, s32[384]{0:T(512)S(1)}, u32[]{:S(2)}, u32[]{:S(2)}) collective-permute-start(s32[384]{0:T(512)S(1)} %copy-done.2), channel_id=1, source_target_pairs={{0,2},{1,3},{2,0},{3,1},{4,6},{5,7},{6,4},{7,5},{8,10},{9,11},{10,... | collective-permute-start | bytes 4616 | tf_op jit(solution)/shard_map/ppermute | solution.py:379
  31.5 3.8 %collective-permute-done.7.refs_0_ = s32[384]{0:T(512)S(1)} collective-permute-done((s32[384]{0:T(512)S(1)}, s32[384]{0:T(512)S(1)}, u32[]{:S(2)}, u32[]{:S(2)}) %collective-permute-start.7) | collective-permute-done | bytes 1568 | tf_op jit(solution)/shard_map/ppermute | solution.py:379
  35.6 2.6 %collective-permute-start.14 = (bf16[384,256]{1,0:T(8,128)(2,1)S(1)}, bf16[384,256]{1,0:T(8,128)(2,1)S(1)}, u32[]{:S(2)}, u32[]{:S(2)}) collective-permute-start(bf16[384,256]{1,0:T(8,128)(2,1)S(1)} %get-tuple-element.37), channel_id=1, source_target_pairs={{0,6},{1,7},{2,4},{3,5},{4,2},{5,3},{6,0},{7,1},{8,14},{9,15},{10,... | collective-permute-start | bytes 589832 | tf_op jit(solution)/shard_map/ppermute | solution.py:379
  38.2 8.3 %attend.4 = (bf16[384,256]{1,0:T(8,128)(2,1)S(1)}, bf16[384,256]{1,0:T(8,128)(2,1)S(1)}) custom-call(s32[384]{0:T(512)S(1)} %collective-permute-done.7.refs_0_, s32[384]{0:T(512)S(1)} %collective-permute-done.8.refs_1_, bf16[384,256]{1,0:T(8,128)(2,1)S(1)} %collective-permute-done.9.refs_2_, bf16[384,256]{1,0:T(8,128)(2,1)S(1)} %collective-permute-done.10.refs_3_, ...), custom_call_target="tpu_custom_call" | custom-call | flops 2415919104 | bytes 3145728 | tf_op jit(solution)/shard_map/attend/pallas_call | solution.py:193
  46.6 0.9 collective-permute-start.12
  47.5 4.6 %attend.5 = bf16[384,256]{1,0:T(8,128)(2,1)S(1)} custom-call(s32[384]{0:T(512)S(1)} %collective-permute-done.13.refs_0_, bf16[384,256]{1,0:T(8,128)(2,1)S(1)} %collective-permute-done.14.refs_1_, bf16[3072,512]{1,0:T(8,128)(2,1)S(1)} %assemble.1.refs_2_.refs_4_), custom_call_target="tpu_custom_call" | custom-call | flops 1207959552 | bytes 3145728 | tf_op jit(solution)/shard_map/attend/pallas_call | solution.py:193
  52.9 2.8 %attend.3.refs_0_ = bf16[384,256]{1,0:T(8,128)(2,1)S(1)} custom-call(s32[384]{0:T(512)S(1)} %copy-done.2, bf16[384,256]{1,0:T(8,128)(2,1)S(1)} %get-tuple-element.28.refs_1_, bf16[3072,512]{1,0:T(8,128)(2,1)S(1)} %assemble.1.refs_2_.refs_4_), custom_call_target="tpu_custom_call" | custom-call | flops 1207959552 | bytes 3145728 | tf_op jit(solution)/shard_map/attend/pallas_call | solution.py:193
  56.3 2.4 %collective-permute-done.15.refs_3_ = bf16[384,256]{1,0:T(8,128)(2,1)S(1)} collective-permute-done((bf16[384,256]{1,0:T(8,128)(2,1)S(1)}, bf16[384,256]{1,0:T(8,128)(2,1)S(1)}, u32[]{:S(2)}, u32[]{:S(2)}) %collective-permute-start.15) | collective-permute-done | bytes 196640 | tf_op jit(solution)/shard_map/ppermute | solution.py:379
  58.7 1.4 %collective-permute-done.19.refs_7_ = bf16[384,256]{1,0:T(8,128)(2,1)S(1)} collective-permute-done((bf16[384,256]{1,0:T(8,128)(2,1)S(1)}, bf16[384,256]{1,0:T(8,128)(2,1)S(1)}, u32[]{:S(2)}, u32[]{:S(2)}) %collective-permute-start.19) | collective-permute-done | bytes 196640 | tf_op jit(solution)/shard_map/ppermute | solution.py:379
  60.2 3.1 %weight_gradient.1 = (f32[128,640]{1,0:T(8,128)S(1)}, bf16[128,640]{1,0:T(8,128)(2,1)S(1)}, bf16[128,640]{1,0:T(8,128)(2,1)S(1)}, bf16[128,640]{1,0:T(8,128)(2,1...) custom-call(bf16[384,256]{1,0:T(8,128)(2,1)S(1)} %attend.3.refs_0_, ...), custom_call_target="tpu_custom_call" | custom-call | flops 1610612736 | bytes 3145728 | tf_op jit(solution)/shard_map/weight_gradient/pallas_call | solution.py:264
  63.3 1.8 %collective-permute-start.27 = (bf16[128,640]{1,0:T(8,128)(2,1)S(1)}, bf16[128,640]{1,0:T(8,128)(2,1)S(1)}, u32[]{:S(2)}, u32[]{:S(2)}) collective-permute-start(bf16[128,640]{1,0:T(8,128)(2,1)S(1)} %get-tuple-element.47), channel_id=1, source_target_pairs={{0,8},{8,0},{16,24},{24,16},{1,9},{9,1},{17,25},{25,17},{2,10},{10... | collective-permute-start | bytes 491528 | tf_op jit(solution)/shard_map/ppermute | solution.py:379
  65.1 1.5 %collective-permute-start.21 = (bf16[128,1408]{1,0:T(8,128)(2,1)S(1)}, bf16[128,1408]{1,0:T(8,128)(2,1)S(1)}, u32[]{:S(2)}, u32[]{:S(2)}) collective-permute-start(bf16[128,1408]{1,0:T(8,128)(2,1)S(1)} %get-tuple-element.39), channel_id=1, source_target_pairs={{0,2},{1,3},{2,0},{3,1},{4,6},{5,7},{6,4},{7,5},{8,10},{9,11},{10,... | collective-permute-start | bytes 1081352 | tf_op jit(solution)/shard_map/ppermute | solution.py:379
  66.6 1.0 collective-permute-start.22
  67.6 1.0 %collective-permute-start.23 = (bf16[128,1408]{1,0:T(8,128)(2,1)S(1)}, bf16[128,1408]{1,0:T(8,128)(2,1)S(1)}, u32[]{:S(2)}, u32[]{:S(2)}) collective-permute-start(bf16[128,1408]{1,0:T(8,128)(2,1)S(1)} %get-tuple-element.41), channel_id=1, source_target_pairs={{0,6},{1,7},{2,4},{3,5},{4,2},{5,3},{6,0},{7,1},{8,14},{9,15},{10,... | collective-permute-start | bytes 1081352 | tf_op jit(solution)/shard_map/ppermute | solution.py:379
  68.6 2.6 %collective-permute-start.28 = (bf16[128,640]{1,0:T(8,128)(2,1)S(1)}, bf16[128,640]{1,0:T(8,128)(2,1)S(1)}, u32[]{:S(2)}, u32[]{:S(2)}) collective-permute-start(bf16[128,640]{1,0:T(8,128)(2,1)S(1)} %get-tuple-element.48), channel_id=1, source_target_pairs={{0,16},{8,24},{16,0},{24,8},{1,17},{9,25},{17,1},{25,9},{2,18},{10... | collective-permute-start | bytes 491528 | tf_op jit(solution)/shard_map/ppermute | solution.py:379
  71.2 2.2 %collective-permute-start.29 = (bf16[128,640]{1,0:T(8,128)(2,1)S(1)}, bf16[128,640]{1,0:T(8,128)(2,1)S(1)}, u32[]{:S(2)}, u32[]{:S(2)}) collective-permute-start(bf16[128,640]{1,0:T(8,128)(2,1)S(1)} %get-tuple-element.49), channel_id=1, source_target_pairs={{0,24},{8,16},{16,8},{24,0},{1,25},{9,17},{17,9},{25,1},{2,26},{10... | collective-permute-start | bytes 491528 | tf_op jit(solution)/shard_map/ppermute | solution.py:379
  73.3 9.0 %collective-permute-done.28.refs_2_ = bf16[128,640]{1,0:T(8,128)(2,1)S(1)} collective-permute-done((bf16[128,640]{1,0:T(8,128)(2,1)S(1)}, bf16[128,640]{1,0:T(8,128)(2,1)S(1)}, u32[]{:S(2)}, u32[]{:S(2)}) %collective-permute-start.28) | collective-permute-done | bytes 163872 | tf_op jit(solution)/shard_map/ppermute | solution.py:379
  82.5 1.7 %collective-permute-start.30 = (bf16[32,640]{1,0:T(8,128)(2,1)S(1)}, bf16[32,640]{1,0:T(8,128)(2,1)S(1)}, u32[]{:S(2)}, u32[]{:S(2)}) collective-permute-start(bf16[32,640]{1,0:T(8,128)(2,1)S(1)} %get-tuple-element.51), channel_id=1, source_target_pairs={{0,2},{1,3},{2,0},{3,1},{4,6},{5,7},{6,4},{7,5},{8,10},{9,11},{10,... | collective-permute-start | bytes 122888 | tf_op jit(solution)/shard_map/ppermute | solution.py:379
  84.2 1.0 collective-permute-start.31
  85.1 0.9 collective-permute-start.32
  86.2 3.3 %collective-permute-start.24 = (bf16[32,1408]{1,0:T(8,128)(2,1)S(1)}, bf16[32,1408]{1,0:T(8,128)(2,1)S(1)}, u32[]{:S(2)}, u32[]{:S(2)}) collective-permute-start(bf16[32,1408]{1,0:T(8,128)(2,1)S(1)} %get-tuple-element.43), channel_id=1, source_target_pairs={{0,8},{8,0},{16,24},{24,16},{1,9},{9,1},{17,25},{25,17},{2,10},{10... | collective-permute-start | bytes 270344 | tf_op jit(solution)/shard_map/ppermute | solution.py:379
  89.5 1.2 %collective-permute-start.25 = (bf16[32,1408]{1,0:T(8,128)(2,1)S(1)}, bf16[32,1408]{1,0:T(8,128)(2,1)S(1)}, u32[]{:S(2)}, u32[]{:S(2)}) collective-permute-start(bf16[32,1408]{1,0:T(8,128)(2,1)S(1)} %get-tuple-element.44), channel_id=1, source_target_pairs={{0,16},{8,24},{16,0},{24,8},{1,17},{9,25},{17,1},{25,9},{2,18},{10... | collective-permute-start | bytes 270344 | tf_op jit(solution)/shard_map/ppermute | solution.py:379
  90.7 1.4 %collective-permute-start.26 = (bf16[32,1408]{1,0:T(8,128)(2,1)S(1)}, bf16[32,1408]{1,0:T(8,128)(2,1)S(1)}, u32[]{:S(2)}, u32[]{:S(2)}) collective-permute-start(bf16[32,1408]{1,0:T(8,128)(2,1)S(1)} %get-tuple-element.45), channel_id=1, source_target_pairs={{0,24},{8,16},{16,8},{24,0},{1,25},{9,17},{17,9},{25,1},{2,26},{10... | collective-permute-start | bytes 270344 | tf_op jit(solution)/shard_map/ppermute | solution.py:379
  92.0 2.9 %project.1 = bf16[384,2048]{1,0:T(8,128)(2,1)} custom-call(bf16[384,256]{1,0:T(8,128)(2,1)S(1)} %attend.3.refs_0_, bf16[384,256]{1,0:T(8,128)(2,1)S(1)} %collective-permute-done.11.refs_1_, bf16[384,256]{1,0:T(8,128)(2,1)S(1)} %collective-permute-done.12.refs_2_, bf16[384,256]{1,0:T(8,128)(2,1)S(1)} %collective-permute-done.15.refs_3_, ...), custom_call_target="tpu_custom_call" | custom-call | flops 1610612736 | bytes 4194304 | tf_op jit(solution)/shard_map/project/pallas_call | solution.py:305
  95.0 2.9 %collective-permute-done.25.refs_2_ = bf16[32,1408]{1,0:T(8,128)(2,1)S(1)} collective-permute-done((bf16[32,1408]{1,0:T(8,128)(2,1)S(1)}, bf16[32,1408]{1,0:T(8,128)(2,1)S(1)}, u32[]{:S(2)}, u32[]{:S(2)}) %collective-permute-start.25) | collective-permute-done | bytes 90144 | tf_op jit(solution)/shard_map/ppermute | solution.py:379
  (51 shorter events, 4.9 us)
Async XLA Ops:
  2.3 13.0 %collective-permute-start = (bf16[384,512]{1,0:T(8,128)(2,1)S(1)}, bf16[384,512]{1,0:T(8,128)(2,1)S(1)}, u32[]{:S(2)}, u32[]{:S(2)}) collective-permute-start(bf16[384,512]{1,0:T(8,128)(2,1)S(1)} %get-tuple-element.30), channel_id=1, source_target_pairs={{0,2},{1,3},{2,0},{3,1},{4,6},{5,7},{6,4},{7,5},{8,10},{9,11},{10,... | collective-permute-start | bytes 1179656 | tf_op jit(solution)/shard_map/ppermute | solution.py:379
  5.4 54.8 %collective-permute-start.20 = (bf16[384,2048]{1,0:T(8,128)(2,1)S(1)}, bf16[384,2048]{1,0:T(8,128)(2,1)S(1)}, u32[]{:S(2)}, u32[]{:S(2)}) collective-permute-start(bf16[384,2048]{1,0:T(8,128)(2,1)S(1)} %bitcast.5), channel_id=1, source_target_pairs={{0,1},{1,0},{2,3},{3,2},{4,5},{5,4},{6,7},{7,6},{8,9},{9,8},{10,11... | collective-permute-start | bytes 4718600 | tf_op jit(solution)/shard_map/ppermute | solution.py:379
  5.4 20.0 %collective-permute-start.1 = (bf16[384,512]{1,0:T(8,128)(2,1)S(1)}, bf16[384,512]{1,0:T(8,128)(2,1)S(1)}, u32[]{:S(2)}, u32[]{:S(2)}) collective-permute-start(bf16[384,512]{1,0:T(8,128)(2,1)S(1)} %get-tuple-element.31), channel_id=1, source_target_pairs={{0,4},{1,5},{2,6},{3,7},{4,0},{5,1},{6,2},{7,3},{8,12},{9,13},{10,... | collective-permute-start | bytes 1179656 | tf_op jit(solution)/shard_map/ppermute | solution.py:379
  6.9 18.4 %collective-permute-start.2 = (bf16[384,512]{1,0:T(8,128)(2,1)S(1)}, bf16[384,512]{1,0:T(8,128)(2,1)S(1)}, u32[]{:S(2)}, u32[]{:S(2)}) collective-permute-start(bf16[384,512]{1,0:T(8,128)(2,1)S(1)} %get-tuple-element.32), channel_id=1, source_target_pairs={{0,6},{1,7},{2,4},{3,5},{4,2},{5,3},{6,0},{7,1},{8,14},{9,15},{10,... | collective-permute-start | bytes 1179656 | tf_op jit(solution)/shard_map/ppermute | solution.py:379
  7.1 20.0 %collective-permute-start.3 = (bf16[384,512]{1,0:T(8,128)(2,1)S(1)}, bf16[384,512]{1,0:T(8,128)(2,1)S(1)}, u32[]{:S(2)}, u32[]{:S(2)}) collective-permute-start(bf16[384,512]{1,0:T(8,128)(2,1)S(1)} %get-tuple-element.29.refs_0_), channel_id=1, source_target_pairs={{0,1},{1,0},{2,3},{3,2},{4,5},{5,4},{6,7},{7,6},{8,9},{9,8},{10,11... | collective-permute-start | bytes 1179656 | tf_op jit(solution)/shard_map/ppermute | solution.py:379
  15.3 13.4 %collective-permute-start.4 = (bf16[384,512]{1,0:T(8,128)(2,1)S(1)}, bf16[384,512]{1,0:T(8,128)(2,1)S(1)}, u32[]{:S(2)}, u32[]{:S(2)}) collective-permute-start(bf16[384,512]{1,0:T(8,128)(2,1)S(1)} %collective-permute-done.refs_1_), channel_id=1, source_target_pairs={{0,1},{1,0},{2,3},{3,2},{4,5},{5,4},{6,7},{7,6},{8,9},{9,8},{10,11... | collective-permute-start | bytes 1179656 | tf_op jit(solution)/shard_map/ppermute | solution.py:379
  25.3 3.9 %collective-permute-start.5 = (bf16[384,512]{1,0:T(8,128)(2,1)S(1)}, bf16[384,512]{1,0:T(8,128)(2,1)S(1)}, u32[]{:S(2)}, u32[]{:S(2)}) collective-permute-start(bf16[384,512]{1,0:T(8,128)(2,1)S(1)} %collective-permute-done.1.refs_2_), channel_id=1, source_target_pairs={{0,1},{1,0},{2,3},{3,2},{4,5},{5,4},{6,7},{7,6},{8,9},{9,8},{10,11... | collective-permute-start | bytes 1179656 | tf_op jit(solution)/shard_map/ppermute | solution.py:379
  25.3 5.4 %collective-permute-start.6 = (bf16[384,512]{1,0:T(8,128)(2,1)S(1)}, bf16[384,512]{1,0:T(8,128)(2,1)S(1)}, u32[]{:S(2)}, u32[]{:S(2)}) collective-permute-start(bf16[384,512]{1,0:T(8,128)(2,1)S(1)} %collective-permute-done.2.refs_3_), channel_id=1, source_target_pairs={{0,1},{1,0},{2,3},{3,2},{4,5},{5,4},{6,7},{7,6},{8,9},{9,8},{10,11... | collective-permute-start | bytes 1179656 | tf_op jit(solution)/shard_map/ppermute | solution.py:379
  27.1 11.1 %collective-permute-start.10 = (bf16[384,256]{1,0:T(8,128)(2,1)S(1)}, bf16[384,256]{1,0:T(8,128)(2,1)S(1)}, u32[]{:S(2)}, u32[]{:S(2)}) collective-permute-start(bf16[384,256]{1,0:T(8,128)(2,1)S(1)} %get-tuple-element.34), channel_id=1, source_target_pairs={{0,4},{1,5},{2,6},{3,7},{4,0},{5,1},{6,2},{7,3},{8,12},{9,13},{10,... | collective-permute-start | bytes 589832 | tf_op jit(solution)/shard_map/ppermute | solution.py:379
  28.7 9.5 %collective-permute-start.9 = (bf16[384,256]{1,0:T(8,128)(2,1)S(1)}, bf16[384,256]{1,0:T(8,128)(2,1)S(1)}, u32[]{:S(2)}, u32[]{:S(2)}) collective-permute-start(bf16[384,256]{1,0:T(8,128)(2,1)S(1)} %get-tuple-element.33), channel_id=1, source_target_pairs={{0,2},{1,3},{2,0},{3,1},{4,6},{5,7},{6,4},{7,5},{8,10},{9,11},{10,... | collective-permute-start | bytes 589832 | tf_op jit(solution)/shard_map/ppermute | solution.py:379
  29.2 6.0 %collective-permute-start.7 = (s32[384]{0:T(512)S(1)}, s32[384]{0:T(512)S(1)}, u32[]{:S(2)}, u32[]{:S(2)}) collective-permute-start(s32[384]{0:T(512)S(1)} %copy-done.2), channel_id=1, source_target_pairs={{0,2},{1,3},{2,0},{3,1},{4,6},{5,7},{6,4},{7,5},{8,10},{9,11},{10,... | collective-permute-start | bytes 4616 | tf_op jit(solution)/shard_map/ppermute | solution.py:379
  30.7 4.9 %collective-permute-start.8 = (s32[384]{0:T(512)S(1)}, s32[384]{0:T(512)S(1)}, u32[]{:S(2)}, u32[]{:S(2)}) collective-permute-start(s32[384]{0:T(512)S(1)} %copy-done.2), channel_id=1, source_target_pairs={{0,4},{1,5},{2,6},{3,7},{4,0},{5,1},{6,2},{7,3},{8,12},{9,13},{10,... | collective-permute-start | bytes 4616 | tf_op jit(solution)/shard_map/ppermute | solution.py:379
  35.3 12.2 %collective-permute-start.13 = (s32[384]{0:T(512)S(1)}, s32[384]{0:T(512)S(1)}, u32[]{:S(2)}, u32[]{:S(2)}) collective-permute-start(s32[384]{0:T(512)S(1)} %copy-done.2), channel_id=1, source_target_pairs={{0,6},{1,7},{2,4},{3,5},{4,2},{5,3},{6,0},{7,1},{8,14},{9,15},{10,... | collective-permute-start | bytes 4616 | tf_op jit(solution)/shard_map/ppermute | solution.py:379
  35.6 11.9 %collective-permute-start.14 = (bf16[384,256]{1,0:T(8,128)(2,1)S(1)}, bf16[384,256]{1,0:T(8,128)(2,1)S(1)}, u32[]{:S(2)}, u32[]{:S(2)}) collective-permute-start(bf16[384,256]{1,0:T(8,128)(2,1)S(1)} %get-tuple-element.37), channel_id=1, source_target_pairs={{0,6},{1,7},{2,4},{3,5},{4,2},{5,3},{6,0},{7,1},{8,14},{9,15},{10,... | collective-permute-start | bytes 589832 | tf_op jit(solution)/shard_map/ppermute | solution.py:379
  46.5 9.3 %collective-permute-start.11 = (bf16[384,256]{1,0:T(8,128)(2,1)S(1)}, bf16[384,256]{1,0:T(8,128)(2,1)S(1)}, u32[]{:S(2)}, u32[]{:S(2)}) collective-permute-start(bf16[384,256]{1,0:T(8,128)(2,1)S(1)} %get-tuple-element.35), channel_id=1, source_target_pairs={{0,2},{1,3},{2,0},{3,1},{4,6},{5,7},{6,4},{7,5},{8,10},{9,11},{10,... | collective-permute-start | bytes 589832 | tf_op jit(solution)/shard_map/ppermute | solution.py:379
  46.6 9.7 %collective-permute-start.12 = (bf16[384,256]{1,0:T(8,128)(2,1)S(1)}, bf16[384,256]{1,0:T(8,128)(2,1)S(1)}, u32[]{:S(2)}, u32[]{:S(2)}) collective-permute-start(bf16[384,256]{1,0:T(8,128)(2,1)S(1)} %get-tuple-element.36), channel_id=1, source_target_pairs={{0,4},{1,5},{2,6},{3,7},{4,0},{5,1},{6,2},{7,3},{8,12},{9,13},{10,... | collective-permute-start | bytes 589832 | tf_op jit(solution)/shard_map/ppermute | solution.py:379
  52.1 6.6 %collective-permute-start.15 = (bf16[384,256]{1,0:T(8,128)(2,1)S(1)}, bf16[384,256]{1,0:T(8,128)(2,1)S(1)}, u32[]{:S(2)}, u32[]{:S(2)}) collective-permute-start(bf16[384,256]{1,0:T(8,128)(2,1)S(1)} %attend.5), channel_id=1, source_target_pairs={{0,6},{1,7},{2,4},{3,5},{4,2},{5,3},{6,0},{7,1},{8,14},{9,15},{10,... | collective-permute-start | bytes 589832 | tf_op jit(solution)/shard_map/ppermute | solution.py:379
  55.7 3.1 %collective-permute-start.16 = (bf16[384,256]{1,0:T(8,128)(2,1)S(1)}, bf16[384,256]{1,0:T(8,128)(2,1)S(1)}, u32[]{:S(2)}, u32[]{:S(2)}) collective-permute-start(bf16[384,256]{1,0:T(8,128)(2,1)S(1)} %attend.3.refs_0_), channel_id=1, source_target_pairs={{0,1},{1,0},{2,3},{3,2},{4,5},{5,4},{6,7},{7,6},{8,9},{9,8},{10,11... | collective-permute-start | bytes 589832 | tf_op jit(solution)/shard_map/ppermute | solution.py:379
  55.8 3.0 %collective-permute-start.17 = (bf16[384,256]{1,0:T(8,128)(2,1)S(1)}, bf16[384,256]{1,0:T(8,128)(2,1)S(1)}, u32[]{:S(2)}, u32[]{:S(2)}) collective-permute-start(bf16[384,256]{1,0:T(8,128)(2,1)S(1)} %collective-permute-done.11.refs_1_), channel_id=1, source_target_pairs={{0,1},{1,0},{2,3},{3,2},{4,5},{5,4},{6,7},{7,6},{8,9},{9,8},{10,11... | collective-permute-start | bytes 589832 | tf_op jit(solution)/shard_map/ppermute | solution.py:379
  56.3 2.5 %collective-permute-start.18 = (bf16[384,256]{1,0:T(8,128)(2,1)S(1)}, bf16[384,256]{1,0:T(8,128)(2,1)S(1)}, u32[]{:S(2)}, u32[]{:S(2)}) collective-permute-start(bf16[384,256]{1,0:T(8,128)(2,1)S(1)} %collective-permute-done.12.refs_2_), channel_id=1, source_target_pairs={{0,1},{1,0},{2,3},{3,2},{4,5},{5,4},{6,7},{7,6},{8,9},{9,8},{10,11... | collective-permute-start | bytes 589832 | tf_op jit(solution)/shard_map/ppermute | solution.py:379
  63.3 7.9 %collective-permute-start.27 = (bf16[128,640]{1,0:T(8,128)(2,1)S(1)}, bf16[128,640]{1,0:T(8,128)(2,1)S(1)}, u32[]{:S(2)}, u32[]{:S(2)}) collective-permute-start(bf16[128,640]{1,0:T(8,128)(2,1)S(1)} %get-tuple-element.47), channel_id=1, source_target_pairs={{0,8},{8,0},{16,24},{24,16},{1,9},{9,1},{17,25},{25,17},{2,10},{10... | collective-permute-start | bytes 491528 | tf_op jit(solution)/shard_map/ppermute | solution.py:379
  65.1 20.1 %collective-permute-start.21 = (bf16[128,1408]{1,0:T(8,128)(2,1)S(1)}, bf16[128,1408]{1,0:T(8,128)(2,1)S(1)}, u32[]{:S(2)}, u32[]{:S(2)}) collective-permute-start(bf16[128,1408]{1,0:T(8,128)(2,1)S(1)} %get-tuple-element.39), channel_id=1, source_target_pairs={{0,2},{1,3},{2,0},{3,1},{4,6},{5,7},{6,4},{7,5},{8,10},{9,11},{10,... | collective-permute-start | bytes 1081352 | tf_op jit(solution)/shard_map/ppermute | solution.py:379
  66.6 19.4 %collective-permute-start.22 = (bf16[128,1408]{1,0:T(8,128)(2,1)S(1)}, bf16[128,1408]{1,0:T(8,128)(2,1)S(1)}, u32[]{:S(2)}, u32[]{:S(2)}) collective-permute-start(bf16[128,1408]{1,0:T(8,128)(2,1)S(1)} %get-tuple-element.40), channel_id=1, source_target_pairs={{0,4},{1,5},{2,6},{3,7},{4,0},{5,1},{6,2},{7,3},{8,12},{9,13},{10,... | collective-permute-start | bytes 1081352 | tf_op jit(solution)/shard_map/ppermute | solution.py:379
  67.6 18.5 %collective-permute-start.23 = (bf16[128,1408]{1,0:T(8,128)(2,1)S(1)}, bf16[128,1408]{1,0:T(8,128)(2,1)S(1)}, u32[]{:S(2)}, u32[]{:S(2)}) collective-permute-start(bf16[128,1408]{1,0:T(8,128)(2,1)S(1)} %get-tuple-element.41), channel_id=1, source_target_pairs={{0,6},{1,7},{2,4},{3,5},{4,2},{5,3},{6,0},{7,1},{8,14},{9,15},{10,... | collective-permute-start | bytes 1081352 | tf_op jit(solution)/shard_map/ppermute | solution.py:379
  68.6 13.8 %collective-permute-start.28 = (bf16[128,640]{1,0:T(8,128)(2,1)S(1)}, bf16[128,640]{1,0:T(8,128)(2,1)S(1)}, u32[]{:S(2)}, u32[]{:S(2)}) collective-permute-start(bf16[128,640]{1,0:T(8,128)(2,1)S(1)} %get-tuple-element.48), channel_id=1, source_target_pairs={{0,16},{8,24},{16,0},{24,8},{1,17},{9,25},{17,1},{25,9},{2,18},{10... | collective-permute-start | bytes 491528 | tf_op jit(solution)/shard_map/ppermute | solution.py:379
  71.2 11.2 %collective-permute-start.29 = (bf16[128,640]{1,0:T(8,128)(2,1)S(1)}, bf16[128,640]{1,0:T(8,128)(2,1)S(1)}, u32[]{:S(2)}, u32[]{:S(2)}) collective-permute-start(bf16[128,640]{1,0:T(8,128)(2,1)S(1)} %get-tuple-element.49), channel_id=1, source_target_pairs={{0,24},{8,16},{16,8},{24,0},{1,25},{9,17},{17,9},{25,1},{2,26},{10... | collective-permute-start | bytes 491528 | tf_op jit(solution)/shard_map/ppermute | solution.py:379
  82.5 8.2 %collective-permute-start.30 = (bf16[32,640]{1,0:T(8,128)(2,1)S(1)}, bf16[32,640]{1,0:T(8,128)(2,1)S(1)}, u32[]{:S(2)}, u32[]{:S(2)}) collective-permute-start(bf16[32,640]{1,0:T(8,128)(2,1)S(1)} %get-tuple-element.51), channel_id=1, source_target_pairs={{0,2},{1,3},{2,0},{3,1},{4,6},{5,7},{6,4},{7,5},{8,10},{9,11},{10,... | collective-permute-start | bytes 122888 | tf_op jit(solution)/shard_map/ppermute | solution.py:379
  84.2 10.8 %collective-permute-start.31 = (bf16[32,640]{1,0:T(8,128)(2,1)S(1)}, bf16[32,640]{1,0:T(8,128)(2,1)S(1)}, u32[]{:S(2)}, u32[]{:S(2)}) collective-permute-start(bf16[32,640]{1,0:T(8,128)(2,1)S(1)} %get-tuple-element.52), channel_id=1, source_target_pairs={{0,4},{1,5},{2,6},{3,7},{4,0},{5,1},{6,2},{7,3},{8,12},{9,13},{10,... | collective-permute-start | bytes 122888 | tf_op jit(solution)/shard_map/ppermute | solution.py:379
  85.1 9.9 %collective-permute-start.32 = (bf16[32,640]{1,0:T(8,128)(2,1)S(1)}, bf16[32,640]{1,0:T(8,128)(2,1)S(1)}, u32[]{:S(2)}, u32[]{:S(2)}) collective-permute-start(bf16[32,640]{1,0:T(8,128)(2,1)S(1)} %get-tuple-element.53), channel_id=1, source_target_pairs={{0,6},{1,7},{2,4},{3,5},{4,2},{5,3},{6,0},{7,1},{8,14},{9,15},{10,... | collective-permute-start | bytes 122888 | tf_op jit(solution)/shard_map/ppermute | solution.py:379
  86.2 8.8 %collective-permute-start.24 = (bf16[32,1408]{1,0:T(8,128)(2,1)S(1)}, bf16[32,1408]{1,0:T(8,128)(2,1)S(1)}, u32[]{:S(2)}, u32[]{:S(2)}) collective-permute-start(bf16[32,1408]{1,0:T(8,128)(2,1)S(1)} %get-tuple-element.43), channel_id=1, source_target_pairs={{0,8},{8,0},{16,24},{24,16},{1,9},{9,1},{17,25},{25,17},{2,10},{10... | collective-permute-start | bytes 270344 | tf_op jit(solution)/shard_map/ppermute | solution.py:379
  89.5 8.4 %collective-permute-start.25 = (bf16[32,1408]{1,0:T(8,128)(2,1)S(1)}, bf16[32,1408]{1,0:T(8,128)(2,1)S(1)}, u32[]{:S(2)}, u32[]{:S(2)}) collective-permute-start(bf16[32,1408]{1,0:T(8,128)(2,1)S(1)} %get-tuple-element.44), channel_id=1, source_target_pairs={{0,16},{8,24},{16,0},{24,8},{1,17},{9,25},{17,1},{25,9},{2,18},{10... | collective-permute-start | bytes 270344 | tf_op jit(solution)/shard_map/ppermute | solution.py:379
  90.7 7.3 %collective-permute-start.26 = (bf16[32,1408]{1,0:T(8,128)(2,1)S(1)}, bf16[32,1408]{1,0:T(8,128)(2,1)S(1)}, u32[]{:S(2)}, u32[]{:S(2)}) collective-permute-start(bf16[32,1408]{1,0:T(8,128)(2,1)S(1)} %get-tuple-element.45), channel_id=1, source_target_pairs={{0,24},{8,16},{16,8},{24,0},{1,25},{9,17},{17,9},{25,1},{2,26},{10... | collective-permute-start | bytes 270344 | tf_op jit(solution)/shard_map/ppermute | solution.py:379
  (4 other events, 66.6 us)
where the time goes:
time: 98.8 us; the launch traced here: 98.7 us
  waiting for transfers between devices  37.9 us (38%)
  starting transfers between devices  34.2 us (35%)
  Pallas kernels  25.9 us (26%)
    ppermute x33, waiting for transfers between devices, over(): return lax.ppermute(value, axis, [(i, i ^ mask) for i in range(size)])  37.9 us
    ppermute x33, starting transfers between devices, over(): return lax.ppermute(value, axis, [(i, i ^ mask) for i in range(size)])  34.2 us
    pallas_call x3, Pallas kernels, attend(): pl.pallas_call(kernel, out_shape=[jax.ShapeDtypeStruct((row_count, width)...  15.7 us
    pallas_call x1, Pallas kernels, weight_gradient(): pl.pallas_call(kernel, out_shape=[shape(chips * group, out_width - split,...  3.12 us
    pallas_call x1, Pallas kernels, project(): pl.pallas_call(kernel, out_shape=jax.ShapeDtypeStruct((row_count, out_wid...  2.93 us
    pallas_call x2, Pallas kernels, cut(): pl.pallas_call(kernel, out_shape=[shape] * chips, in_specs=[HBM] * count,...  2.92 us
  transfers between devices with their start and end apart: 33, of which 7 were waited for; matrix products, arithmetic and copies ran while one was open for 0% of the time, Pallas kernels for 21%

commit v1 on v0

--- a/solution.py
+++ b/solution.py
@@ -28,7 +28,7 @@
     return pltpu.CompilerParams(vmem_limit_bytes=mebibytes * 1024 * 1024)
 
 
-def cut(sources, chips, width):
+def cut(sources, aways, width):
     row_count = sources[0].shape[0]
     count = len(sources)
 
@@ -36,13 +36,13 @@
         ins, outs, sems = refs[:count], refs[count:-1], refs[-1]
         chip, _ = place()
         copies = []
-        for away in reversed(range(chips)):
+        for out, away in zip(outs, aways):
             columns = pl.ds(pl.multiple_of((chip ^ away) * width, width), width)
             for at, source in enumerate(ins):
                 copies.append(
                     pltpu.make_async_copy(
                         source.at[:, columns],
-                        outs[away].at[:, at * width : (at + 1) * width],
+                        out.at[:, at * width : (at + 1) * width],
                         sems.at[len(copies)],
                     )
                 )
@@ -54,10 +54,10 @@
     shape = jax.ShapeDtypeStruct((row_count, count * width), sources[0].dtype)
     return pl.pallas_call(
         kernel,
-        out_shape=[shape] * chips,
+        out_shape=[shape] * len(aways),
         in_specs=[HBM] * count,
-        out_specs=[VMEM] * chips,
-        scratch_shapes=[pltpu.SemaphoreType.DMA((count * chips,))],
+        out_specs=[VMEM] * len(aways),
+        scratch_shapes=[pltpu.SemaphoreType.DMA((count * len(aways),))],
         compiler_params=params(16),
         name="cut",
     )(*(pltpu.with_memory_space_constraint(source, pltpu.HBM) for source in sources))
@@ -387,8 +387,11 @@
     def meet(pieces):
         return [pieces[0]] + [over("dp", planes, pieces[away], away) for away in range(1, planes)]
 
-    near = spread(cut([key_rows[0], value_rows[0]], chips, width))
-    queries = spread(cut([query_rows[0]], chips, width))
+    sources = [key_rows[0], value_rows[0]]
+    last = cut(sources, [chips - 1], width)
+    rest = cut(sources, range(chips - 1), width)
+    near = spread([*rest, *last])
+    queries = spread(cut([query_rows[0]], range(chips), width))
     ends = spread([scale_end] * chips)
     far = [other_core(piece) for piece in near]
     grad_near = grad_out[0]
@@ -396,9 +399,7 @@
     both = assemble(near, far, chips)
     mine = [None] * chips
     for aways in ([chips - 1], list(range(1, chips - 1)), [0]):
-        results = attend(
-            [queries[i] for i in aways], [ends[i] for i in aways], aways, both, width
-        )
+        results = attend([queries[i] for i in aways], [ends[i] for i in aways], aways, both, width)
         for away, piece in zip(aways, results):
             mine[away] = over("seq", seq, piece, 2 * away) if away else piece
     others = [other_core(piece) for piece in mine]

time: 98.8 us -> 98.7 us (level)
  waiting for transfers between devices: 37.9 us -> 36.7 us
    ppermute x33, waiting for transfers between devices: 37.9 us -> 36.7 us  [over(): return lax.ppermute(value, axis, [(i, i ^ mask) for i in range(size)])]
    pallas_call x2 -> x3, Pallas kernels: 2.92 us -> 3.82 us  [cut(): pl.pallas_call(kernel, out_shape=[shape] * len(aways), in_specs=[HBM] * c...]
  transfers between devices with their start and end apart: 33 -> 33, of which waited for: 7 -> 7; matrix products, arithmetic and copies ran while one was open for 0% -> 0% of each run, Pallas kernels for 21% -> 22%
where the time goes in v1:
time: 98.7 us; the launch traced here: 98.6 us
  waiting for transfers between devices  36.7 us (37%)
  starting transfers between devices  34.3 us (35%)
  Pallas kernels  26.8 us (27%)
    ppermute x33, waiting for transfers between devices, over(): return lax.ppermute(value, axis, [(i, i ^ mask) for i in range(size)])  36.7 us
    ppermute x33, starting transfers between devices, over(): return lax.ppermute(value, axis, [(i, i ^ mask) for i in range(size)])  34.3 us
    pallas_call x3, Pallas kernels, attend(): pl.pallas_call(kernel, out_shape=[jax.ShapeDtypeStruct((row_count, width)...  15.7 us
    pallas_call x3, Pallas kernels, cut(): pl.pallas_call(kernel, out_shape=[shape] * len(aways), in_specs=[HBM] * c...  3.82 us
    pallas_call x1, Pallas kernels, weight_gradient(): pl.pallas_call(kernel, out_shape=[shape(chips * group, out_width - split,...  3.11 us
    pallas_call x1, Pallas kernels, project(): pl.pallas_call(kernel, out_shape=jax.ShapeDtypeStruct((row_count, out_wid...  2.93 us
  transfers between devices with their start and end apart: 33, of which 7 were waited for; matrix products, arithmetic and copies ran while one was open for 0% of the time, Pallas kernels for 22%

profile of v1, /device:TPU:0, one launch (start us, length us, event | category | flops | bytes accessed | tf_op | source)
XLA Modules:
  0.0 98.6 jit_solution(7110336308319225439)
XLA Ops:
  0.6 1.5 %cut.4 = (bf16[384,512]{1,0:T(8,128)(2,1)S(1)}, bf16[384,512]{1,0:T(8,128)(2,1)S(1)}, bf16[384,512]{1,0:T(8,128)(2,1)S(1)}) custom-call(bf16[384,1024]{1,0:T(8,128)(2,1)} %bitcast.7, bf16[384,1024]{1,0:T(8,128)(2,1)} %bitcast.9), custom_call_target="tpu_custom_call" | custom-call | tf_op jit(solution)/shard_map/cut/pallas_call | solution.py:55
  2.2 3.0 %collective-permute-start = (bf16[384,512]{1,0:T(8,128)(2,1)S(1)}, bf16[384,512]{1,0:T(8,128)(2,1)S(1)}, u32[]{:S(2)}, u32[]{:S(2)}) collective-permute-start(bf16[384,512]{1,0:T(8,128)(2,1)S(1)} %get-tuple-element.29), channel_id=1, source_target_pairs={{0,2},{1,3},{2,0},{3,1},{4,6},{5,7},{6,4},{7,5},{8,10},{9,11},{10,... | collective-permute-start | bytes 1179656 | tf_op jit(solution)/shard_map/ppermute | solution.py:379
  5.2 1.5 %collective-permute-start.1 = (bf16[384,512]{1,0:T(8,128)(2,1)S(1)}, bf16[384,512]{1,0:T(8,128)(2,1)S(1)}, u32[]{:S(2)}, u32[]{:S(2)}) collective-permute-start(bf16[384,512]{1,0:T(8,128)(2,1)S(1)} %get-tuple-element.30), channel_id=1, source_target_pairs={{0,4},{1,5},{2,6},{3,7},{4,0},{5,1},{6,2},{7,3},{8,12},{9,13},{10,... | collective-permute-start | bytes 1179656 | tf_op jit(solution)/shard_map/ppermute | solution.py:379
  6.7 1.0 %cut.5 = bf16[384,512]{1,0:T(8,128)(2,1)S(1)} custom-call(bf16[384,1024]{1,0:T(8,128)(2,1)} %bitcast.8, bf16[384,1024]{1,0:T(8,128)(2,1)} %bitcast.10), custom_call_target="tpu_custom_call" | custom-call | tf_op jit(solution)/shard_map/cut/pallas_call | solution.py:55
  8.2 7.0 %collective-permute-done.refs_1_ = bf16[384,512]{1,0:T(8,128)(2,1)S(1)} collective-permute-done((bf16[384,512]{1,0:T(8,128)(2,1)S(1)}, bf16[384,512]{1,0:T(8,128)(2,1)S(1)}, u32[]{:S(2)}, u32[]{:S(2)}) %collective-permute-start) | collective-permute-done | bytes 393248 | tf_op jit(solution)/shard_map/ppermute | solution.py:379
  15.2 10.0 %collective-permute-done.1.refs_2_ = bf16[384,512]{1,0:T(8,128)(2,1)S(1)} collective-permute-done((bf16[384,512]{1,0:T(8,128)(2,1)S(1)}, bf16[384,512]{1,0:T(8,128)(2,1)S(1)}, u32[]{:S(2)}, u32[]{:S(2)}) %collective-permute-start.1) | collective-permute-done | bytes 393248 | tf_op jit(solution)/shard_map/ppermute | solution.py:379
  25.7 1.3 %cut.3 = (bf16[384,256]{1,0:T(8,128)(2,1)S(1)}, bf16[384,256]{1,0:T(8,128)(2,1)S(1)}, bf16[384,256]{1,0:T(8,128)(2,1)S(1)}, bf16[384,256]{1,0:T(8,128)(2,1)S(1)}) custom-call(bf16[384,1024]{1,0:T(8,128)(2,1)} %bitcast.12), custom_call_target="tpu_custom_call" | custom-call | tf_op jit(solution)/shard_map/cut/pallas_call | solution.py:55
  27.0 1.6 %collective-permute-start.10 = (bf16[384,256]{1,0:T(8,128)(2,1)S(1)}, bf16[384,256]{1,0:T(8,128)(2,1)S(1)}, u32[]{:S(2)}, u32[]{:S(2)}) collective-permute-start(bf16[384,256]{1,0:T(8,128)(2,1)S(1)} %get-tuple-element.32), channel_id=1, source_target_pairs={{0,4},{1,5},{2,6},{3,7},{4,0},{5,1},{6,2},{7,3},{8,12},{9,13},{10,... | collective-permute-start | bytes 589832 | tf_op jit(solution)/shard_map/ppermute | solution.py:379
  29.1 1.5 %collective-permute-start.7 = (s32[384]{0:T(512)S(1)}, s32[384]{0:T(512)S(1)}, u32[]{:S(2)}, u32[]{:S(2)}) collective-permute-start(s32[384]{0:T(512)S(1)} %copy-done.2), channel_id=1, source_target_pairs={{0,2},{1,3},{2,0},{3,1},{4,6},{5,7},{6,4},{7,5},{8,10},{9,11},{10,... | collective-permute-start | bytes 4616 | tf_op jit(solution)/shard_map/ppermute | solution.py:379
  31.3 3.8 %collective-permute-done.7.refs_0_ = s32[384]{0:T(512)S(1)} collective-permute-done((s32[384]{0:T(512)S(1)}, s32[384]{0:T(512)S(1)}, u32[]{:S(2)}, u32[]{:S(2)}) %collective-permute-start.7) | collective-permute-done | bytes 1568 | tf_op jit(solution)/shard_map/ppermute | solution.py:379
  35.5 2.6 %collective-permute-start.14 = (bf16[384,256]{1,0:T(8,128)(2,1)S(1)}, bf16[384,256]{1,0:T(8,128)(2,1)S(1)}, u32[]{:S(2)}, u32[]{:S(2)}) collective-permute-start(bf16[384,256]{1,0:T(8,128)(2,1)S(1)} %get-tuple-element.35), channel_id=1, source_target_pairs={{0,6},{1,7},{2,4},{3,5},{4,2},{5,3},{6,0},{7,1},{8,14},{9,15},{10,... | collective-permute-start | bytes 589832 | tf_op jit(solution)/shard_map/ppermute | solution.py:379
  38.1 8.3 %attend.4 = (bf16[384,256]{1,0:T(8,128)(2,1)S(1)}, bf16[384,256]{1,0:T(8,128)(2,1)S(1)}) custom-call(s32[384]{0:T(512)S(1)} %collective-permute-done.7.refs_0_, s32[384]{0:T(512)S(1)} %collective-permute-done.8.refs_1_, bf16[384,256]{1,0:T(8,128)(2,1)S(1)} %collective-permute-done.9.refs_2_, bf16[384,256]{1,0:T(8,128)(2,1)S(1)} %collective-permute-done.10.refs_3_, ...), custom_call_target="tpu_custom_call" | custom-call | flops 2415919104 | bytes 3145728 | tf_op jit(solution)/shard_map/attend/pallas_call | solution.py:193
  47.3 4.6 %attend.5 = bf16[384,256]{1,0:T(8,128)(2,1)S(1)} custom-call(s32[384]{0:T(512)S(1)} %collective-permute-done.13.refs_0_, bf16[384,256]{1,0:T(8,128)(2,1)S(1)} %collective-permute-done.14.refs_1_, bf16[3072,512]{1,0:T(8,128)(2,1)S(1)} %assemble.1.refs_2_.refs_4_), custom_call_target="tpu_custom_call" | custom-call | flops 1207959552 | bytes 3145728 | tf_op jit(solution)/shard_map/attend/pallas_call | solution.py:193
  52.7 2.8 %attend.3.refs_0_ = bf16[384,256]{1,0:T(8,128)(2,1)S(1)} custom-call(s32[384]{0:T(512)S(1)} %copy-done.2, bf16[384,256]{1,0:T(8,128)(2,1)S(1)} %get-tuple-element.27.refs_1_, bf16[3072,512]{1,0:T(8,128)(2,1)S(1)} %assemble.1.refs_2_.refs_4_), custom_call_target="tpu_custom_call" | custom-call | flops 1207959552 | bytes 3145728 | tf_op jit(solution)/shard_map/attend/pallas_call | solution.py:193
  56.2 2.4 %collective-permute-done.15.refs_3_ = bf16[384,256]{1,0:T(8,128)(2,1)S(1)} collective-permute-done((bf16[384,256]{1,0:T(8,128)(2,1)S(1)}, bf16[384,256]{1,0:T(8,128)(2,1)S(1)}, u32[]{:S(2)}, u32[]{:S(2)}) %collective-permute-start.15) | collective-permute-done | bytes 196640 | tf_op jit(solution)/shard_map/ppermute | solution.py:379
  58.6 1.4 %collective-permute-done.19.refs_7_ = bf16[384,256]{1,0:T(8,128)(2,1)S(1)} collective-permute-done((bf16[384,256]{1,0:T(8,128)(2,1)S(1)}, bf16[384,256]{1,0:T(8,128)(2,1)S(1)}, u32[]{:S(2)}, u32[]{:S(2)}) %collective-permute-start.19) | collective-permute-done | bytes 196640 | tf_op jit(solution)/shard_map/ppermute | solution.py:379
  60.0 3.1 %weight_gradient.1 = (f32[128,640]{1,0:T(8,128)S(1)}, bf16[128,640]{1,0:T(8,128)(2,1)S(1)}, bf16[128,640]{1,0:T(8,128)(2,1)S(1)}, bf16[128,640]{1,0:T(8,128)(2,1...) custom-call(bf16[384,256]{1,0:T(8,128)(2,1)S(1)} %attend.3.refs_0_, ...), custom_call_target="tpu_custom_call" | custom-call | flops 1610612736 | bytes 3145728 | tf_op jit(solution)/shard_map/weight_gradient/pallas_call | solution.py:264
  63.1 1.8 %collective-permute-start.27 = (bf16[128,640]{1,0:T(8,128)(2,1)S(1)}, bf16[128,640]{1,0:T(8,128)(2,1)S(1)}, u32[]{:S(2)}, u32[]{:S(2)}) collective-permute-start(bf16[128,640]{1,0:T(8,128)(2,1)S(1)} %get-tuple-element.45), channel_id=1, source_target_pairs={{0,8},{8,0},{16,24},{24,16},{1,9},{9,1},{17,25},{25,17},{2,10},{10... | collective-permute-start | bytes 491528 | tf_op jit(solution)/shard_map/ppermute | solution.py:379
  64.9 1.5 %collective-permute-start.21 = (bf16[128,1408]{1,0:T(8,128)(2,1)S(1)}, bf16[128,1408]{1,0:T(8,128)(2,1)S(1)}, u32[]{:S(2)}, u32[]{:S(2)}) collective-permute-start(bf16[128,1408]{1,0:T(8,128)(2,1)S(1)} %get-tuple-element.37), channel_id=1, source_target_pairs={{0,2},{1,3},{2,0},{3,1},{4,6},{5,7},{6,4},{7,5},{8,10},{9,11},{10,... | collective-permute-start | bytes 1081352 | tf_op jit(solution)/shard_map/ppermute | solution.py:379
  66.5 1.0 collective-permute-start.22
  67.4 1.0 %collective-permute-start.23 = (bf16[128,1408]{1,0:T(8,128)(2,1)S(1)}, bf16[128,1408]{1,0:T(8,128)(2,1)S(1)}, u32[]{:S(2)}, u32[]{:S(2)}) collective-permute-start(bf16[128,1408]{1,0:T(8,128)(2,1)S(1)} %get-tuple-element.39), channel_id=1, source_target_pairs={{0,6},{1,7},{2,4},{3,5},{4,2},{5,3},{6,0},{7,1},{8,14},{9,15},{10,... | collective-permute-start | bytes 1081352 | tf_op jit(solution)/shard_map/ppermute | solution.py:379
  68.4 2.6 %collective-permute-start.28 = (bf16[128,640]{1,0:T(8,128)(2,1)S(1)}, bf16[128,640]{1,0:T(8,128)(2,1)S(1)}, u32[]{:S(2)}, u32[]{:S(2)}) collective-permute-start(bf16[128,640]{1,0:T(8,128)(2,1)S(1)} %get-tuple-element.46), channel_id=1, source_target_pairs={{0,16},{8,24},{16,0},{24,8},{1,17},{9,25},{17,1},{25,9},{2,18},{10... | collective-permute-start | bytes 491528 | tf_op jit(solution)/shard_map/ppermute | solution.py:379
  71.0 2.2 %collective-permute-start.29 = (bf16[128,640]{1,0:T(8,128)(2,1)S(1)}, bf16[128,640]{1,0:T(8,128)(2,1)S(1)}, u32[]{:S(2)}, u32[]{:S(2)}) collective-permute-start(bf16[128,640]{1,0:T(8,128)(2,1)S(1)} %get-tuple-element.47), channel_id=1, source_target_pairs={{0,24},{8,16},{16,8},{24,0},{1,25},{9,17},{17,9},{25,1},{2,26},{10... | collective-permute-start | bytes 491528 | tf_op jit(solution)/shard_map/ppermute | solution.py:379
  73.2 9.1 %collective-permute-done.28.refs_2_ = bf16[128,640]{1,0:T(8,128)(2,1)S(1)} collective-permute-done((bf16[128,640]{1,0:T(8,128)(2,1)S(1)}, bf16[128,640]{1,0:T(8,128)(2,1)S(1)}, u32[]{:S(2)}, u32[]{:S(2)}) %collective-permute-start.28) | collective-permute-done | bytes 163872 | tf_op jit(solution)/shard_map/ppermute | solution.py:379
  82.3 1.7 %collective-permute-start.30 = (bf16[32,640]{1,0:T(8,128)(2,1)S(1)}, bf16[32,640]{1,0:T(8,128)(2,1)S(1)}, u32[]{:S(2)}, u32[]{:S(2)}) collective-permute-start(bf16[32,640]{1,0:T(8,128)(2,1)S(1)} %get-tuple-element.49), channel_id=1, source_target_pairs={{0,2},{1,3},{2,0},{3,1},{4,6},{5,7},{6,4},{7,5},{8,10},{9,11},{10,... | collective-permute-start | bytes 122888 | tf_op jit(solution)/shard_map/ppermute | solution.py:379
  84.0 1.0 collective-permute-start.31
  85.0 0.9 collective-permute-start.32
  86.1 3.3 %collective-permute-start.24 = (bf16[32,1408]{1,0:T(8,128)(2,1)S(1)}, bf16[32,1408]{1,0:T(8,128)(2,1)S(1)}, u32[]{:S(2)}, u32[]{:S(2)}) collective-permute-start(bf16[32,1408]{1,0:T(8,128)(2,1)S(1)} %get-tuple-element.41), channel_id=1, source_target_pairs={{0,8},{8,0},{16,24},{24,16},{1,9},{9,1},{17,25},{25,17},{2,10},{10... | collective-permute-start | bytes 270344 | tf_op jit(solution)/shard_map/ppermute | solution.py:379
  89.4 1.2 %collective-permute-start.25 = (bf16[32,1408]{1,0:T(8,128)(2,1)S(1)}, bf16[32,1408]{1,0:T(8,128)(2,1)S(1)}, u32[]{:S(2)}, u32[]{:S(2)}) collective-permute-start(bf16[32,1408]{1,0:T(8,128)(2,1)S(1)} %get-tuple-element.42), channel_id=1, source_target_pairs={{0,16},{8,24},{16,0},{24,8},{1,17},{9,25},{17,1},{25,9},{2,18},{10... | collective-permute-start | bytes 270344 | tf_op jit(solution)/shard_map/ppermute | solution.py:379
  90.5 1.4 %collective-permute-start.26 = (bf16[32,1408]{1,0:T(8,128)(2,1)S(1)}, bf16[32,1408]{1,0:T(8,128)(2,1)S(1)}, u32[]{:S(2)}, u32[]{:S(2)}) collective-permute-start(bf16[32,1408]{1,0:T(8,128)(2,1)S(1)} %get-tuple-element.43), channel_id=1, source_target_pairs={{0,24},{8,16},{16,8},{24,0},{1,25},{9,17},{17,9},{25,1},{2,26},{10... | collective-permute-start | bytes 270344 | tf_op jit(solution)/shard_map/ppermute | solution.py:379
  91.9 2.9 %project.1 = bf16[384,2048]{1,0:T(8,128)(2,1)} custom-call(bf16[384,256]{1,0:T(8,128)(2,1)S(1)} %attend.3.refs_0_, bf16[384,256]{1,0:T(8,128)(2,1)S(1)} %collective-permute-done.11.refs_1_, bf16[384,256]{1,0:T(8,128)(2,1)S(1)} %collective-permute-done.12.refs_2_, bf16[384,256]{1,0:T(8,128)(2,1)S(1)} %collective-permute-done.15.refs_3_, ...), custom_call_target="tpu_custom_call" | custom-call | flops 1610612736 | bytes 4194304 | tf_op jit(solution)/shard_map/project/pallas_call | solution.py:305
  94.9 2.9 %collective-permute-done.25.refs_2_ = bf16[32,1408]{1,0:T(8,128)(2,1)S(1)} collective-permute-done((bf16[32,1408]{1,0:T(8,128)(2,1)S(1)}, bf16[32,1408]{1,0:T(8,128)(2,1)S(1)}, u32[]{:S(2)}, u32[]{:S(2)}) %collective-permute-start.25) | collective-permute-done | bytes 90144 | tf_op jit(solution)/shard_map/ppermute | solution.py:379
  (52 shorter events, 6.0 us)
Async XLA Ops:
  2.2 13.0 %collective-permute-start = (bf16[384,512]{1,0:T(8,128)(2,1)S(1)}, bf16[384,512]{1,0:T(8,128)(2,1)S(1)}, u32[]{:S(2)}, u32[]{:S(2)}) collective-permute-start(bf16[384,512]{1,0:T(8,128)(2,1)S(1)} %get-tuple-element.29), channel_id=1, source_target_pairs={{0,2},{1,3},{2,0},{3,1},{4,6},{5,7},{6,4},{7,5},{8,10},{9,11},{10,... | collective-permute-start | bytes 1179656 | tf_op jit(solution)/shard_map/ppermute | solution.py:379
  5.2 54.8 %collective-permute-start.20 = (bf16[384,2048]{1,0:T(8,128)(2,1)S(1)}, bf16[384,2048]{1,0:T(8,128)(2,1)S(1)}, u32[]{:S(2)}, u32[]{:S(2)}) collective-permute-start(bf16[384,2048]{1,0:T(8,128)(2,1)S(1)} %bitcast.5), channel_id=1, source_target_pairs={{0,1},{1,0},{2,3},{3,2},{4,5},{5,4},{6,7},{7,6},{8,9},{9,8},{10,11... | collective-permute-start | bytes 4718600 | tf_op jit(solution)/shard_map/ppermute | solution.py:379
  5.2 20.0 %collective-permute-start.1 = (bf16[384,512]{1,0:T(8,128)(2,1)S(1)}, bf16[384,512]{1,0:T(8,128)(2,1)S(1)}, u32[]{:S(2)}, u32[]{:S(2)}) collective-permute-start(bf16[384,512]{1,0:T(8,128)(2,1)S(1)} %get-tuple-element.30), channel_id=1, source_target_pairs={{0,4},{1,5},{2,6},{3,7},{4,0},{5,1},{6,2},{7,3},{8,12},{9,13},{10,... | collective-permute-start | bytes 1179656 | tf_op jit(solution)/shard_map/ppermute | solution.py:379
  7.8 17.4 %collective-permute-start.2 = (bf16[384,512]{1,0:T(8,128)(2,1)S(1)}, bf16[384,512]{1,0:T(8,128)(2,1)S(1)}, u32[]{:S(2)}, u32[]{:S(2)}) collective-permute-start(bf16[384,512]{1,0:T(8,128)(2,1)S(1)} %cut.5), channel_id=1, source_target_pairs={{0,6},{1,7},{2,4},{3,5},{4,2},{5,3},{6,0},{7,1},{8,14},{9,15},{10,... | collective-permute-start | bytes 1179656 | tf_op jit(solution)/shard_map/ppermute | solution.py:379
  8.1 18.9 %collective-permute-start.3 = (bf16[384,512]{1,0:T(8,128)(2,1)S(1)}, bf16[384,512]{1,0:T(8,128)(2,1)S(1)}, u32[]{:S(2)}, u32[]{:S(2)}) collective-permute-start(bf16[384,512]{1,0:T(8,128)(2,1)S(1)} %get-tuple-element.28.refs_0_), channel_id=1, source_target_pairs={{0,1},{1,0},{2,3},{3,2},{4,5},{5,4},{6,7},{7,6},{8,9},{9,8},{10,11... | collective-permute-start | bytes 1179656 | tf_op jit(solution)/shard_map/ppermute | solution.py:379
  15.2 13.4 %collective-permute-start.4 = (bf16[384,512]{1,0:T(8,128)(2,1)S(1)}, bf16[384,512]{1,0:T(8,128)(2,1)S(1)}, u32[]{:S(2)}, u32[]{:S(2)}) collective-permute-start(bf16[384,512]{1,0:T(8,128)(2,1)S(1)} %collective-permute-done.refs_1_), channel_id=1, source_target_pairs={{0,1},{1,0},{2,3},{3,2},{4,5},{5,4},{6,7},{7,6},{8,9},{9,8},{10,11... | collective-permute-start | bytes 1179656 | tf_op jit(solution)/shard_map/ppermute | solution.py:379
  25.2 3.9 %collective-permute-start.5 = (bf16[384,512]{1,0:T(8,128)(2,1)S(1)}, bf16[384,512]{1,0:T(8,128)(2,1)S(1)}, u32[]{:S(2)}, u32[]{:S(2)}) collective-permute-start(bf16[384,512]{1,0:T(8,128)(2,1)S(1)} %collective-permute-done.1.refs_2_), channel_id=1, source_target_pairs={{0,1},{1,0},{2,3},{3,2},{4,5},{5,4},{6,7},{7,6},{8,9},{9,8},{10,11... | collective-permute-start | bytes 1179656 | tf_op jit(solution)/shard_map/ppermute | solution.py:379
  25.2 5.4 %collective-permute-start.6 = (bf16[384,512]{1,0:T(8,128)(2,1)S(1)}, bf16[384,512]{1,0:T(8,128)(2,1)S(1)}, u32[]{:S(2)}, u32[]{:S(2)}) collective-permute-start(bf16[384,512]{1,0:T(8,128)(2,1)S(1)} %collective-permute-done.2.refs_3_), channel_id=1, source_target_pairs={{0,1},{1,0},{2,3},{3,2},{4,5},{5,4},{6,7},{7,6},{8,9},{9,8},{10,11... | collective-permute-start | bytes 1179656 | tf_op jit(solution)/shard_map/ppermute | solution.py:379
  27.0 11.1 %collective-permute-start.10 = (bf16[384,256]{1,0:T(8,128)(2,1)S(1)}, bf16[384,256]{1,0:T(8,128)(2,1)S(1)}, u32[]{:S(2)}, u32[]{:S(2)}) collective-permute-start(bf16[384,256]{1,0:T(8,128)(2,1)S(1)} %get-tuple-element.32), channel_id=1, source_target_pairs={{0,4},{1,5},{2,6},{3,7},{4,0},{5,1},{6,2},{7,3},{8,12},{9,13},{10,... | collective-permute-start | bytes 589832 | tf_op jit(solution)/shard_map/ppermute | solution.py:379
  28.6 9.5 %collective-permute-start.9 = (bf16[384,256]{1,0:T(8,128)(2,1)S(1)}, bf16[384,256]{1,0:T(8,128)(2,1)S(1)}, u32[]{:S(2)}, u32[]{:S(2)}) collective-permute-start(bf16[384,256]{1,0:T(8,128)(2,1)S(1)} %get-tuple-element.31), channel_id=1, source_target_pairs={{0,2},{1,3},{2,0},{3,1},{4,6},{5,7},{6,4},{7,5},{8,10},{9,11},{10,... | collective-permute-start | bytes 589832 | tf_op jit(solution)/shard_map/ppermute | solution.py:379
  29.1 6.0 %collective-permute-start.7 = (s32[384]{0:T(512)S(1)}, s32[384]{0:T(512)S(1)}, u32[]{:S(2)}, u32[]{:S(2)}) collective-permute-start(s32[384]{0:T(512)S(1)} %copy-done.2), channel_id=1, source_target_pairs={{0,2},{1,3},{2,0},{3,1},{4,6},{5,7},{6,4},{7,5},{8,10},{9,11},{10,... | collective-permute-start | bytes 4616 | tf_op jit(solution)/shard_map/ppermute | solution.py:379
  30.6 4.9 %collective-permute-start.8 = (s32[384]{0:T(512)S(1)}, s32[384]{0:T(512)S(1)}, u32[]{:S(2)}, u32[]{:S(2)}) collective-permute-start(s32[384]{0:T(512)S(1)} %copy-done.2), channel_id=1, source_target_pairs={{0,4},{1,5},{2,6},{3,7},{4,0},{5,1},{6,2},{7,3},{8,12},{9,13},{10,... | collective-permute-start | bytes 4616 | tf_op jit(solution)/shard_map/ppermute | solution.py:379
  35.1 12.2 %collective-permute-start.13 = (s32[384]{0:T(512)S(1)}, s32[384]{0:T(512)S(1)}, u32[]{:S(2)}, u32[]{:S(2)}) collective-permute-start(s32[384]{0:T(512)S(1)} %copy-done.2), channel_id=1, source_target_pairs={{0,6},{1,7},{2,4},{3,5},{4,2},{5,3},{6,0},{7,1},{8,14},{9,15},{10,... | collective-permute-start | bytes 4616 | tf_op jit(solution)/shard_map/ppermute | solution.py:379
  35.5 11.9 %collective-permute-start.14 = (bf16[384,256]{1,0:T(8,128)(2,1)S(1)}, bf16[384,256]{1,0:T(8,128)(2,1)S(1)}, u32[]{:S(2)}, u32[]{:S(2)}) collective-permute-start(bf16[384,256]{1,0:T(8,128)(2,1)S(1)} %get-tuple-element.35), channel_id=1, source_target_pairs={{0,6},{1,7},{2,4},{3,5},{4,2},{5,3},{6,0},{7,1},{8,14},{9,15},{10,... | collective-permute-start | bytes 589832 | tf_op jit(solution)/shard_map/ppermute | solution.py:379
  46.4 9.3 %collective-permute-start.11 = (bf16[384,256]{1,0:T(8,128)(2,1)S(1)}, bf16[384,256]{1,0:T(8,128)(2,1)S(1)}, u32[]{:S(2)}, u32[]{:S(2)}) collective-permute-start(bf16[384,256]{1,0:T(8,128)(2,1)S(1)} %get-tuple-element.33), channel_id=1, source_target_pairs={{0,2},{1,3},{2,0},{3,1},{4,6},{5,7},{6,4},{7,5},{8,10},{9,11},{10,... | collective-permute-start | bytes 589832 | tf_op jit(solution)/shard_map/ppermute | solution.py:379
  46.4 9.7 %collective-permute-start.12 = (bf16[384,256]{1,0:T(8,128)(2,1)S(1)}, bf16[384,256]{1,0:T(8,128)(2,1)S(1)}, u32[]{:S(2)}, u32[]{:S(2)}) collective-permute-start(bf16[384,256]{1,0:T(8,128)(2,1)S(1)} %get-tuple-element.34), channel_id=1, source_target_pairs={{0,4},{1,5},{2,6},{3,7},{4,0},{5,1},{6,2},{7,3},{8,12},{9,13},{10,... | collective-permute-start | bytes 589832 | tf_op jit(solution)/shard_map/ppermute | solution.py:379
  51.9 6.6 %collective-permute-start.15 = (bf16[384,256]{1,0:T(8,128)(2,1)S(1)}, bf16[384,256]{1,0:T(8,128)(2,1)S(1)}, u32[]{:S(2)}, u32[]{:S(2)}) collective-permute-start(bf16[384,256]{1,0:T(8,128)(2,1)S(1)} %attend.5), channel_id=1, source_target_pairs={{0,6},{1,7},{2,4},{3,5},{4,2},{5,3},{6,0},{7,1},{8,14},{9,15},{10,... | collective-permute-start | bytes 589832 | tf_op jit(solution)/shard_map/ppermute | solution.py:379
  55.5 3.1 %collective-permute-start.16 = (bf16[384,256]{1,0:T(8,128)(2,1)S(1)}, bf16[384,256]{1,0:T(8,128)(2,1)S(1)}, u32[]{:S(2)}, u32[]{:S(2)}) collective-permute-start(bf16[384,256]{1,0:T(8,128)(2,1)S(1)} %attend.3.refs_0_), channel_id=1, source_target_pairs={{0,1},{1,0},{2,3},{3,2},{4,5},{5,4},{6,7},{7,6},{8,9},{9,8},{10,11... | collective-permute-start | bytes 589832 | tf_op jit(solution)/shard_map/ppermute | solution.py:379
  55.6 3.0 %collective-permute-start.17 = (bf16[384,256]{1,0:T(8,128)(2,1)S(1)}, bf16[384,256]{1,0:T(8,128)(2,1)S(1)}, u32[]{:S(2)}, u32[]{:S(2)}) collective-permute-start(bf16[384,256]{1,0:T(8,128)(2,1)S(1)} %collective-permute-done.11.refs_1_), channel_id=1, source_target_pairs={{0,1},{1,0},{2,3},{3,2},{4,5},{5,4},{6,7},{7,6},{8,9},{9,8},{10,11... | collective-permute-start | bytes 589832 | tf_op jit(solution)/shard_map/ppermute | solution.py:379
  56.1 2.5 %collective-permute-start.18 = (bf16[384,256]{1,0:T(8,128)(2,1)S(1)}, bf16[384,256]{1,0:T(8,128)(2,1)S(1)}, u32[]{:S(2)}, u32[]{:S(2)}) collective-permute-start(bf16[384,256]{1,0:T(8,128)(2,1)S(1)} %collective-permute-done.12.refs_2_), channel_id=1, source_target_pairs={{0,1},{1,0},{2,3},{3,2},{4,5},{5,4},{6,7},{7,6},{8,9},{9,8},{10,11... | collective-permute-start | bytes 589832 | tf_op jit(solution)/shard_map/ppermute | solution.py:379
  63.1 7.9 %collective-permute-start.27 = (bf16[128,640]{1,0:T(8,128)(2,1)S(1)}, bf16[128,640]{1,0:T(8,128)(2,1)S(1)}, u32[]{:S(2)}, u32[]{:S(2)}) collective-permute-start(bf16[128,640]{1,0:T(8,128)(2,1)S(1)} %get-tuple-element.45), channel_id=1, source_target_pairs={{0,8},{8,0},{16,24},{24,16},{1,9},{9,1},{17,25},{25,17},{2,10},{10... | collective-permute-start | bytes 491528 | tf_op jit(solution)/shard_map/ppermute | solution.py:379
  64.9 20.1 %collective-permute-start.21 = (bf16[128,1408]{1,0:T(8,128)(2,1)S(1)}, bf16[128,1408]{1,0:T(8,128)(2,1)S(1)}, u32[]{:S(2)}, u32[]{:S(2)}) collective-permute-start(bf16[128,1408]{1,0:T(8,128)(2,1)S(1)} %get-tuple-element.37), channel_id=1, source_target_pairs={{0,2},{1,3},{2,0},{3,1},{4,6},{5,7},{6,4},{7,5},{8,10},{9,11},{10,... | collective-permute-start | bytes 1081352 | tf_op jit(solution)/shard_map/ppermute | solution.py:379
  66.5 19.4 %collective-permute-start.22 = (bf16[128,1408]{1,0:T(8,128)(2,1)S(1)}, bf16[128,1408]{1,0:T(8,128)(2,1)S(1)}, u32[]{:S(2)}, u32[]{:S(2)}) collective-permute-start(bf16[128,1408]{1,0:T(8,128)(2,1)S(1)} %get-tuple-element.38), channel_id=1, source_target_pairs={{0,4},{1,5},{2,6},{3,7},{4,0},{5,1},{6,2},{7,3},{8,12},{9,13},{10,... | collective-permute-start | bytes 1081352 | tf_op jit(solution)/shard_map/ppermute | solution.py:379
  67.4 18.5 %collective-permute-start.23 = (bf16[128,1408]{1,0:T(8,128)(2,1)S(1)}, bf16[128,1408]{1,0:T(8,128)(2,1)S(1)}, u32[]{:S(2)}, u32[]{:S(2)}) collective-permute-start(bf16[128,1408]{1,0:T(8,128)(2,1)S(1)} %get-tuple-element.39), channel_id=1, source_target_pairs={{0,6},{1,7},{2,4},{3,5},{4,2},{5,3},{6,0},{7,1},{8,14},{9,15},{10,... | collective-permute-start | bytes 1081352 | tf_op jit(solution)/shard_map/ppermute | solution.py:379
  68.4 13.8 %collective-permute-start.28 = (bf16[128,640]{1,0:T(8,128)(2,1)S(1)}, bf16[128,640]{1,0:T(8,128)(2,1)S(1)}, u32[]{:S(2)}, u32[]{:S(2)}) collective-permute-start(bf16[128,640]{1,0:T(8,128)(2,1)S(1)} %get-tuple-element.46), channel_id=1, source_target_pairs={{0,16},{8,24},{16,0},{24,8},{1,17},{9,25},{17,1},{25,9},{2,18},{10... | collective-permute-start | bytes 491528 | tf_op jit(solution)/shard_map/ppermute | solution.py:379
  71.0 11.2 %collective-permute-start.29 = (bf16[128,640]{1,0:T(8,128)(2,1)S(1)}, bf16[128,640]{1,0:T(8,128)(2,1)S(1)}, u32[]{:S(2)}, u32[]{:S(2)}) collective-permute-start(bf16[128,640]{1,0:T(8,128)(2,1)S(1)} %get-tuple-element.47), channel_id=1, source_target_pairs={{0,24},{8,16},{16,8},{24,0},{1,25},{9,17},{17,9},{25,1},{2,26},{10... | collective-permute-start | bytes 491528 | tf_op jit(solution)/shard_map/ppermute | solution.py:379
  82.3 8.2 %collective-permute-start.30 = (bf16[32,640]{1,0:T(8,128)(2,1)S(1)}, bf16[32,640]{1,0:T(8,128)(2,1)S(1)}, u32[]{:S(2)}, u32[]{:S(2)}) collective-permute-start(bf16[32,640]{1,0:T(8,128)(2,1)S(1)} %get-tuple-element.49), channel_id=1, source_target_pairs={{0,2},{1,3},{2,0},{3,1},{4,6},{5,7},{6,4},{7,5},{8,10},{9,11},{10,... | collective-permute-start | bytes 122888 | tf_op jit(solution)/shard_map/ppermute | solution.py:379
  84.0 10.8 %collective-permute-start.31 = (bf16[32,640]{1,0:T(8,128)(2,1)S(1)}, bf16[32,640]{1,0:T(8,128)(2,1)S(1)}, u32[]{:S(2)}, u32[]{:S(2)}) collective-permute-start(bf16[32,640]{1,0:T(8,128)(2,1)S(1)} %get-tuple-element.50), channel_id=1, source_target_pairs={{0,4},{1,5},{2,6},{3,7},{4,0},{5,1},{6,2},{7,3},{8,12},{9,13},{10,... | collective-permute-start | bytes 122888 | tf_op jit(solution)/shard_map/ppermute | solution.py:379
  85.0 9.9 %collective-permute-start.32 = (bf16[32,640]{1,0:T(8,128)(2,1)S(1)}, bf16[32,640]{1,0:T(8,128)(2,1)S(1)}, u32[]{:S(2)}, u32[]{:S(2)}) collective-permute-start(bf16[32,640]{1,0:T(8,128)(2,1)S(1)} %get-tuple-element.51), channel_id=1, source_target_pairs={{0,6},{1,7},{2,4},{3,5},{4,2},{5,3},{6,0},{7,1},{8,14},{9,15},{10,... | collective-permute-start | bytes 122888 | tf_op jit(solution)/shard_map/ppermute | solution.py:379
  86.1 8.8 %collective-permute-start.24 = (bf16[32,1408]{1,0:T(8,128)(2,1)S(1)}, bf16[32,1408]{1,0:T(8,128)(2,1)S(1)}, u32[]{:S(2)}, u32[]{:S(2)}) collective-permute-start(bf16[32,1408]{1,0:T(8,128)(2,1)S(1)} %get-tuple-element.41), channel_id=1, source_target_pairs={{0,8},{8,0},{16,24},{24,16},{1,9},{9,1},{17,25},{25,17},{2,10},{10... | collective-permute-start | bytes 270344 | tf_op jit(solution)/shard_map/ppermute | solution.py:379
  89.4 8.4 %collective-permute-start.25 = (bf16[32,1408]{1,0:T(8,128)(2,1)S(1)}, bf16[32,1408]{1,0:T(8,128)(2,1)S(1)}, u32[]{:S(2)}, u32[]{:S(2)}) collective-permute-start(bf16[32,1408]{1,0:T(8,128)(2,1)S(1)} %get-tuple-element.42), channel_id=1, source_target_pairs={{0,16},{8,24},{16,0},{24,8},{1,17},{9,25},{17,1},{25,9},{2,18},{10... | collective-permute-start | bytes 270344 | tf_op jit(solution)/shard_map/ppermute | solution.py:379
  90.5 7.3 %collective-permute-start.26 = (bf16[32,1408]{1,0:T(8,128)(2,1)S(1)}, bf16[32,1408]{1,0:T(8,128)(2,1)S(1)}, u32[]{:S(2)}, u32[]{:S(2)}) collective-permute-start(bf16[32,1408]{1,0:T(8,128)(2,1)S(1)} %get-tuple-element.43), channel_id=1, source_target_pairs={{0,24},{8,16},{16,8},{24,0},{1,25},{9,17},{17,9},{25,1},{2,26},{10... | collective-permute-start | bytes 270344 | tf_op jit(solution)/shard_map/ppermute | solution.py:379
  (4 other events, 64.8 us)

commit v2 on v1

--- a/solution.py
+++ b/solution.py
@@ -213,73 +213,75 @@
     )(*ends, *queries, both)
 
 
-def weight_gradient(near, far, grad_near, grad_far, chips, width, planes, split):
+def turn_over(near, far, chips, width):
     row_count = near[0].shape[0]
-    full = chips * width
-    out_width = grad_near.shape[1]
-    group = full // (planes * chips * 2)
-
-    def kernel(*refs):
-        pieces = (refs[0:chips], refs[chips : 2 * chips])
-        grads = refs[2 * chips : 2 * chips + 2]
-        by_plane = refs[2 * chips + 2 : 2 * chips + 2 + planes]
-        by_chip = refs[2 * chips + 2 + planes : 3 * chips + 2 + planes]
-        turned, left = refs[3 * chips + 2 + planes :]
-        chip, core = place()
-        here = lax.axis_index("dp")
+
+    def kernel(*refs):
+        pieces, out = (refs[:chips], refs[chips : 2 * chips]), refs[2 * chips]
+        chip, _ = place()
         for side in range(2):
             for away in range(chips):
                 start = pl.multiple_of((chip ^ away) * width, width)
-                turned[pl.ds(start, width), side * row_count : (side + 1) * row_count] = (
+                out[pl.ds(start, width), side * row_count : (side + 1) * row_count] = (
                     pieces[side][away][...].T
                 )
 
-        def product(outs, columns, picks):
-            for out, starts in zip(outs, picks):
-                for at, start in enumerate(starts):
-                    rows = pl.ds(pl.multiple_of((start * 2 + core) * group, group), group)
-                    left[at * group : (at + 1) * group, :] = turned[rows, :]
-                size = len(starts) * group
-                value = jnp.dot(
-                    left[:size, :row_count], grads[0][:, columns], preferred_element_type=jnp.float32
-                ) + jnp.dot(
-                    left[:size, row_count:], grads[1][:, columns], preferred_element_type=jnp.float32
-                )
-                out[...] = value.astype(out.dtype)
-
-        product(
-            by_plane,
-            slice(split, out_width),
-            [[(here ^ far_) * chips + at for at in range(chips)] for far_ in range(planes)],
-        )
-        product(
-            by_chip,
-            slice(0, split),
-            [[at * chips + (chip ^ far_) for at in range(planes)] for far_ in range(chips)],
-        )
-
-    def shape(rows, columns, away):
-        return jax.ShapeDtypeStruct((rows, columns), jnp.float32 if away == 0 else jnp.bfloat16)
-
-    outs = pl.pallas_call(
-        kernel,
-        out_shape=[shape(chips * group, out_width - split, away) for away in range(planes)]
-        + [shape(planes * group, split, away) for away in range(chips)],
-        in_specs=[VMEM] * (2 * chips + 2),
-        out_specs=[VMEM] * (planes + chips),
-        scratch_shapes=[
-            pltpu.VMEM((full, 2 * row_count), jnp.bfloat16),
-            pltpu.VMEM((max(planes, chips) * group, 2 * row_count), jnp.bfloat16),
-        ],
+    return kernel, jax.ShapeDtypeStruct((chips * width, 2 * row_count), near[0].dtype)
+
+
+def weight_gradient(turned, grad_near, grad_far, columns, axis, chips, planes, pieces=None):
+    row_count = grad_near.shape[0]
+    if pieces is None:
+        turn, shape, sources = None, turned.shape, [turned]
+    else:
+        turn, target = turn_over(*pieces)
+        shape, sources = target.shape, [*pieces[0], *pieces[1]]
+    group = shape[0] // (planes * chips * 2)
+    size = planes if axis == "dp" else chips
+    other = chips if axis == "dp" else planes
+
+    def kernel(*refs):
+        ins, rest = refs[: len(sources)], refs[len(sources) :]
+        grads, outs, left = rest[:2], rest[2 : 2 + size], rest[-1]
+        flat = ins[0]
+        if turn is not None:
+            flat = rest[2 + size]
+            turn(*ins, flat)
+        chip, core = place()
+        plane = lax.axis_index("dp")
+        for away, out in enumerate(outs):
+            for at in range(other):
+                start = (plane ^ away) * chips + at if axis == "dp" else at * chips + (chip ^ away)
+                rows = pl.ds(pl.multiple_of((start * 2 + core) * group, group), group)
+                left[at * group : (at + 1) * group, :] = flat[rows, :]
+            value = jnp.dot(
+                left[:, :row_count], grads[0][:, columns], preferred_element_type=jnp.float32
+            ) + jnp.dot(
+                left[:, row_count:], grads[1][:, columns], preferred_element_type=jnp.float32
+            )
+            out[...] = value.astype(out.dtype)
+
+    width = columns.stop - columns.start
+    shapes = [
+        jax.ShapeDtypeStruct((other * group, width), jnp.float32 if away == 0 else jnp.bfloat16)
+        for away in range(size)
+    ]
+    if turn is not None:
+        shapes.append(target)
+    return pl.pallas_call(
+        kernel,
+        out_shape=shapes,
+        in_specs=[VMEM] * (len(sources) + 2),
+        out_specs=[VMEM] * len(shapes),
+        scratch_shapes=[pltpu.VMEM((other * group, 2 * row_count), jnp.bfloat16)],
         compiler_params=params(32),
         cost_estimate=pl.CostEstimate(
-            flops=2 * full * row_count * out_width,
-            bytes_accessed=4 * row_count * out_width,
+            flops=2 * shape[0] * row_count * width,
+            bytes_accessed=4 * row_count * width,
             transcendentals=0,
         ),
         name="weight_gradient",
-    )(*near, *far, grad_near, grad_far)
-    return outs[:planes], outs[planes:]
+    )(*sources, grad_near, grad_far)
 
 
 def project(pieces, out_weight, chips, width):
@@ -405,11 +407,15 @@
     others = [other_core(piece) for piece in mine]
     out_width = out_weight.shape[1]
     split = out_width * 11 // 16
-    by_plane, by_chip = weight_gradient(
-        mine, others, grad_near, grad_far, chips, width, planes, split
+    grads = (grad_near, grad_far)
+    *by_chip, turned = weight_gradient(
+        None, *grads, slice(0, split), "seq", chips, planes, (mine, others, chips, width)
+    )
+    gathered = spread(by_chip)
+    by_plane = weight_gradient(
+        turned, *grads, slice(split, out_width), "dp", chips, planes
     )
     met = meet(by_plane)
-    gathered = spread(by_chip)
     mixed_out = project(mine, out_weight, chips, width)[None]
     lefts = meet(add_up(gathered[0], gathered[1:], "dp", planes))
     rights = spread(add_up(met[0], met[1:], "seq", chips))

time: 98.7 us -> 98.9 us (level)
    pallas_call x1 -> x2, Pallas kernels: 3.11 us -> 3.25 us  [weight_gradient(): pl.pallas_call(kernel, out_shape=shapes, in_specs=[VMEM] * (len(sources)...]
where the time goes in v2:
time: 98.9 us; the launch traced here: 98.7 us
  waiting for transfers between devices  36.7 us (37%)
  starting transfers between devices  34.3 us (35%)
  Pallas kernels  26.9 us (27%)
    ppermute x33, waiting for transfers between devices, over(): return lax.ppermute(value, axis, [(i, i ^ mask) for i in range(size)])  36.7 us
    ppermute x33, starting transfers between devices, over(): return lax.ppermute(value, axis, [(i, i ^ mask) for i in range(size)])  34.3 us
    pallas_call x3, Pallas kernels, attend(): pl.pallas_call(kernel, out_shape=[jax.ShapeDtypeStruct((row_count, width)...  15.7 us
    pallas_call x3, Pallas kernels, cut(): pl.pallas_call(kernel, out_shape=[shape] * len(aways), in_specs=[HBM] * c...  3.82 us
    pallas_call x2, Pallas kernels, weight_gradient(): pl.pallas_call(kernel, out_shape=shapes, in_specs=[VMEM] * (len(sources)...  3.25 us
    pallas_call x1, Pallas kernels, project(): pl.pallas_call(kernel, out_shape=jax.ShapeDtypeStruct((row_count, out_wid...  2.93 us
  transfers between devices with their start and end apart: 33, of which 7 were waited for; matrix products, arithmetic and copies ran while one was open for 0% of the time, Pallas kernels for 22%

profile of v2, /device:TPU:0, one launch (start us, length us, event | category | flops | bytes accessed | tf_op | source)
XLA Modules:
  0.0 98.7 jit_solution(12434090456453470897)
XLA Ops:
  0.6 1.5 %cut.4 = (bf16[384,512]{1,0:T(8,128)(2,1)S(1)}, bf16[384,512]{1,0:T(8,128)(2,1)S(1)}, bf16[384,512]{1,0:T(8,128)(2,1)S(1)}) custom-call(bf16[384,1024]{1,0:T(8,128)(2,1)} %bitcast.8, bf16[384,1024]{1,0:T(8,128)(2,1)} %bitcast.10), custom_call_target="tpu_custom_call" | custom-call | tf_op jit(solution)/shard_map/cut/pallas_call | solution.py:55
  2.2 3.0 %collective-permute-start = (bf16[384,512]{1,0:T(8,128)(2,1)S(1)}, bf16[384,512]{1,0:T(8,128)(2,1)S(1)}, u32[]{:S(2)}, u32[]{:S(2)}) collective-permute-start(bf16[384,512]{1,0:T(8,128)(2,1)S(1)} %get-tuple-element.30), channel_id=1, source_target_pairs={{0,2},{1,3},{2,0},{3,1},{4,6},{5,7},{6,4},{7,5},{8,10},{9,11},{10,... | collective-permute-start | bytes 1179656 | tf_op jit(solution)/shard_map/ppermute | solution.py:381
  5.2 1.5 %collective-permute-start.1 = (bf16[384,512]{1,0:T(8,128)(2,1)S(1)}, bf16[384,512]{1,0:T(8,128)(2,1)S(1)}, u32[]{:S(2)}, u32[]{:S(2)}) collective-permute-start(bf16[384,512]{1,0:T(8,128)(2,1)S(1)} %get-tuple-element.31), channel_id=1, source_target_pairs={{0,4},{1,5},{2,6},{3,7},{4,0},{5,1},{6,2},{7,3},{8,12},{9,13},{10,... | collective-permute-start | bytes 1179656 | tf_op jit(solution)/shard_map/ppermute | solution.py:381
  6.7 1.0 %cut.5 = bf16[384,512]{1,0:T(8,128)(2,1)S(1)} custom-call(bf16[384,1024]{1,0:T(8,128)(2,1)} %bitcast.9, bf16[384,1024]{1,0:T(8,128)(2,1)} %bitcast.11), custom_call_target="tpu_custom_call" | custom-call | tf_op jit(solution)/shard_map/cut/pallas_call | solution.py:55
  8.2 7.0 %collective-permute-done.refs_1_ = bf16[384,512]{1,0:T(8,128)(2,1)S(1)} collective-permute-done((bf16[384,512]{1,0:T(8,128)(2,1)S(1)}, bf16[384,512]{1,0:T(8,128)(2,1)S(1)}, u32[]{:S(2)}, u32[]{:S(2)}) %collective-permute-start) | collective-permute-done | bytes 393248 | tf_op jit(solution)/shard_map/ppermute | solution.py:381
  15.2 10.0 %collective-permute-done.1.refs_2_ = bf16[384,512]{1,0:T(8,128)(2,1)S(1)} collective-permute-done((bf16[384,512]{1,0:T(8,128)(2,1)S(1)}, bf16[384,512]{1,0:T(8,128)(2,1)S(1)}, u32[]{:S(2)}, u32[]{:S(2)}) %collective-permute-start.1) | collective-permute-done | bytes 393248 | tf_op jit(solution)/shard_map/ppermute | solution.py:381
  25.7 1.3 %cut.3 = (bf16[384,256]{1,0:T(8,128)(2,1)S(1)}, bf16[384,256]{1,0:T(8,128)(2,1)S(1)}, bf16[384,256]{1,0:T(8,128)(2,1)S(1)}, bf16[384,256]{1,0:T(8,128)(2,1)S(1)}) custom-call(bf16[384,1024]{1,0:T(8,128)(2,1)} %bitcast.13), custom_call_target="tpu_custom_call" | custom-call | tf_op jit(solution)/shard_map/cut/pallas_call | solution.py:55
  27.0 1.6 %collective-permute-start.10 = (bf16[384,256]{1,0:T(8,128)(2,1)S(1)}, bf16[384,256]{1,0:T(8,128)(2,1)S(1)}, u32[]{:S(2)}, u32[]{:S(2)}) collective-permute-start(bf16[384,256]{1,0:T(8,128)(2,1)S(1)} %get-tuple-element.33), channel_id=1, source_target_pairs={{0,4},{1,5},{2,6},{3,7},{4,0},{5,1},{6,2},{7,3},{8,12},{9,13},{10,... | collective-permute-start | bytes 589832 | tf_op jit(solution)/shard_map/ppermute | solution.py:381
  29.1 1.5 %collective-permute-start.7 = (s32[384]{0:T(512)S(1)}, s32[384]{0:T(512)S(1)}, u32[]{:S(2)}, u32[]{:S(2)}) collective-permute-start(s32[384]{0:T(512)S(1)} %copy-done.2), channel_id=1, source_target_pairs={{0,2},{1,3},{2,0},{3,1},{4,6},{5,7},{6,4},{7,5},{8,10},{9,11},{10,... | collective-permute-start | bytes 4616 | tf_op jit(solution)/shard_map/ppermute | solution.py:381
  31.3 3.8 %collective-permute-done.7.refs_0_ = s32[384]{0:T(512)S(1)} collective-permute-done((s32[384]{0:T(512)S(1)}, s32[384]{0:T(512)S(1)}, u32[]{:S(2)}, u32[]{:S(2)}) %collective-permute-start.7) | collective-permute-done | bytes 1568 | tf_op jit(solution)/shard_map/ppermute | solution.py:381
  35.5 2.6 %collective-permute-start.14 = (bf16[384,256]{1,0:T(8,128)(2,1)S(1)}, bf16[384,256]{1,0:T(8,128)(2,1)S(1)}, u32[]{:S(2)}, u32[]{:S(2)}) collective-permute-start(bf16[384,256]{1,0:T(8,128)(2,1)S(1)} %get-tuple-element.36), channel_id=1, source_target_pairs={{0,6},{1,7},{2,4},{3,5},{4,2},{5,3},{6,0},{7,1},{8,14},{9,15},{10,... | collective-permute-start | bytes 589832 | tf_op jit(solution)/shard_map/ppermute | solution.py:381
  38.1 8.3 %attend.4 = (bf16[384,256]{1,0:T(8,128)(2,1)S(1)}, bf16[384,256]{1,0:T(8,128)(2,1)S(1)}) custom-call(s32[384]{0:T(512)S(1)} %collective-permute-done.7.refs_0_, s32[384]{0:T(512)S(1)} %collective-permute-done.8.refs_1_, bf16[384,256]{1,0:T(8,128)(2,1)S(1)} %collective-permute-done.9.refs_2_, bf16[384,256]{1,0:T(8,128)(2,1)S(1)} %collective-permute-done.10.refs_3_, ...), custom_call_target="tpu_custom_call" | custom-call | flops 2415919104 | bytes 3145728 | tf_op jit(solution)/shard_map/attend/pallas_call | solution.py:193
  47.3 4.6 %attend.5 = bf16[384,256]{1,0:T(8,128)(2,1)S(1)} custom-call(s32[384]{0:T(512)S(1)} %collective-permute-done.13.refs_0_, bf16[384,256]{1,0:T(8,128)(2,1)S(1)} %collective-permute-done.14.refs_1_, bf16[3072,512]{1,0:T(8,128)(2,1)S(1)} %assemble.1.refs_2_.refs_4_), custom_call_target="tpu_custom_call" | custom-call | flops 1207959552 | bytes 3145728 | tf_op jit(solution)/shard_map/attend/pallas_call | solution.py:193
  52.7 2.8 %attend.3.refs_0_ = bf16[384,256]{1,0:T(8,128)(2,1)S(1)} custom-call(s32[384]{0:T(512)S(1)} %copy-done.2, bf16[384,256]{1,0:T(8,128)(2,1)S(1)} %get-tuple-element.28.refs_1_, bf16[3072,512]{1,0:T(8,128)(2,1)S(1)} %assemble.1.refs_2_.refs_4_), custom_call_target="tpu_custom_call" | custom-call | flops 1207959552 | bytes 3145728 | tf_op jit(solution)/shard_map/attend/pallas_call | solution.py:193
  56.2 2.4 %collective-permute-done.15.refs_3_ = bf16[384,256]{1,0:T(8,128)(2,1)S(1)} collective-permute-done((bf16[384,256]{1,0:T(8,128)(2,1)S(1)}, bf16[384,256]{1,0:T(8,128)(2,1)S(1)}, u32[]{:S(2)}, u32[]{:S(2)}) %collective-permute-start.15) | collective-permute-done | bytes 196640 | tf_op jit(solution)/shard_map/ppermute | solution.py:381
  58.6 1.4 %collective-permute-done.19.refs_7_ = bf16[384,256]{1,0:T(8,128)(2,1)S(1)} collective-permute-done((bf16[384,256]{1,0:T(8,128)(2,1)S(1)}, bf16[384,256]{1,0:T(8,128)(2,1)S(1)}, u32[]{:S(2)}, u32[]{:S(2)}) %collective-permute-start.19) | collective-permute-done | bytes 196640 | tf_op jit(solution)/shard_map/ppermute | solution.py:381
  60.0 2.3 %weight_gradient.2 = (f32[128,1408]{1,0:T(8,128)S(1)}, bf16[128,1408]{1,0:T(8,128)(2,1)S(1)}, bf16[128,1408]{1,0:T(8,128)(2,1)S(1)}, bf16[128,1408]{1,0:T(8,128)(2,1)S(1)}, bf16[1024,768]{1,0:T(8,128)(2,1)S(1)}) custom-call(bf16[384,256]{1,0:T(8,128)(2,1)S(1)} %attend.3.refs_0_, bf16[384,256]{1,0:T(8,128)(2,1)S(1)} %collective-permute-done.11.refs_1_, ...), custom_call_target="tpu_custom_call" | custom-call | flops 1107296256 | bytes 2162688 | tf_op jit(solution)/shard_map/weight_gradient/pallas_call | solution.py:271
  62.3 1.0 %weight_gradient.3 = (f32[128,640]{1,0:T(8,128)S(1)}, bf16[128,640]{1,0:T(8,128)(2,1)S(1)}, bf16[128,640]{1,0:T(8,128)(2,1)S(1)}, bf16[128,640]{1,0:T(8,128)(2,1)S(1)}) custom-call(bf16[1024,768]{1,0:T(8,128)(2,1)S(1)} %get-tuple-element.45.refs_0_, bf16[384,2048]{1,0:T(8,128)(2,1)S(1)} %bitcast.7, bf16[384,2048]{1,0:T(8,128)(2,1)S(1)} %collective-permute-done.20.refs_9_.refs_2_), custom_call_target="tpu_custom_call" | custom-call | flops 503316480 | bytes 983040 | tf_op jit(solution)/shard_map/weight_gradient/pallas_call | solution.py:271
  63.3 1.8 %collective-permute-start.27 = (bf16[128,640]{1,0:T(8,128)(2,1)S(1)}, bf16[128,640]{1,0:T(8,128)(2,1)S(1)}, u32[]{:S(2)}, u32[]{:S(2)}) collective-permute-start(bf16[128,640]{1,0:T(8,128)(2,1)S(1)} %get-tuple-element.47), channel_id=1, source_target_pairs={{0,8},{8,0},{16,24},{24,16},{1,9},{9,1},{17,25},{25,17},{2,10},{10... | collective-permute-start | bytes 491528 | tf_op jit(solution)/shard_map/ppermute | solution.py:381
  65.1 1.5 %collective-permute-start.21 = (bf16[128,1408]{1,0:T(8,128)(2,1)S(1)}, bf16[128,1408]{1,0:T(8,128)(2,1)S(1)}, u32[]{:S(2)}, u32[]{:S(2)}) collective-permute-start(bf16[128,1408]{1,0:T(8,128)(2,1)S(1)} %get-tuple-element.38), channel_id=1, source_target_pairs={{0,2},{1,3},{2,0},{3,1},{4,6},{5,7},{6,4},{7,5},{8,10},{9,11},{10,... | collective-permute-start | bytes 1081352 | tf_op jit(solution)/shard_map/ppermute | solution.py:381
  66.6 1.0 collective-permute-start.22
  67.6 1.0 collective-permute-start.23
  68.6 2.6 %collective-permute-start.28 = (bf16[128,640]{1,0:T(8,128)(2,1)S(1)}, bf16[128,640]{1,0:T(8,128)(2,1)S(1)}, u32[]{:S(2)}, u32[]{:S(2)}) collective-permute-start(bf16[128,640]{1,0:T(8,128)(2,1)S(1)} %get-tuple-element.48), channel_id=1, source_target_pairs={{0,16},{8,24},{16,0},{24,8},{1,17},{9,25},{17,1},{25,9},{2,18},{10... | collective-permute-start | bytes 491528 | tf_op jit(solution)/shard_map/ppermute | solution.py:381
  71.2 2.2 %collective-permute-start.29 = (bf16[128,640]{1,0:T(8,128)(2,1)S(1)}, bf16[128,640]{1,0:T(8,128)(2,1)S(1)}, u32[]{:S(2)}, u32[]{:S(2)}) collective-permute-start(bf16[128,640]{1,0:T(8,128)(2,1)S(1)} %get-tuple-element.49), channel_id=1, source_target_pairs={{0,24},{8,16},{16,8},{24,0},{1,25},{9,17},{17,9},{25,1},{2,26},{10... | collective-permute-start | bytes 491528 | tf_op jit(solution)/shard_map/ppermute | solution.py:381
  73.3 9.0 %collective-permute-done.28.refs_2_ = bf16[128,640]{1,0:T(8,128)(2,1)S(1)} collective-permute-done((bf16[128,640]{1,0:T(8,128)(2,1)S(1)}, bf16[128,640]{1,0:T(8,128)(2,1)S(1)}, u32[]{:S(2)}, u32[]{:S(2)}) %collective-permute-start.28) | collective-permute-done | bytes 163872 | tf_op jit(solution)/shard_map/ppermute | solution.py:381
  82.5 1.7 %collective-permute-start.30 = (bf16[32,640]{1,0:T(8,128)(2,1)S(1)}, bf16[32,640]{1,0:T(8,128)(2,1)S(1)}, u32[]{:S(2)}, u32[]{:S(2)}) collective-permute-start(bf16[32,640]{1,0:T(8,128)(2,1)S(1)} %get-tuple-element.51), channel_id=1, source_target_pairs={{0,2},{1,3},{2,0},{3,1},{4,6},{5,7},{6,4},{7,5},{8,10},{9,11},{10,... | collective-permute-start | bytes 122888 | tf_op jit(solution)/shard_map/ppermute | solution.py:381
  84.2 1.0 collective-permute-start.31
  86.2 3.3 %collective-permute-start.24 = (bf16[32,1408]{1,0:T(8,128)(2,1)S(1)}, bf16[32,1408]{1,0:T(8,128)(2,1)S(1)}, u32[]{:S(2)}, u32[]{:S(2)}) collective-permute-start(bf16[32,1408]{1,0:T(8,128)(2,1)S(1)} %get-tuple-element.42), channel_id=1, source_target_pairs={{0,8},{8,0},{16,24},{24,16},{1,9},{9,1},{17,25},{25,17},{2,10},{10... | collective-permute-start | bytes 270344 | tf_op jit(solution)/shard_map/ppermute | solution.py:381
  89.5 1.2 %collective-permute-start.25 = (bf16[32,1408]{1,0:T(8,128)(2,1)S(1)}, bf16[32,1408]{1,0:T(8,128)(2,1)S(1)}, u32[]{:S(2)}, u32[]{:S(2)}) collective-permute-start(bf16[32,1408]{1,0:T(8,128)(2,1)S(1)} %get-tuple-element.43), channel_id=1, source_target_pairs={{0,16},{8,24},{16,0},{24,8},{1,17},{9,25},{17,1},{25,9},{2,18},{10... | collective-permute-start | bytes 270344 | tf_op jit(solution)/shard_map/ppermute | solution.py:381
  90.7 1.4 %collective-permute-start.26 = (bf16[32,1408]{1,0:T(8,128)(2,1)S(1)}, bf16[32,1408]{1,0:T(8,128)(2,1)S(1)}, u32[]{:S(2)}, u32[]{:S(2)}) collective-permute-start(bf16[32,1408]{1,0:T(8,128)(2,1)S(1)} %get-tuple-element.44), channel_id=1, source_target_pairs={{0,24},{8,16},{16,8},{24,0},{1,25},{9,17},{17,9},{25,1},{2,26},{10... | collective-permute-start | bytes 270344 | tf_op jit(solution)/shard_map/ppermute | solution.py:381
  92.1 2.9 %project.1 = bf16[384,2048]{1,0:T(8,128)(2,1)} custom-call(bf16[384,256]{1,0:T(8,128)(2,1)S(1)} %attend.3.refs_0_, bf16[384,256]{1,0:T(8,128)(2,1)S(1)} %collective-permute-done.11.refs_1_, bf16[384,256]{1,0:T(8,128)(2,1)S(1)} %collective-permute-done.12.refs_2_, bf16[384,256]{1,0:T(8,128)(2,1)S(1)} %collective-permute-done.15.refs_3_, ...), custom_call_target="tpu_custom_call" | custom-call | flops 1610612736 | bytes 4194304 | tf_op jit(solution)/shard_map/project/pallas_call | solution.py:307
  95.0 2.9 %collective-permute-done.25.refs_2_ = bf16[32,1408]{1,0:T(8,128)(2,1)S(1)} collective-permute-done((bf16[32,1408]{1,0:T(8,128)(2,1)S(1)}, bf16[32,1408]{1,0:T(8,128)(2,1)S(1)}, u32[]{:S(2)}, u32[]{:S(2)}) %collective-permute-start.25) | collective-permute-done | bytes 90144 | tf_op jit(solution)/shard_map/ppermute | solution.py:381
  (53 shorter events, 6.9 us)
Async XLA Ops:
  2.2 13.0 %collective-permute-start = (bf16[384,512]{1,0:T(8,128)(2,1)S(1)}, bf16[384,512]{1,0:T(8,128)(2,1)S(1)}, u32[]{:S(2)}, u32[]{:S(2)}) collective-permute-start(bf16[384,512]{1,0:T(8,128)(2,1)S(1)} %get-tuple-element.30), channel_id=1, source_target_pairs={{0,2},{1,3},{2,0},{3,1},{4,6},{5,7},{6,4},{7,5},{8,10},{9,11},{10,... | collective-permute-start | bytes 1179656 | tf_op jit(solution)/shard_map/ppermute | solution.py:381
  5.2 54.8 %collective-permute-start.20 = (bf16[384,2048]{1,0:T(8,128)(2,1)S(1)}, bf16[384,2048]{1,0:T(8,128)(2,1)S(1)}, u32[]{:S(2)}, u32[]{:S(2)}) collective-permute-start(bf16[384,2048]{1,0:T(8,128)(2,1)S(1)} %bitcast.5), channel_id=1, source_target_pairs={{0,1},{1,0},{2,3},{3,2},{4,5},{5,4},{6,7},{7,6},{8,9},{9,8},{10,11... | collective-permute-start | bytes 4718600 | tf_op jit(solution)/shard_map/ppermute | solution.py:381
  5.2 20.0 %collective-permute-start.1 = (bf16[384,512]{1,0:T(8,128)(2,1)S(1)}, bf16[384,512]{1,0:T(8,128)(2,1)S(1)}, u32[]{:S(2)}, u32[]{:S(2)}) collective-permute-start(bf16[384,512]{1,0:T(8,128)(2,1)S(1)} %get-tuple-element.31), channel_id=1, source_target_pairs={{0,4},{1,5},{2,6},{3,7},{4,0},{5,1},{6,2},{7,3},{8,12},{9,13},{10,... | collective-permute-start | bytes 1179656 | tf_op jit(solution)/shard_map/ppermute | solution.py:381
  7.8 17.4 %collective-permute-start.2 = (bf16[384,512]{1,0:T(8,128)(2,1)S(1)}, bf16[384,512]{1,0:T(8,128)(2,1)S(1)}, u32[]{:S(2)}, u32[]{:S(2)}) collective-permute-start(bf16[384,512]{1,0:T(8,128)(2,1)S(1)} %cut.5), channel_id=1, source_target_pairs={{0,6},{1,7},{2,4},{3,5},{4,2},{5,3},{6,0},{7,1},{8,14},{9,15},{10,... | collective-permute-start | bytes 1179656 | tf_op jit(solution)/shard_map/ppermute | solution.py:381
  8.1 18.9 %collective-permute-start.3 = (bf16[384,512]{1,0:T(8,128)(2,1)S(1)}, bf16[384,512]{1,0:T(8,128)(2,1)S(1)}, u32[]{:S(2)}, u32[]{:S(2)}) collective-permute-start(bf16[384,512]{1,0:T(8,128)(2,1)S(1)} %get-tuple-element.29.refs_0_), channel_id=1, source_target_pairs={{0,1},{1,0},{2,3},{3,2},{4,5},{5,4},{6,7},{7,6},{8,9},{9,8},{10,11... | collective-permute-start | bytes 1179656 | tf_op jit(solution)/shard_map/ppermute | solution.py:381
  15.2 13.4 %collective-permute-start.4 = (bf16[384,512]{1,0:T(8,128)(2,1)S(1)}, bf16[384,512]{1,0:T(8,128)(2,1)S(1)}, u32[]{:S(2)}, u32[]{:S(2)}) collective-permute-start(bf16[384,512]{1,0:T(8,128)(2,1)S(1)} %collective-permute-done.refs_1_), channel_id=1, source_target_pairs={{0,1},{1,0},{2,3},{3,2},{4,5},{5,4},{6,7},{7,6},{8,9},{9,8},{10,11... | collective-permute-start | bytes 1179656 | tf_op jit(solution)/shard_map/ppermute | solution.py:381
  25.2 3.9 %collective-permute-start.5 = (bf16[384,512]{1,0:T(8,128)(2,1)S(1)}, bf16[384,512]{1,0:T(8,128)(2,1)S(1)}, u32[]{:S(2)}, u32[]{:S(2)}) collective-permute-start(bf16[384,512]{1,0:T(8,128)(2,1)S(1)} %collective-permute-done.1.refs_2_), channel_id=1, source_target_pairs={{0,1},{1,0},{2,3},{3,2},{4,5},{5,4},{6,7},{7,6},{8,9},{9,8},{10,11... | collective-permute-start | bytes 1179656 | tf_op jit(solution)/shard_map/ppermute | solution.py:381
  25.2 5.4 %collective-permute-start.6 = (bf16[384,512]{1,0:T(8,128)(2,1)S(1)}, bf16[384,512]{1,0:T(8,128)(2,1)S(1)}, u32[]{:S(2)}, u32[]{:S(2)}) collective-permute-start(bf16[384,512]{1,0:T(8,128)(2,1)S(1)} %collective-permute-done.2.refs_3_), channel_id=1, source_target_pairs={{0,1},{1,0},{2,3},{3,2},{4,5},{5,4},{6,7},{7,6},{8,9},{9,8},{10,11... | collective-permute-start | bytes 1179656 | tf_op jit(solution)/shard_map/ppermute | solution.py:381
  27.0 11.1 %collective-permute-start.10 = (bf16[384,256]{1,0:T(8,128)(2,1)S(1)}, bf16[384,256]{1,0:T(8,128)(2,1)S(1)}, u32[]{:S(2)}, u32[]{:S(2)}) collective-permute-start(bf16[384,256]{1,0:T(8,128)(2,1)S(1)} %get-tuple-element.33), channel_id=1, source_target_pairs={{0,4},{1,5},{2,6},{3,7},{4,0},{5,1},{6,2},{7,3},{8,12},{9,13},{10,... | collective-permute-start | bytes 589832 | tf_op jit(solution)/shard_map/ppermute | solution.py:381
  28.6 9.5 %collective-permute-start.9 = (bf16[384,256]{1,0:T(8,128)(2,1)S(1)}, bf16[384,256]{1,0:T(8,128)(2,1)S(1)}, u32[]{:S(2)}, u32[]{:S(2)}) collective-permute-start(bf16[384,256]{1,0:T(8,128)(2,1)S(1)} %get-tuple-element.32), channel_id=1, source_target_pairs={{0,2},{1,3},{2,0},{3,1},{4,6},{5,7},{6,4},{7,5},{8,10},{9,11},{10,... | collective-permute-start | bytes 589832 | tf_op jit(solution)/shard_map/ppermute | solution.py:381
  29.1 6.0 %collective-permute-start.7 = (s32[384]{0:T(512)S(1)}, s32[384]{0:T(512)S(1)}, u32[]{:S(2)}, u32[]{:S(2)}) collective-permute-start(s32[384]{0:T(512)S(1)} %copy-done.2), channel_id=1, source_target_pairs={{0,2},{1,3},{2,0},{3,1},{4,6},{5,7},{6,4},{7,5},{8,10},{9,11},{10,... | collective-permute-start | bytes 4616 | tf_op jit(solution)/shard_map/ppermute | solution.py:381
  30.6 4.9 %collective-permute-start.8 = (s32[384]{0:T(512)S(1)}, s32[384]{0:T(512)S(1)}, u32[]{:S(2)}, u32[]{:S(2)}) collective-permute-start(s32[384]{0:T(512)S(1)} %copy-done.2), channel_id=1, source_target_pairs={{0,4},{1,5},{2,6},{3,7},{4,0},{5,1},{6,2},{7,3},{8,12},{9,13},{10,... | collective-permute-start | bytes 4616 | tf_op jit(solution)/shard_map/ppermute | solution.py:381
  35.1 12.2 %collective-permute-start.13 = (s32[384]{0:T(512)S(1)}, s32[384]{0:T(512)S(1)}, u32[]{:S(2)}, u32[]{:S(2)}) collective-permute-start(s32[384]{0:T(512)S(1)} %copy-done.2), channel_id=1, source_target_pairs={{0,6},{1,7},{2,4},{3,5},{4,2},{5,3},{6,0},{7,1},{8,14},{9,15},{10,... | collective-permute-start | bytes 4616 | tf_op jit(solution)/shard_map/ppermute | solution.py:381
  35.5 11.9 %collective-permute-start.14 = (bf16[384,256]{1,0:T(8,128)(2,1)S(1)}, bf16[384,256]{1,0:T(8,128)(2,1)S(1)}, u32[]{:S(2)}, u32[]{:S(2)}) collective-permute-start(bf16[384,256]{1,0:T(8,128)(2,1)S(1)} %get-tuple-element.36), channel_id=1, source_target_pairs={{0,6},{1,7},{2,4},{3,5},{4,2},{5,3},{6,0},{7,1},{8,14},{9,15},{10,... | collective-permute-start | bytes 589832 | tf_op jit(solution)/shard_map/ppermute | solution.py:381
  46.4 9.3 %collective-permute-start.11 = (bf16[384,256]{1,0:T(8,128)(2,1)S(1)}, bf16[384,256]{1,0:T(8,128)(2,1)S(1)}, u32[]{:S(2)}, u32[]{:S(2)}) collective-permute-start(bf16[384,256]{1,0:T(8,128)(2,1)S(1)} %get-tuple-element.34), channel_id=1, source_target_pairs={{0,2},{1,3},{2,0},{3,1},{4,6},{5,7},{6,4},{7,5},{8,10},{9,11},{10,... | collective-permute-start | bytes 589832 | tf_op jit(solution)/shard_map/ppermute | solution.py:381
  46.4 9.7 %collective-permute-start.12 = (bf16[384,256]{1,0:T(8,128)(2,1)S(1)}, bf16[384,256]{1,0:T(8,128)(2,1)S(1)}, u32[]{:S(2)}, u32[]{:S(2)}) collective-permute-start(bf16[384,256]{1,0:T(8,128)(2,1)S(1)} %get-tuple-element.35), channel_id=1, source_target_pairs={{0,4},{1,5},{2,6},{3,7},{4,0},{5,1},{6,2},{7,3},{8,12},{9,13},{10,... | collective-permute-start | bytes 589832 | tf_op jit(solution)/shard_map/ppermute | solution.py:381
  51.9 6.6 %collective-permute-start.15 = (bf16[384,256]{1,0:T(8,128)(2,1)S(1)}, bf16[384,256]{1,0:T(8,128)(2,1)S(1)}, u32[]{:S(2)}, u32[]{:S(2)}) collective-permute-start(bf16[384,256]{1,0:T(8,128)(2,1)S(1)} %attend.5), channel_id=1, source_target_pairs={{0,6},{1,7},{2,4},{3,5},{4,2},{5,3},{6,0},{7,1},{8,14},{9,15},{10,... | collective-permute-start | bytes 589832 | tf_op jit(solution)/shard_map/ppermute | solution.py:381
  55.5 3.1 %collective-permute-start.16 = (bf16[384,256]{1,0:T(8,128)(2,1)S(1)}, bf16[384,256]{1,0:T(8,128)(2,1)S(1)}, u32[]{:S(2)}, u32[]{:S(2)}) collective-permute-start(bf16[384,256]{1,0:T(8,128)(2,1)S(1)} %attend.3.refs_0_), channel_id=1, source_target_pairs={{0,1},{1,0},{2,3},{3,2},{4,5},{5,4},{6,7},{7,6},{8,9},{9,8},{10,11... | collective-permute-start | bytes 589832 | tf_op jit(solution)/shard_map/ppermute | solution.py:381
  55.6 3.0 %collective-permute-start.17 = (bf16[384,256]{1,0:T(8,128)(2,1)S(1)}, bf16[384,256]{1,0:T(8,128)(2,1)S(1)}, u32[]{:S(2)}, u32[]{:S(2)}) collective-permute-start(bf16[384,256]{1,0:T(8,128)(2,1)S(1)} %collective-permute-done.11.refs_1_), channel_id=1, source_target_pairs={{0,1},{1,0},{2,3},{3,2},{4,5},{5,4},{6,7},{7,6},{8,9},{9,8},{10,11... | collective-permute-start | bytes 589832 | tf_op jit(solution)/shard_map/ppermute | solution.py:381
  56.1 2.5 %collective-permute-start.18 = (bf16[384,256]{1,0:T(8,128)(2,1)S(1)}, bf16[384,256]{1,0:T(8,128)(2,1)S(1)}, u32[]{:S(2)}, u32[]{:S(2)}) collective-permute-start(bf16[384,256]{1,0:T(8,128)(2,1)S(1)} %collective-permute-done.12.refs_2_), channel_id=1, source_target_pairs={{0,1},{1,0},{2,3},{3,2},{4,5},{5,4},{6,7},{7,6},{8,9},{9,8},{10,11... | collective-permute-start | bytes 589832 | tf_op jit(solution)/shard_map/ppermute | solution.py:381
  63.3 7.9 %collective-permute-start.27 = (bf16[128,640]{1,0:T(8,128)(2,1)S(1)}, bf16[128,640]{1,0:T(8,128)(2,1)S(1)}, u32[]{:S(2)}, u32[]{:S(2)}) collective-permute-start(bf16[128,640]{1,0:T(8,128)(2,1)S(1)} %get-tuple-element.47), channel_id=1, source_target_pairs={{0,8},{8,0},{16,24},{24,16},{1,9},{9,1},{17,25},{25,17},{2,10},{10... | collective-permute-start | bytes 491528 | tf_op jit(solution)/shard_map/ppermute | solution.py:381
  65.1 20.1 %collective-permute-start.21 = (bf16[128,1408]{1,0:T(8,128)(2,1)S(1)}, bf16[128,1408]{1,0:T(8,128)(2,1)S(1)}, u32[]{:S(2)}, u32[]{:S(2)}) collective-permute-start(bf16[128,1408]{1,0:T(8,128)(2,1)S(1)} %get-tuple-element.38), channel_id=1, source_target_pairs={{0,2},{1,3},{2,0},{3,1},{4,6},{5,7},{6,4},{7,5},{8,10},{9,11},{10,... | collective-permute-start | bytes 1081352 | tf_op jit(solution)/shard_map/ppermute | solution.py:381
  66.6 19.4 %collective-permute-start.22 = (bf16[128,1408]{1,0:T(8,128)(2,1)S(1)}, bf16[128,1408]{1,0:T(8,128)(2,1)S(1)}, u32[]{:S(2)}, u32[]{:S(2)}) collective-permute-start(bf16[128,1408]{1,0:T(8,128)(2,1)S(1)} %get-tuple-element.39), channel_id=1, source_target_pairs={{0,4},{1,5},{2,6},{3,7},{4,0},{5,1},{6,2},{7,3},{8,12},{9,13},{10,... | collective-permute-start | bytes 1081352 | tf_op jit(solution)/shard_map/ppermute | solution.py:381
  67.6 18.5 %collective-permute-start.23 = (bf16[128,1408]{1,0:T(8,128)(2,1)S(1)}, bf16[128,1408]{1,0:T(8,128)(2,1)S(1)}, u32[]{:S(2)}, u32[]{:S(2)}) collective-permute-start(bf16[128,1408]{1,0:T(8,128)(2,1)S(1)} %get-tuple-element.40), channel_id=1, source_target_pairs={{0,6},{1,7},{2,4},{3,5},{4,2},{5,3},{6,0},{7,1},{8,14},{9,15},{10,... | collective-permute-start | bytes 1081352 | tf_op jit(solution)/shard_map/ppermute | solution.py:381
  68.6 13.8 %collective-permute-start.28 = (bf16[128,640]{1,0:T(8,128)(2,1)S(1)}, bf16[128,640]{1,0:T(8,128)(2,1)S(1)}, u32[]{:S(2)}, u32[]{:S(2)}) collective-permute-start(bf16[128,640]{1,0:T(8,128)(2,1)S(1)} %get-tuple-element.48), channel_id=1, source_target_pairs={{0,16},{8,24},{16,0},{24,8},{1,17},{9,25},{17,1},{25,9},{2,18},{10... | collective-permute-start | bytes 491528 | tf_op jit(solution)/shard_map/ppermute | solution.py:381
  71.2 11.2 %collective-permute-start.29 = (bf16[128,640]{1,0:T(8,128)(2,1)S(1)}, bf16[128,640]{1,0:T(8,128)(2,1)S(1)}, u32[]{:S(2)}, u32[]{:S(2)}) collective-permute-start(bf16[128,640]{1,0:T(8,128)(2,1)S(1)} %get-tuple-element.49), channel_id=1, source_target_pairs={{0,24},{8,16},{16,8},{24,0},{1,25},{9,17},{17,9},{25,1},{2,26},{10... | collective-permute-start | bytes 491528 | tf_op jit(solution)/shard_map/ppermute | solution.py:381
  82.5 8.2 %collective-permute-start.30 = (bf16[32,640]{1,0:T(8,128)(2,1)S(1)}, bf16[32,640]{1,0:T(8,128)(2,1)S(1)}, u32[]{:S(2)}, u32[]{:S(2)}) collective-permute-start(bf16[32,640]{1,0:T(8,128)(2,1)S(1)} %get-tuple-element.51), channel_id=1, source_target_pairs={{0,2},{1,3},{2,0},{3,1},{4,6},{5,7},{6,4},{7,5},{8,10},{9,11},{10,... | collective-permute-start | bytes 122888 | tf_op jit(solution)/shard_map/ppermute | solution.py:381
  84.2 10.8 %collective-permute-start.31 = (bf16[32,640]{1,0:T(8,128)(2,1)S(1)}, bf16[32,640]{1,0:T(8,128)(2,1)S(1)}, u32[]{:S(2)}, u32[]{:S(2)}) collective-permute-start(bf16[32,640]{1,0:T(8,128)(2,1)S(1)} %get-tuple-element.52), channel_id=1, source_target_pairs={{0,4},{1,5},{2,6},{3,7},{4,0},{5,1},{6,2},{7,3},{8,12},{9,13},{10,... | collective-permute-start | bytes 122888 | tf_op jit(solution)/shard_map/ppermute | solution.py:381
  85.1 9.9 %collective-permute-start.32 = (bf16[32,640]{1,0:T(8,128)(2,1)S(1)}, bf16[32,640]{1,0:T(8,128)(2,1)S(1)}, u32[]{:S(2)}, u32[]{:S(2)}) collective-permute-start(bf16[32,640]{1,0:T(8,128)(2,1)S(1)} %get-tuple-element.53), channel_id=1, source_target_pairs={{0,6},{1,7},{2,4},{3,5},{4,2},{5,3},{6,0},{7,1},{8,14},{9,15},{10,... | collective-permute-start | bytes 122888 | tf_op jit(solution)/shard_map/ppermute | solution.py:381
  86.2 8.8 %collective-permute-start.24 = (bf16[32,1408]{1,0:T(8,128)(2,1)S(1)}, bf16[32,1408]{1,0:T(8,128)(2,1)S(1)}, u32[]{:S(2)}, u32[]{:S(2)}) collective-permute-start(bf16[32,1408]{1,0:T(8,128)(2,1)S(1)} %get-tuple-element.42), channel_id=1, source_target_pairs={{0,8},{8,0},{16,24},{24,16},{1,9},{9,1},{17,25},{25,17},{2,10},{10... | collective-permute-start | bytes 270344 | tf_op jit(solution)/shard_map/ppermute | solution.py:381
  89.5 8.4 %collective-permute-start.25 = (bf16[32,1408]{1,0:T(8,128)(2,1)S(1)}, bf16[32,1408]{1,0:T(8,128)(2,1)S(1)}, u32[]{:S(2)}, u32[]{:S(2)}) collective-permute-start(bf16[32,1408]{1,0:T(8,128)(2,1)S(1)} %get-tuple-element.43), channel_id=1, source_target_pairs={{0,16},{8,24},{16,0},{24,8},{1,17},{9,25},{17,1},{25,9},{2,18},{10... | collective-permute-start | bytes 270344 | tf_op jit(solution)/shard_map/ppermute | solution.py:381
  90.7 7.3 %collective-permute-start.26 = (bf16[32,1408]{1,0:T(8,128)(2,1)S(1)}, bf16[32,1408]{1,0:T(8,128)(2,1)S(1)}, u32[]{:S(2)}, u32[]{:S(2)}) collective-permute-start(bf16[32,1408]{1,0:T(8,128)(2,1)S(1)} %get-tuple-element.44), channel_id=1, source_target_pairs={{0,24},{8,16},{16,8},{24,0},{1,25},{9,17},{17,9},{25,1},{2,26},{10... | collective-permute-start | bytes 270344 | tf_op jit(solution)/shard_map/ppermute | solution.py:381
  (4 other events, 62.7 us)

commit v3 on v2

--- a/solution.py
+++ b/solution.py
@@ -105,7 +105,7 @@
             shifts, factors = [], []
             for head in range(heads):
                 columns = slice(head * HEAD, (head + 1) * HEAD)
-                query = qbuf[index, :, columns]
+                query = q_in[0][:, columns] if count == 1 else qbuf[index, :, columns]
                 top = None
                 for at in range(base, base + steps * step_k, step_k):
                     score = lax.dot_general(
@@ -146,7 +146,8 @@
 
         starts, limits = [], []
         for index, away in enumerate(aways):
-            qbuf[index] = q_in[index][...]
+            if count > 1:
+                qbuf[index] = q_in[index][...]
             start = ((chip ^ away) * 2 + core) * row_count
             limit = [ends_in[index][0]]
             for _ in range(SCALES - 1):
@@ -180,11 +181,17 @@
                     part(index, room, base, steps)
 
             for head in range(heads):
-                obuf[index, :, head * HEAD : (head + 1) * HEAD] = (
-                    sums[head] / jnp.sum(tallies[head], axis=1, keepdims=True)
-                ).astype(obuf.dtype)
+                value = sums[head] / jnp.sum(tallies[head], axis=1, keepdims=True)
+                columns = slice(head * HEAD, (head + 1) * HEAD)
+                if count == 1:
+                    outs[0][:, columns] = value.astype(obuf.dtype)
+                else:
+                    obuf[index, :, columns] = value.astype(obuf.dtype)
             return carry
 
+        if count == 1:
+            turn(0, 0)
+            return
         lax.fori_loop(0, count, turn, 0)
         for index in range(count):
             outs[index][...] = obuf[index]
@@ -249,17 +256,22 @@
             turn(*ins, flat)
         chip, core = place()
         plane = lax.axis_index("dp")
-        for away, out in enumerate(outs):
+        for away in range(size):
             for at in range(other):
                 start = (plane ^ away) * chips + at if axis == "dp" else at * chips + (chip ^ away)
                 rows = pl.ds(pl.multiple_of((start * 2 + core) * group, group), group)
-                left[at * group : (at + 1) * group, :] = flat[rows, :]
+                target = (away * other + at) * group
+                left[target : target + group, :] = flat[rows, :]
+        for first in range(columns.start, columns.stop, 512):
+            part = slice(first, min(first + 512, columns.stop))
             value = jnp.dot(
-                left[:, :row_count], grads[0][:, columns], preferred_element_type=jnp.float32
-            ) + jnp.dot(
-                left[:, row_count:], grads[1][:, columns], preferred_element_type=jnp.float32
-            )
-            out[...] = value.astype(out.dtype)
+                left[:, :row_count], grads[0][:, part], preferred_element_type=jnp.float32
+            ) + jnp.dot(left[:, row_count:], grads[1][:, part], preferred_element_type=jnp.float32)
+            for away, out in enumerate(outs):
+                rows = slice(away * other * group, (away + 1) * other * group)
+                out[:, part.start - columns.start : part.stop - columns.start] = value[rows].astype(
+                    out.dtype
+                )
 
     width = columns.stop - columns.start
     shapes = [
@@ -273,7 +285,7 @@
         out_shape=shapes,
         in_specs=[VMEM] * (len(sources) + 2),
         out_specs=[VMEM] * len(shapes),
-        scratch_shapes=[pltpu.VMEM((other * group, 2 * row_count), jnp.bfloat16)],
+        scratch_shapes=[pltpu.VMEM((size * other * group, 2 * row_count), jnp.bfloat16)],
         compiler_params=params(32),
         cost_estimate=pl.CostEstimate(
             flops=2 * shape[0] * row_count * width,

time: 98.9 us -> 98.7 us (level)
  no operation moved by 1% of the time
where the time goes in v3:
time: 98.7 us; the launch traced here: 98.5 us
  waiting for transfers between devices  36.7 us (37%)
  starting transfers between devices  34.3 us (35%)
  Pallas kernels  26.7 us (27%)
    ppermute x33, waiting for transfers between devices, over(): return lax.ppermute(value, axis, [(i, i ^ mask) for i in range(size)])  36.7 us
    ppermute x33, starting transfers between devices, over(): return lax.ppermute(value, axis, [(i, i ^ mask) for i in range(size)])  34.3 us
    pallas_call x3, Pallas kernels, attend(): pl.pallas_call(kernel, out_shape=[jax.ShapeDtypeStruct((row_count, width)...  15.6 us
    pallas_call x3, Pallas kernels, cut(): pl.pallas_call(kernel, out_shape=[shape] * len(aways), in_specs=[HBM] * c...  3.82 us
    pallas_call x2, Pallas kernels, weight_gradient(): pl.pallas_call(kernel, out_shape=shapes, in_specs=[VMEM] * (len(sources)...  3.1 us
    pallas_call x1, Pallas kernels, project(): pl.pallas_call(kernel, out_shape=jax.ShapeDtypeStruct((row_count, out_wid...  2.93 us
  transfers between devices with their start and end apart: 33, of which 7 were waited for; matrix products, arithmetic and copies ran while one was open for 0% of the time, Pallas kernels for 22%

profile of v3, /device:TPU:0, one launch (start us, length us, event | category | flops | bytes accessed | tf_op | source)
XLA Modules:
  0.0 98.5 jit_solution(22925714255566413)
XLA Ops:
  0.6 1.5 %cut.4 = (bf16[384,512]{1,0:T(8,128)(2,1)S(1)}, bf16[384,512]{1,0:T(8,128)(2,1)S(1)}, bf16[384,512]{1,0:T(8,128)(2,1)S(1)}) custom-call(bf16[384,1024]{1,0:T(8,128)(2,1)} %bitcast.8, bf16[384,1024]{1,0:T(8,128)(2,1)} %bitcast.10), custom_call_target="tpu_custom_call" | custom-call | tf_op jit(solution)/shard_map/cut/pallas_call | solution.py:55
  2.2 3.0 %collective-permute-start = (bf16[384,512]{1,0:T(8,128)(2,1)S(1)}, bf16[384,512]{1,0:T(8,128)(2,1)S(1)}, u32[]{:S(2)}, u32[]{:S(2)}) collective-permute-start(bf16[384,512]{1,0:T(8,128)(2,1)S(1)} %get-tuple-element.30), channel_id=1, source_target_pairs={{0,2},{1,3},{2,0},{3,1},{4,6},{5,7},{6,4},{7,5},{8,10},{9,11},{10,... | collective-permute-start | bytes 1179656 | tf_op jit(solution)/shard_map/ppermute | solution.py:393
  5.2 1.5 %collective-permute-start.1 = (bf16[384,512]{1,0:T(8,128)(2,1)S(1)}, bf16[384,512]{1,0:T(8,128)(2,1)S(1)}, u32[]{:S(2)}, u32[]{:S(2)}) collective-permute-start(bf16[384,512]{1,0:T(8,128)(2,1)S(1)} %get-tuple-element.31), channel_id=1, source_target_pairs={{0,4},{1,5},{2,6},{3,7},{4,0},{5,1},{6,2},{7,3},{8,12},{9,13},{10,... | collective-permute-start | bytes 1179656 | tf_op jit(solution)/shard_map/ppermute | solution.py:393
  6.7 1.0 %cut.5 = bf16[384,512]{1,0:T(8,128)(2,1)S(1)} custom-call(bf16[384,1024]{1,0:T(8,128)(2,1)} %bitcast.9, bf16[384,1024]{1,0:T(8,128)(2,1)} %bitcast.11), custom_call_target="tpu_custom_call" | custom-call | tf_op jit(solution)/shard_map/cut/pallas_call | solution.py:55
  8.2 7.0 %collective-permute-done.refs_1_ = bf16[384,512]{1,0:T(8,128)(2,1)S(1)} collective-permute-done((bf16[384,512]{1,0:T(8,128)(2,1)S(1)}, bf16[384,512]{1,0:T(8,128)(2,1)S(1)}, u32[]{:S(2)}, u32[]{:S(2)}) %collective-permute-start) | collective-permute-done | bytes 393248 | tf_op jit(solution)/shard_map/ppermute | solution.py:393
  15.2 10.0 %collective-permute-done.1.refs_2_ = bf16[384,512]{1,0:T(8,128)(2,1)S(1)} collective-permute-done((bf16[384,512]{1,0:T(8,128)(2,1)S(1)}, bf16[384,512]{1,0:T(8,128)(2,1)S(1)}, u32[]{:S(2)}, u32[]{:S(2)}) %collective-permute-start.1) | collective-permute-done | bytes 393248 | tf_op jit(solution)/shard_map/ppermute | solution.py:393
  25.7 1.3 %cut.3 = (bf16[384,256]{1,0:T(8,128)(2,1)S(1)}, bf16[384,256]{1,0:T(8,128)(2,1)S(1)}, bf16[384,256]{1,0:T(8,128)(2,1)S(1)}, bf16[384,256]{1,0:T(8,128)(2,1)S(1)}) custom-call(bf16[384,1024]{1,0:T(8,128)(2,1)} %bitcast.13), custom_call_target="tpu_custom_call" | custom-call | tf_op jit(solution)/shard_map/cut/pallas_call | solution.py:55
  27.0 1.6 %collective-permute-start.10 = (bf16[384,256]{1,0:T(8,128)(2,1)S(1)}, bf16[384,256]{1,0:T(8,128)(2,1)S(1)}, u32[]{:S(2)}, u32[]{:S(2)}) collective-permute-start(bf16[384,256]{1,0:T(8,128)(2,1)S(1)} %get-tuple-element.33), channel_id=1, source_target_pairs={{0,4},{1,5},{2,6},{3,7},{4,0},{5,1},{6,2},{7,3},{8,12},{9,13},{10,... | collective-permute-start | bytes 589832 | tf_op jit(solution)/shard_map/ppermute | solution.py:393
  29.1 1.5 %collective-permute-start.7 = (s32[384]{0:T(512)S(1)}, s32[384]{0:T(512)S(1)}, u32[]{:S(2)}, u32[]{:S(2)}) collective-permute-start(s32[384]{0:T(512)S(1)} %copy-done.2), channel_id=1, source_target_pairs={{0,2},{1,3},{2,0},{3,1},{4,6},{5,7},{6,4},{7,5},{8,10},{9,11},{10,... | collective-permute-start | bytes 4616 | tf_op jit(solution)/shard_map/ppermute | solution.py:393
  31.3 3.8 %collective-permute-done.7.refs_0_ = s32[384]{0:T(512)S(1)} collective-permute-done((s32[384]{0:T(512)S(1)}, s32[384]{0:T(512)S(1)}, u32[]{:S(2)}, u32[]{:S(2)}) %collective-permute-start.7) | collective-permute-done | bytes 1568 | tf_op jit(solution)/shard_map/ppermute | solution.py:393
  35.5 2.6 %collective-permute-start.14 = (bf16[384,256]{1,0:T(8,128)(2,1)S(1)}, bf16[384,256]{1,0:T(8,128)(2,1)S(1)}, u32[]{:S(2)}, u32[]{:S(2)}) collective-permute-start(bf16[384,256]{1,0:T(8,128)(2,1)S(1)} %get-tuple-element.36), channel_id=1, source_target_pairs={{0,6},{1,7},{2,4},{3,5},{4,2},{5,3},{6,0},{7,1},{8,14},{9,15},{10,... | collective-permute-start | bytes 589832 | tf_op jit(solution)/shard_map/ppermute | solution.py:393
  38.1 8.3 %attend.4 = (bf16[384,256]{1,0:T(8,128)(2,1)S(1)}, bf16[384,256]{1,0:T(8,128)(2,1)S(1)}) custom-call(s32[384]{0:T(512)S(1)} %collective-permute-done.7.refs_0_, s32[384]{0:T(512)S(1)} %collective-permute-done.8.refs_1_, bf16[384,256]{1,0:T(8,128)(2,1)S(1)} %collective-permute-done.9.refs_2_, bf16[384,256]{1,0:T(8,128)(2,1)S(1)} %collective-permute-done.10.refs_3_, ...), custom_call_target="tpu_custom_call" | custom-call | flops 2415919104 | bytes 3145728 | tf_op jit(solution)/shard_map/attend/pallas_call | solution.py:200
  47.3 4.6 %attend.5 = bf16[384,256]{1,0:T(8,128)(2,1)S(1)} custom-call(s32[384]{0:T(512)S(1)} %collective-permute-done.13.refs_0_, bf16[384,256]{1,0:T(8,128)(2,1)S(1)} %collective-permute-done.14.refs_1_, bf16[3072,512]{1,0:T(8,128)(2,1)S(1)} %assemble.1.refs_2_.refs_4_), custom_call_target="tpu_custom_call" | custom-call | flops 1207959552 | bytes 3145728 | tf_op jit(solution)/shard_map/attend/pallas_call | solution.py:200
  52.7 2.7 %attend.3.refs_0_ = bf16[384,256]{1,0:T(8,128)(2,1)S(1)} custom-call(s32[384]{0:T(512)S(1)} %copy-done.2, bf16[384,256]{1,0:T(8,128)(2,1)S(1)} %get-tuple-element.28.refs_1_, bf16[3072,512]{1,0:T(8,128)(2,1)S(1)} %assemble.1.refs_2_.refs_4_), custom_call_target="tpu_custom_call" | custom-call | flops 1207959552 | bytes 3145728 | tf_op jit(solution)/shard_map/attend/pallas_call | solution.py:200
  56.1 2.4 %collective-permute-done.15.refs_3_ = bf16[384,256]{1,0:T(8,128)(2,1)S(1)} collective-permute-done((bf16[384,256]{1,0:T(8,128)(2,1)S(1)}, bf16[384,256]{1,0:T(8,128)(2,1)S(1)}, u32[]{:S(2)}, u32[]{:S(2)}) %collective-permute-start.15) | collective-permute-done | bytes 196640 | tf_op jit(solution)/shard_map/ppermute | solution.py:393
  58.6 1.4 %collective-permute-done.19.refs_7_ = bf16[384,256]{1,0:T(8,128)(2,1)S(1)} collective-permute-done((bf16[384,256]{1,0:T(8,128)(2,1)S(1)}, bf16[384,256]{1,0:T(8,128)(2,1)S(1)}, u32[]{:S(2)}, u32[]{:S(2)}) %collective-permute-start.19) | collective-permute-done | bytes 196640 | tf_op jit(solution)/shard_map/ppermute | solution.py:393
  60.0 2.2 %weight_gradient.2 = (f32[128,1408]{1,0:T(8,128)S(1)}, bf16[128,1408]{1,0:T(8,128)(2,1)S(1)}, bf16[128,1408]{1,0:T(8,128)(2,1)S(1)}, bf16[128,1408]{1,0:T(8,128)(2,1)S(1)}, bf16[1024,768]{1,0:T(8,128)(2,1)S(1)}) custom-call(bf16[384,256]{1,0:T(8,128)(2,1)S(1)} %attend.3.refs_0_, bf16[384,256]{1,0:T(8,128)(2,1)S(1)} %collective-permute-done.11.refs_1_, ...), custom_call_target="tpu_custom_call" | custom-call | flops 1107296256 | bytes 2162688 | tf_op jit(solution)/shard_map/weight_gradient/pallas_call | solution.py:283
  63.1 1.8 %collective-permute-start.27 = (bf16[128,640]{1,0:T(8,128)(2,1)S(1)}, bf16[128,640]{1,0:T(8,128)(2,1)S(1)}, u32[]{:S(2)}, u32[]{:S(2)}) collective-permute-start(bf16[128,640]{1,0:T(8,128)(2,1)S(1)} %get-tuple-element.47), channel_id=1, source_target_pairs={{0,8},{8,0},{16,24},{24,16},{1,9},{9,1},{17,25},{25,17},{2,10},{10... | collective-permute-start | bytes 491528 | tf_op jit(solution)/shard_map/ppermute | solution.py:393
  64.9 1.5 %collective-permute-start.21 = (bf16[128,1408]{1,0:T(8,128)(2,1)S(1)}, bf16[128,1408]{1,0:T(8,128)(2,1)S(1)}, u32[]{:S(2)}, u32[]{:S(2)}) collective-permute-start(bf16[128,1408]{1,0:T(8,128)(2,1)S(1)} %get-tuple-element.38), channel_id=1, source_target_pairs={{0,2},{1,3},{2,0},{3,1},{4,6},{5,7},{6,4},{7,5},{8,10},{9,11},{10,... | collective-permute-start | bytes 1081352 | tf_op jit(solution)/shard_map/ppermute | solution.py:393
  66.4 0.9 collective-permute-start.22
  67.3 1.1 %collective-permute-start.23 = (bf16[128,1408]{1,0:T(8,128)(2,1)S(1)}, bf16[128,1408]{1,0:T(8,128)(2,1)S(1)}, u32[]{:S(2)}, u32[]{:S(2)}) collective-permute-start(bf16[128,1408]{1,0:T(8,128)(2,1)S(1)} %get-tuple-element.40), channel_id=1, source_target_pairs={{0,6},{1,7},{2,4},{3,5},{4,2},{5,3},{6,0},{7,1},{8,14},{9,15},{10,... | collective-permute-start | bytes 1081352 | tf_op jit(solution)/shard_map/ppermute | solution.py:393
  68.4 2.6 %collective-permute-start.28 = (bf16[128,640]{1,0:T(8,128)(2,1)S(1)}, bf16[128,640]{1,0:T(8,128)(2,1)S(1)}, u32[]{:S(2)}, u32[]{:S(2)}) collective-permute-start(bf16[128,640]{1,0:T(8,128)(2,1)S(1)} %get-tuple-element.48), channel_id=1, source_target_pairs={{0,16},{8,24},{16,0},{24,8},{1,17},{9,25},{17,1},{25,9},{2,18},{10... | collective-permute-start | bytes 491528 | tf_op jit(solution)/shard_map/ppermute | solution.py:393
  71.0 2.2 %collective-permute-start.29 = (bf16[128,640]{1,0:T(8,128)(2,1)S(1)}, bf16[128,640]{1,0:T(8,128)(2,1)S(1)}, u32[]{:S(2)}, u32[]{:S(2)}) collective-permute-start(bf16[128,640]{1,0:T(8,128)(2,1)S(1)} %get-tuple-element.49), channel_id=1, source_target_pairs={{0,24},{8,16},{16,8},{24,0},{1,25},{9,17},{17,9},{25,1},{2,26},{10... | collective-permute-start | bytes 491528 | tf_op jit(solution)/shard_map/ppermute | solution.py:393
  73.2 9.0 %collective-permute-done.28.refs_2_ = bf16[128,640]{1,0:T(8,128)(2,1)S(1)} collective-permute-done((bf16[128,640]{1,0:T(8,128)(2,1)S(1)}, bf16[128,640]{1,0:T(8,128)(2,1)S(1)}, u32[]{:S(2)}, u32[]{:S(2)}) %collective-permute-start.28) | collective-permute-done | bytes 163872 | tf_op jit(solution)/shard_map/ppermute | solution.py:393
  82.3 1.6 %collective-permute-start.30 = (bf16[32,640]{1,0:T(8,128)(2,1)S(1)}, bf16[32,640]{1,0:T(8,128)(2,1)S(1)}, u32[]{:S(2)}, u32[]{:S(2)}) collective-permute-start(bf16[32,640]{1,0:T(8,128)(2,1)S(1)} %get-tuple-element.51), channel_id=1, source_target_pairs={{0,2},{1,3},{2,0},{3,1},{4,6},{5,7},{6,4},{7,5},{8,10},{9,11},{10,... | collective-permute-start | bytes 122888 | tf_op jit(solution)/shard_map/ppermute | solution.py:393
  83.9 1.0 collective-permute-start.31
  84.9 1.0 collective-permute-start.32
  86.0 3.3 %collective-permute-start.24 = (bf16[32,1408]{1,0:T(8,128)(2,1)S(1)}, bf16[32,1408]{1,0:T(8,128)(2,1)S(1)}, u32[]{:S(2)}, u32[]{:S(2)}) collective-permute-start(bf16[32,1408]{1,0:T(8,128)(2,1)S(1)} %get-tuple-element.42), channel_id=1, source_target_pairs={{0,8},{8,0},{16,24},{24,16},{1,9},{9,1},{17,25},{25,17},{2,10},{10... | collective-permute-start | bytes 270344 | tf_op jit(solution)/shard_map/ppermute | solution.py:393
  89.3 1.2 %collective-permute-start.25 = (bf16[32,1408]{1,0:T(8,128)(2,1)S(1)}, bf16[32,1408]{1,0:T(8,128)(2,1)S(1)}, u32[]{:S(2)}, u32[]{:S(2)}) collective-permute-start(bf16[32,1408]{1,0:T(8,128)(2,1)S(1)} %get-tuple-element.43), channel_id=1, source_target_pairs={{0,16},{8,24},{16,0},{24,8},{1,17},{9,25},{17,1},{25,9},{2,18},{10... | collective-permute-start | bytes 270344 | tf_op jit(solution)/shard_map/ppermute | solution.py:393
  90.5 1.4 %collective-permute-start.26 = (bf16[32,1408]{1,0:T(8,128)(2,1)S(1)}, bf16[32,1408]{1,0:T(8,128)(2,1)S(1)}, u32[]{:S(2)}, u32[]{:S(2)}) collective-permute-start(bf16[32,1408]{1,0:T(8,128)(2,1)S(1)} %get-tuple-element.44), channel_id=1, source_target_pairs={{0,24},{8,16},{16,8},{24,0},{1,25},{9,17},{17,9},{25,1},{2,26},{10... | collective-permute-start | bytes 270344 | tf_op jit(solution)/shard_map/ppermute | solution.py:393
  91.9 2.9 %project.1 = bf16[384,2048]{1,0:T(8,128)(2,1)} custom-call(bf16[384,256]{1,0:T(8,128)(2,1)S(1)} %attend.3.refs_0_, bf16[384,256]{1,0:T(8,128)(2,1)S(1)} %collective-permute-done.11.refs_1_, bf16[384,256]{1,0:T(8,128)(2,1)S(1)} %collective-permute-done.12.refs_2_, bf16[384,256]{1,0:T(8,128)(2,1)S(1)} %collective-permute-done.15.refs_3_, ...), custom_call_target="tpu_custom_call" | custom-call | flops 1610612736 | bytes 4194304 | tf_op jit(solution)/shard_map/project/pallas_call | solution.py:319
  94.8 2.9 %collective-permute-done.25.refs_2_ = bf16[32,1408]{1,0:T(8,128)(2,1)S(1)} collective-permute-done((bf16[32,1408]{1,0:T(8,128)(2,1)S(1)}, bf16[32,1408]{1,0:T(8,128)(2,1)S(1)}, u32[]{:S(2)}, u32[]{:S(2)}) %collective-permute-start.25) | collective-permute-done | bytes 90144 | tf_op jit(solution)/shard_map/ppermute | solution.py:393
  (53 shorter events, 6.9 us)
Async XLA Ops:
  2.2 13.0 %collective-permute-start = (bf16[384,512]{1,0:T(8,128)(2,1)S(1)}, bf16[384,512]{1,0:T(8,128)(2,1)S(1)}, u32[]{:S(2)}, u32[]{:S(2)}) collective-permute-start(bf16[384,512]{1,0:T(8,128)(2,1)S(1)} %get-tuple-element.30), channel_id=1, source_target_pairs={{0,2},{1,3},{2,0},{3,1},{4,6},{5,7},{6,4},{7,5},{8,10},{9,11},{10,... | collective-permute-start | bytes 1179656 | tf_op jit(solution)/shard_map/ppermute | solution.py:393
  5.2 54.8 %collective-permute-start.20 = (bf16[384,2048]{1,0:T(8,128)(2,1)S(1)}, bf16[384,2048]{1,0:T(8,128)(2,1)S(1)}, u32[]{:S(2)}, u32[]{:S(2)}) collective-permute-start(bf16[384,2048]{1,0:T(8,128)(2,1)S(1)} %bitcast.5), channel_id=1, source_target_pairs={{0,1},{1,0},{2,3},{3,2},{4,5},{5,4},{6,7},{7,6},{8,9},{9,8},{10,11... | collective-permute-start | bytes 4718600 | tf_op jit(solution)/shard_map/ppermute | solution.py:393
  5.2 20.0 %collective-permute-start.1 = (bf16[384,512]{1,0:T(8,128)(2,1)S(1)}, bf16[384,512]{1,0:T(8,128)(2,1)S(1)}, u32[]{:S(2)}, u32[]{:S(2)}) collective-permute-start(bf16[384,512]{1,0:T(8,128)(2,1)S(1)} %get-tuple-element.31), channel_id=1, source_target_pairs={{0,4},{1,5},{2,6},{3,7},{4,0},{5,1},{6,2},{7,3},{8,12},{9,13},{10,... | collective-permute-start | bytes 1179656 | tf_op jit(solution)/shard_map/ppermute | solution.py:393
  7.8 17.4 %collective-permute-start.2 = (bf16[384,512]{1,0:T(8,128)(2,1)S(1)}, bf16[384,512]{1,0:T(8,128)(2,1)S(1)}, u32[]{:S(2)}, u32[]{:S(2)}) collective-permute-start(bf16[384,512]{1,0:T(8,128)(2,1)S(1)} %cut.5), channel_id=1, source_target_pairs={{0,6},{1,7},{2,4},{3,5},{4,2},{5,3},{6,0},{7,1},{8,14},{9,15},{10,... | collective-permute-start | bytes 1179656 | tf_op jit(solution)/shard_map/ppermute | solution.py:393
  8.1 18.9 %collective-permute-start.3 = (bf16[384,512]{1,0:T(8,128)(2,1)S(1)}, bf16[384,512]{1,0:T(8,128)(2,1)S(1)}, u32[]{:S(2)}, u32[]{:S(2)}) collective-permute-start(bf16[384,512]{1,0:T(8,128)(2,1)S(1)} %get-tuple-element.29.refs_0_), channel_id=1, source_target_pairs={{0,1},{1,0},{2,3},{3,2},{4,5},{5,4},{6,7},{7,6},{8,9},{9,8},{10,11... | collective-permute-start | bytes 1179656 | tf_op jit(solution)/shard_map/ppermute | solution.py:393
  15.2 13.4 %collective-permute-start.4 = (bf16[384,512]{1,0:T(8,128)(2,1)S(1)}, bf16[384,512]{1,0:T(8,128)(2,1)S(1)}, u32[]{:S(2)}, u32[]{:S(2)}) collective-permute-start(bf16[384,512]{1,0:T(8,128)(2,1)S(1)} %collective-permute-done.refs_1_), channel_id=1, source_target_pairs={{0,1},{1,0},{2,3},{3,2},{4,5},{5,4},{6,7},{7,6},{8,9},{9,8},{10,11... | collective-permute-start | bytes 1179656 | tf_op jit(solution)/shard_map/ppermute | solution.py:393
  25.2 3.9 %collective-permute-start.5 = (bf16[384,512]{1,0:T(8,128)(2,1)S(1)}, bf16[384,512]{1,0:T(8,128)(2,1)S(1)}, u32[]{:S(2)}, u32[]{:S(2)}) collective-permute-start(bf16[384,512]{1,0:T(8,128)(2,1)S(1)} %collective-permute-done.1.refs_2_), channel_id=1, source_target_pairs={{0,1},{1,0},{2,3},{3,2},{4,5},{5,4},{6,7},{7,6},{8,9},{9,8},{10,11... | collective-permute-start | bytes 1179656 | tf_op jit(solution)/shard_map/ppermute | solution.py:393
  25.2 5.4 %collective-permute-start.6 = (bf16[384,512]{1,0:T(8,128)(2,1)S(1)}, bf16[384,512]{1,0:T(8,128)(2,1)S(1)}, u32[]{:S(2)}, u32[]{:S(2)}) collective-permute-start(bf16[384,512]{1,0:T(8,128)(2,1)S(1)} %collective-permute-done.2.refs_3_), channel_id=1, source_target_pairs={{0,1},{1,0},{2,3},{3,2},{4,5},{5,4},{6,7},{7,6},{8,9},{9,8},{10,11... | collective-permute-start | bytes 1179656 | tf_op jit(solution)/shard_map/ppermute | solution.py:393
  27.0 11.1 %collective-permute-start.10 = (bf16[384,256]{1,0:T(8,128)(2,1)S(1)}, bf16[384,256]{1,0:T(8,128)(2,1)S(1)}, u32[]{:S(2)}, u32[]{:S(2)}) collective-permute-start(bf16[384,256]{1,0:T(8,128)(2,1)S(1)} %get-tuple-element.33), channel_id=1, source_target_pairs={{0,4},{1,5},{2,6},{3,7},{4,0},{5,1},{6,2},{7,3},{8,12},{9,13},{10,... | collective-permute-start | bytes 589832 | tf_op jit(solution)/shard_map/ppermute | solution.py:393
  28.6 9.5 %collective-permute-start.9 = (bf16[384,256]{1,0:T(8,128)(2,1)S(1)}, bf16[384,256]{1,0:T(8,128)(2,1)S(1)}, u32[]{:S(2)}, u32[]{:S(2)}) collective-permute-start(bf16[384,256]{1,0:T(8,128)(2,1)S(1)} %get-tuple-element.32), channel_id=1, source_target_pairs={{0,2},{1,3},{2,0},{3,1},{4,6},{5,7},{6,4},{7,5},{8,10},{9,11},{10,... | collective-permute-start | bytes 589832 | tf_op jit(solution)/shard_map/ppermute | solution.py:393
  29.1 6.0 %collective-permute-start.7 = (s32[384]{0:T(512)S(1)}, s32[384]{0:T(512)S(1)}, u32[]{:S(2)}, u32[]{:S(2)}) collective-permute-start(s32[384]{0:T(512)S(1)} %copy-done.2), channel_id=1, source_target_pairs={{0,2},{1,3},{2,0},{3,1},{4,6},{5,7},{6,4},{7,5},{8,10},{9,11},{10,... | collective-permute-start | bytes 4616 | tf_op jit(solution)/shard_map/ppermute | solution.py:393
  30.6 4.9 %collective-permute-start.8 = (s32[384]{0:T(512)S(1)}, s32[384]{0:T(512)S(1)}, u32[]{:S(2)}, u32[]{:S(2)}) collective-permute-start(s32[384]{0:T(512)S(1)} %copy-done.2), channel_id=1, source_target_pairs={{0,4},{1,5},{2,6},{3,7},{4,0},{5,1},{6,2},{7,3},{8,12},{9,13},{10,... | collective-permute-start | bytes 4616 | tf_op jit(solution)/shard_map/ppermute | solution.py:393
  35.1 12.2 %collective-permute-start.13 = (s32[384]{0:T(512)S(1)}, s32[384]{0:T(512)S(1)}, u32[]{:S(2)}, u32[]{:S(2)}) collective-permute-start(s32[384]{0:T(512)S(1)} %copy-done.2), channel_id=1, source_target_pairs={{0,6},{1,7},{2,4},{3,5},{4,2},{5,3},{6,0},{7,1},{8,14},{9,15},{10,... | collective-permute-start | bytes 4616 | tf_op jit(solution)/shard_map/ppermute | solution.py:393
  35.5 11.9 %collective-permute-start.14 = (bf16[384,256]{1,0:T(8,128)(2,1)S(1)}, bf16[384,256]{1,0:T(8,128)(2,1)S(1)}, u32[]{:S(2)}, u32[]{:S(2)}) collective-permute-start(bf16[384,256]{1,0:T(8,128)(2,1)S(1)} %get-tuple-element.36), channel_id=1, source_target_pairs={{0,6},{1,7},{2,4},{3,5},{4,2},{5,3},{6,0},{7,1},{8,14},{9,15},{10,... | collective-permute-start | bytes 589832 | tf_op jit(solution)/shard_map/ppermute | solution.py:393
  46.4 9.2 %collective-permute-start.11 = (bf16[384,256]{1,0:T(8,128)(2,1)S(1)}, bf16[384,256]{1,0:T(8,128)(2,1)S(1)}, u32[]{:S(2)}, u32[]{:S(2)}) collective-permute-start(bf16[384,256]{1,0:T(8,128)(2,1)S(1)} %get-tuple-element.34), channel_id=1, source_target_pairs={{0,2},{1,3},{2,0},{3,1},{4,6},{5,7},{6,4},{7,5},{8,10},{9,11},{10,... | collective-permute-start | bytes 589832 | tf_op jit(solution)/shard_map/ppermute | solution.py:393
  46.4 9.6 %collective-permute-start.12 = (bf16[384,256]{1,0:T(8,128)(2,1)S(1)}, bf16[384,256]{1,0:T(8,128)(2,1)S(1)}, u32[]{:S(2)}, u32[]{:S(2)}) collective-permute-start(bf16[384,256]{1,0:T(8,128)(2,1)S(1)} %get-tuple-element.35), channel_id=1, source_target_pairs={{0,4},{1,5},{2,6},{3,7},{4,0},{5,1},{6,2},{7,3},{8,12},{9,13},{10,... | collective-permute-start | bytes 589832 | tf_op jit(solution)/shard_map/ppermute | solution.py:393
  51.9 6.6 %collective-permute-start.15 = (bf16[384,256]{1,0:T(8,128)(2,1)S(1)}, bf16[384,256]{1,0:T(8,128)(2,1)S(1)}, u32[]{:S(2)}, u32[]{:S(2)}) collective-permute-start(bf16[384,256]{1,0:T(8,128)(2,1)S(1)} %attend.5), channel_id=1, source_target_pairs={{0,6},{1,7},{2,4},{3,5},{4,2},{5,3},{6,0},{7,1},{8,14},{9,15},{10,... | collective-permute-start | bytes 589832 | tf_op jit(solution)/shard_map/ppermute | solution.py:393
  55.5 3.1 %collective-permute-start.16 = (bf16[384,256]{1,0:T(8,128)(2,1)S(1)}, bf16[384,256]{1,0:T(8,128)(2,1)S(1)}, u32[]{:S(2)}, u32[]{:S(2)}) collective-permute-start(bf16[384,256]{1,0:T(8,128)(2,1)S(1)} %attend.3.refs_0_), channel_id=1, source_target_pairs={{0,1},{1,0},{2,3},{3,2},{4,5},{5,4},{6,7},{7,6},{8,9},{9,8},{10,11... | collective-permute-start | bytes 589832 | tf_op jit(solution)/shard_map/ppermute | solution.py:393
  55.5 3.0 %collective-permute-start.17 = (bf16[384,256]{1,0:T(8,128)(2,1)S(1)}, bf16[384,256]{1,0:T(8,128)(2,1)S(1)}, u32[]{:S(2)}, u32[]{:S(2)}) collective-permute-start(bf16[384,256]{1,0:T(8,128)(2,1)S(1)} %collective-permute-done.11.refs_1_), channel_id=1, source_target_pairs={{0,1},{1,0},{2,3},{3,2},{4,5},{5,4},{6,7},{7,6},{8,9},{9,8},{10,11... | collective-permute-start | bytes 589832 | tf_op jit(solution)/shard_map/ppermute | solution.py:393
  56.0 2.5 %collective-permute-start.18 = (bf16[384,256]{1,0:T(8,128)(2,1)S(1)}, bf16[384,256]{1,0:T(8,128)(2,1)S(1)}, u32[]{:S(2)}, u32[]{:S(2)}) collective-permute-start(bf16[384,256]{1,0:T(8,128)(2,1)S(1)} %collective-permute-done.12.refs_2_), channel_id=1, source_target_pairs={{0,1},{1,0},{2,3},{3,2},{4,5},{5,4},{6,7},{7,6},{8,9},{9,8},{10,11... | collective-permute-start | bytes 589832 | tf_op jit(solution)/shard_map/ppermute | solution.py:393
  63.1 7.9 %collective-permute-start.27 = (bf16[128,640]{1,0:T(8,128)(2,1)S(1)}, bf16[128,640]{1,0:T(8,128)(2,1)S(1)}, u32[]{:S(2)}, u32[]{:S(2)}) collective-permute-start(bf16[128,640]{1,0:T(8,128)(2,1)S(1)} %get-tuple-element.47), channel_id=1, source_target_pairs={{0,8},{8,0},{16,24},{24,16},{1,9},{9,1},{17,25},{25,17},{2,10},{10... | collective-permute-start | bytes 491528 | tf_op jit(solution)/shard_map/ppermute | solution.py:393
  64.9 20.0 %collective-permute-start.21 = (bf16[128,1408]{1,0:T(8,128)(2,1)S(1)}, bf16[128,1408]{1,0:T(8,128)(2,1)S(1)}, u32[]{:S(2)}, u32[]{:S(2)}) collective-permute-start(bf16[128,1408]{1,0:T(8,128)(2,1)S(1)} %get-tuple-element.38), channel_id=1, source_target_pairs={{0,2},{1,3},{2,0},{3,1},{4,6},{5,7},{6,4},{7,5},{8,10},{9,11},{10,... | collective-permute-start | bytes 1081352 | tf_op jit(solution)/shard_map/ppermute | solution.py:393
  66.4 19.5 %collective-permute-start.22 = (bf16[128,1408]{1,0:T(8,128)(2,1)S(1)}, bf16[128,1408]{1,0:T(8,128)(2,1)S(1)}, u32[]{:S(2)}, u32[]{:S(2)}) collective-permute-start(bf16[128,1408]{1,0:T(8,128)(2,1)S(1)} %get-tuple-element.39), channel_id=1, source_target_pairs={{0,4},{1,5},{2,6},{3,7},{4,0},{5,1},{6,2},{7,3},{8,12},{9,13},{10,... | collective-permute-start | bytes 1081352 | tf_op jit(solution)/shard_map/ppermute | solution.py:393
  67.3 18.5 %collective-permute-start.23 = (bf16[128,1408]{1,0:T(8,128)(2,1)S(1)}, bf16[128,1408]{1,0:T(8,128)(2,1)S(1)}, u32[]{:S(2)}, u32[]{:S(2)}) collective-permute-start(bf16[128,1408]{1,0:T(8,128)(2,1)S(1)} %get-tuple-element.40), channel_id=1, source_target_pairs={{0,6},{1,7},{2,4},{3,5},{4,2},{5,3},{6,0},{7,1},{8,14},{9,15},{10,... | collective-permute-start | bytes 1081352 | tf_op jit(solution)/shard_map/ppermute | solution.py:393
  68.4 13.8 %collective-permute-start.28 = (bf16[128,640]{1,0:T(8,128)(2,1)S(1)}, bf16[128,640]{1,0:T(8,128)(2,1)S(1)}, u32[]{:S(2)}, u32[]{:S(2)}) collective-permute-start(bf16[128,640]{1,0:T(8,128)(2,1)S(1)} %get-tuple-element.48), channel_id=1, source_target_pairs={{0,16},{8,24},{16,0},{24,8},{1,17},{9,25},{17,1},{25,9},{2,18},{10... | collective-permute-start | bytes 491528 | tf_op jit(solution)/shard_map/ppermute | solution.py:393
  71.0 11.2 %collective-permute-start.29 = (bf16[128,640]{1,0:T(8,128)(2,1)S(1)}, bf16[128,640]{1,0:T(8,128)(2,1)S(1)}, u32[]{:S(2)}, u32[]{:S(2)}) collective-permute-start(bf16[128,640]{1,0:T(8,128)(2,1)S(1)} %get-tuple-element.49), channel_id=1, source_target_pairs={{0,24},{8,16},{16,8},{24,0},{1,25},{9,17},{17,9},{25,1},{2,26},{10... | collective-permute-start | bytes 491528 | tf_op jit(solution)/shard_map/ppermute | solution.py:393
  82.3 8.2 %collective-permute-start.30 = (bf16[32,640]{1,0:T(8,128)(2,1)S(1)}, bf16[32,640]{1,0:T(8,128)(2,1)S(1)}, u32[]{:S(2)}, u32[]{:S(2)}) collective-permute-start(bf16[32,640]{1,0:T(8,128)(2,1)S(1)} %get-tuple-element.51), channel_id=1, source_target_pairs={{0,2},{1,3},{2,0},{3,1},{4,6},{5,7},{6,4},{7,5},{8,10},{9,11},{10,... | collective-permute-start | bytes 122888 | tf_op jit(solution)/shard_map/ppermute | solution.py:393
  83.9 10.9 %collective-permute-start.31 = (bf16[32,640]{1,0:T(8,128)(2,1)S(1)}, bf16[32,640]{1,0:T(8,128)(2,1)S(1)}, u32[]{:S(2)}, u32[]{:S(2)}) collective-permute-start(bf16[32,640]{1,0:T(8,128)(2,1)S(1)} %get-tuple-element.52), channel_id=1, source_target_pairs={{0,4},{1,5},{2,6},{3,7},{4,0},{5,1},{6,2},{7,3},{8,12},{9,13},{10,... | collective-permute-start | bytes 122888 | tf_op jit(solution)/shard_map/ppermute | solution.py:393
  84.9 9.9 %collective-permute-start.32 = (bf16[32,640]{1,0:T(8,128)(2,1)S(1)}, bf16[32,640]{1,0:T(8,128)(2,1)S(1)}, u32[]{:S(2)}, u32[]{:S(2)}) collective-permute-start(bf16[32,640]{1,0:T(8,128)(2,1)S(1)} %get-tuple-element.53), channel_id=1, source_target_pairs={{0,6},{1,7},{2,4},{3,5},{4,2},{5,3},{6,0},{7,1},{8,14},{9,15},{10,... | collective-permute-start | bytes 122888 | tf_op jit(solution)/shard_map/ppermute | solution.py:393
  86.0 8.8 %collective-permute-start.24 = (bf16[32,1408]{1,0:T(8,128)(2,1)S(1)}, bf16[32,1408]{1,0:T(8,128)(2,1)S(1)}, u32[]{:S(2)}, u32[]{:S(2)}) collective-permute-start(bf16[32,1408]{1,0:T(8,128)(2,1)S(1)} %get-tuple-element.42), channel_id=1, source_target_pairs={{0,8},{8,0},{16,24},{24,16},{1,9},{9,1},{17,25},{25,17},{2,10},{10... | collective-permute-start | bytes 270344 | tf_op jit(solution)/shard_map/ppermute | solution.py:393
  89.3 8.4 %collective-permute-start.25 = (bf16[32,1408]{1,0:T(8,128)(2,1)S(1)}, bf16[32,1408]{1,0:T(8,128)(2,1)S(1)}, u32[]{:S(2)}, u32[]{:S(2)}) collective-permute-start(bf16[32,1408]{1,0:T(8,128)(2,1)S(1)} %get-tuple-element.43), channel_id=1, source_target_pairs={{0,16},{8,24},{16,0},{24,8},{1,17},{9,25},{17,1},{25,9},{2,18},{10... | collective-permute-start | bytes 270344 | tf_op jit(solution)/shard_map/ppermute | solution.py:393
  90.5 7.2 %collective-permute-start.26 = (bf16[32,1408]{1,0:T(8,128)(2,1)S(1)}, bf16[32,1408]{1,0:T(8,128)(2,1)S(1)}, u32[]{:S(2)}, u32[]{:S(2)}) collective-permute-start(bf16[32,1408]{1,0:T(8,128)(2,1)S(1)} %get-tuple-element.44), channel_id=1, source_target_pairs={{0,24},{8,16},{16,8},{24,0},{1,25},{9,17},{17,9},{25,1},{2,26},{10... | collective-permute-start | bytes 270344 | tf_op jit(solution)/shard_map/ppermute | solution.py:393
  (4 other events, 62.7 us)

commit v4 on v3

--- a/solution.py
+++ b/solution.py
@@ -10,13 +10,11 @@
 
 HEAD = 128
 FLOOR = -1e30
-SCALES = 4
 LOG2E = 1.4426950408889634
 
 
 HBM = pl.BlockSpec(memory_space=pltpu.HBM)
 VMEM = pl.BlockSpec(memory_space=pltpu.VMEM)
-SMEM = pl.BlockSpec(memory_space=pltpu.SMEM)
 
 
 def place():
@@ -85,7 +83,7 @@
     )(*near, *far)
 
 
-def attend(queries, ends, aways, both, width):
+def attend(queries, ends, both, width):
     row_count = queries[0].shape[0]
     total = both.shape[0]
     heads = width // HEAD
@@ -99,7 +97,6 @@
         both_ref = refs[2 * count]
         outs = refs[2 * count + 1 : 3 * count + 1]
         qbuf, obuf, sbuf, sums, tallies, tops = refs[3 * count + 1 :]
-        chip, core = place()
 
         def part(index, room, base, steps):
             shifts, factors = [], []
@@ -144,36 +141,30 @@
                     tally = tally + tallies[head] * factors[head]
                 sums[head], tallies[head], tops[head] = acc, tally, shifts[head]
 
-        starts, limits = [], []
-        for index, away in enumerate(aways):
+        for index in range(count):
             if count > 1:
                 qbuf[index] = q_in[index][...]
-            start = ((chip ^ away) * 2 + core) * row_count
-            limit = [ends_in[index][0]]
-            for _ in range(SCALES - 1):
-                limit.append(ends_in[index][jnp.minimum(limit[-1] - start, row_count - 1)])
-            starts.append(start)
-            limits.append(limit)
 
         def turn(index, carry):
-            def pick(values):
-                value = values[0]
-                for at in range(1, count):
-                    value = jnp.where(index == at, values[at], value)
-                return value
-
-            limit = [pick([one[at] for one in limits]) for at in range(SCALES)]
-            needed = (limit[-1] + step_k - 1) // step_k
-            token = pick(starts) + lax.broadcasted_iota(jnp.int32, (row_count, HEAD), 0)
-            bound = jnp.full((row_count, HEAD), limit[-1], jnp.int32)
-            for value in reversed(limit[:-1]):
-                bound = jnp.where(token < value, value, bound)
-            room = bound - lax.broadcasted_iota(jnp.int32, (row_count, HEAD), 1)
+            end = ends_in[0][...]
+            for at in range(1, count):
+                end = jnp.where(index == at, ends_in[at][...], end)
+            end = end.astype(jnp.float32)
+            reach = jnp.max(end)
+            bound = jnp.concatenate(
+                [
+                    jnp.broadcast_to(end[at : at + 1], (HEAD, HEAD)).T
+                    for at in range(row_count // HEAD)
+                ],
+                axis=0,
+            )
+            lane = lax.broadcasted_iota(jnp.int32, (row_count, HEAD), 1)
+            room = bound - lane.astype(jnp.float32)
             for test, base, steps in (
-                (needed == 1, 0, 1),
-                (needed >= 2, 0, 2),
-                (needed == 3, 2 * step_k, 1),
-                (needed == 4, 2 * step_k, 2),
+                (reach <= step_k, 0, 1),
+                (reach > step_k, 0, 2),
+                ((reach > 2 * step_k) & (reach <= 3 * step_k), 2 * step_k, 1),
+                (reach > 3 * step_k, 2 * step_k, 2),
             ):
 
                 @pl.when(test)
@@ -200,7 +191,7 @@
     return pl.pallas_call(
         kernel,
         out_shape=[jax.ShapeDtypeStruct((row_count, width), jnp.bfloat16)] * count,
-        in_specs=[SMEM] * count + [VMEM] * (count + 1),
+        in_specs=[VMEM] * (2 * count + 1),
         out_specs=[VMEM] * count,
         scratch_shapes=[
             pltpu.VMEM((count, row_count, width), jnp.bfloat16),
@@ -406,14 +397,16 @@
     rest = cut(sources, range(chips - 1), width)
     near = spread([*rest, *last])
     queries = spread(cut([query_rows[0]], range(chips), width))
-    ends = spread([scale_end] * chips)
+    ends = spread([scale_end.reshape(-1, HEAD)] * chips)
     far = [other_core(piece) for piece in near]
     grad_near = grad_out[0]
     grad_far = other_core(grad_near)
     both = assemble(near, far, chips)
     mine = [None] * chips
-    for aways in ([chips - 1], list(range(1, chips - 1)), [0]):
-        results = attend([queries[i] for i in aways], [ends[i] for i in aways], aways, both, width)
+    for aways in ([0], [chips - 1], list(range(1, chips - 1))):
+        results = attend(
+            [queries[i] for i in aways], [ends[i] for i in aways], both, width
+        )
         for away, piece in zip(aways, results):
             mine[away] = over("seq", seq, piece, 2 * away) if away else piece
     others = [other_core(piece) for piece in mine]

time: 98.7 us -> 97.7 us (0.990)
  Pallas kernels: 26.7 us -> 25.3 us
    pallas_call x3, Pallas kernels: 15.6 us -> 14.2 us  [attend(): pl.pallas_call(kernel, out_shape=[jax.ShapeDtypeStruct((row_count, width)...]
  transfers between devices with their start and end apart: 33 -> 33, of which waited for: 7 -> 7; matrix products, arithmetic and copies ran while one was open for 0% -> 0% of each run, Pallas kernels for 22% -> 20%
where the time goes in v4:
time: 97.7 us; the launch traced here: 97.6 us
  waiting for transfers between devices  37.2 us (38%)
  starting transfers between devices  34.3 us (35%)
  Pallas kernels  25.3 us (26%)
    ppermute x33, waiting for transfers between devices, over(): return lax.ppermute(value, axis, [(i, i ^ mask) for i in range(size)])  37.2 us
    ppermute x33, starting transfers between devices, over(): return lax.ppermute(value, axis, [(i, i ^ mask) for i in range(size)])  34.3 us
    pallas_call x3, Pallas kernels, attend(): pl.pallas_call(kernel, out_shape=[jax.ShapeDtypeStruct((row_count, width)...  14.2 us
    pallas_call x3, Pallas kernels, cut(): pl.pallas_call(kernel, out_shape=[shape] * len(aways), in_specs=[HBM] * c...  3.82 us
    pallas_call x2, Pallas kernels, weight_gradient(): pl.pallas_call(kernel, out_shape=shapes, in_specs=[VMEM] * (len(sources)...  3.09 us
    pallas_call x1, Pallas kernels, project(): pl.pallas_call(kernel, out_shape=jax.ShapeDtypeStruct((row_count, out_wid...  2.93 us
  transfers between devices with their start and end apart: 33, of which 7 were waited for; matrix products, arithmetic and copies ran while one was open for 0% of the time, Pallas kernels for 20%

profile of v4, /device:TPU:0, one launch (start us, length us, event | category | flops | bytes accessed | tf_op | source)
XLA Modules:
  0.0 97.6 jit_solution(3080961699033914767)
XLA Ops:
  0.6 1.5 %cut.4 = (bf16[384,512]{1,0:T(8,128)(2,1)S(1)}, bf16[384,512]{1,0:T(8,128)(2,1)S(1)}, bf16[384,512]{1,0:T(8,128)(2,1)S(1)}) custom-call(bf16[384,1024]{1,0:T(8,128)(2,1)} %bitcast.13, bf16[384,1024]{1,0:T(8,128)(2,1)} %bitcast.15), custom_call_target="tpu_custom_call" | custom-call | tf_op jit(solution)/shard_map/cut/pallas_call | solution.py:53
  2.2 3.0 %collective-permute-start = (bf16[384,512]{1,0:T(8,128)(2,1)S(1)}, bf16[384,512]{1,0:T(8,128)(2,1)S(1)}, u32[]{:S(2)}, u32[]{:S(2)}) collective-permute-start(bf16[384,512]{1,0:T(8,128)(2,1)S(1)} %get-tuple-element.30), channel_id=1, source_target_pairs={{0,2},{1,3},{2,0},{3,1},{4,6},{5,7},{6,4},{7,5},{8,10},{9,11},{10,... | collective-permute-start | bytes 1179656 | tf_op jit(solution)/shard_map/ppermute | solution.py:384
  5.2 1.5 %collective-permute-start.1 = (bf16[384,512]{1,0:T(8,128)(2,1)S(1)}, bf16[384,512]{1,0:T(8,128)(2,1)S(1)}, u32[]{:S(2)}, u32[]{:S(2)}) collective-permute-start(bf16[384,512]{1,0:T(8,128)(2,1)S(1)} %get-tuple-element.31), channel_id=1, source_target_pairs={{0,4},{1,5},{2,6},{3,7},{4,0},{5,1},{6,2},{7,3},{8,12},{9,13},{10,... | collective-permute-start | bytes 1179656 | tf_op jit(solution)/shard_map/ppermute | solution.py:384
  6.7 1.0 %cut.5 = bf16[384,512]{1,0:T(8,128)(2,1)S(1)} custom-call(bf16[384,1024]{1,0:T(8,128)(2,1)} %bitcast.14, bf16[384,1024]{1,0:T(8,128)(2,1)} %bitcast.16), custom_call_target="tpu_custom_call" | custom-call | tf_op jit(solution)/shard_map/cut/pallas_call | solution.py:53
  8.2 7.0 %collective-permute-done.refs_1_ = bf16[384,512]{1,0:T(8,128)(2,1)S(1)} collective-permute-done((bf16[384,512]{1,0:T(8,128)(2,1)S(1)}, bf16[384,512]{1,0:T(8,128)(2,1)S(1)}, u32[]{:S(2)}, u32[]{:S(2)}) %collective-permute-start) | collective-permute-done | bytes 393248 | tf_op jit(solution)/shard_map/ppermute | solution.py:384
  15.2 10.0 %collective-permute-done.1.refs_2_ = bf16[384,512]{1,0:T(8,128)(2,1)S(1)} collective-permute-done((bf16[384,512]{1,0:T(8,128)(2,1)S(1)}, bf16[384,512]{1,0:T(8,128)(2,1)S(1)}, u32[]{:S(2)}, u32[]{:S(2)}) %collective-permute-start.1) | collective-permute-done | bytes 393248 | tf_op jit(solution)/shard_map/ppermute | solution.py:384
  25.7 1.3 %cut.3 = (bf16[384,256]{1,0:T(8,128)(2,1)S(1)}, bf16[384,256]{1,0:T(8,128)(2,1)S(1)}, bf16[384,256]{1,0:T(8,128)(2,1)S(1)}, bf16[384,256]{1,0:T(8,128)(2,1)S(1)}) custom-call(bf16[384,1024]{1,0:T(8,128)(2,1)} %bitcast.18), custom_call_target="tpu_custom_call" | custom-call | tf_op jit(solution)/shard_map/cut/pallas_call | solution.py:53
  27.0 1.6 %collective-permute-start.10 = (bf16[384,256]{1,0:T(8,128)(2,1)S(1)}, bf16[384,256]{1,0:T(8,128)(2,1)S(1)}, u32[]{:S(2)}, u32[]{:S(2)}) collective-permute-start(bf16[384,256]{1,0:T(8,128)(2,1)S(1)} %get-tuple-element.33), channel_id=1, source_target_pairs={{0,4},{1,5},{2,6},{3,7},{4,0},{5,1},{6,2},{7,3},{8,12},{9,13},{10,... | collective-permute-start | bytes 589832 | tf_op jit(solution)/shard_map/ppermute | solution.py:384
  29.1 1.5 %collective-permute-start.7 = (s32[3,128]{1,0:T(4,128)S(1)}, s32[3,128]{1,0:T(4,128)S(1)}, u32[]{:S(2)}, u32[]{:S(2)}) collective-permute-start(s32[3,128]{1,0:T(4,128)S(1)} %bitcast.9), channel_id=1, source_target_pairs={{0,2},{1,3},{2,0},{3,1},{4,6},{5,7},{6,4},{7,5},{8,10},{9,11},{10,... | collective-permute-start | bytes 4616 | tf_op jit(solution)/shard_map/ppermute | solution.py:384
  31.3 3.8 %collective-permute-done.7.refs_0_ = s32[3,128]{1,0:T(4,128)S(1)} collective-permute-done((s32[3,128]{1,0:T(4,128)S(1)}, s32[3,128]{1,0:T(4,128)S(1)}, u32[]{:S(2)}, u32[]{:S(2)}) %collective-permute-start.7) | collective-permute-done | bytes 1568 | tf_op jit(solution)/shard_map/ppermute | solution.py:384
  35.5 2.6 %collective-permute-start.14 = (bf16[384,256]{1,0:T(8,128)(2,1)S(1)}, bf16[384,256]{1,0:T(8,128)(2,1)S(1)}, u32[]{:S(2)}, u32[]{:S(2)}) collective-permute-start(bf16[384,256]{1,0:T(8,128)(2,1)S(1)} %get-tuple-element.36), channel_id=1, source_target_pairs={{0,6},{1,7},{2,4},{3,5},{4,2},{5,3},{6,0},{7,1},{8,14},{9,15},{10,... | collective-permute-start | bytes 589832 | tf_op jit(solution)/shard_map/ppermute | solution.py:384
  38.1 7.8 %attend.4 = (bf16[384,256]{1,0:T(8,128)(2,1)S(1)}, bf16[384,256]{1,0:T(8,128)(2,1)S(1)}) custom-call(s32[3,128]{1,0:T(4,128)S(1)} %collective-permute-done.7.refs_0_, s32[3,128]{1,0:T(4,128)S(1)} %collective-permute-done.8.refs_1_, bf16[384,256]{1,0:T(8,128)(2,1)S(1)} %collective-permute-done.9.refs_2_, ...), custom_call_target="tpu_custom_call" | custom-call | flops 2415919104 | bytes 3145728 | tf_op jit(solution)/shard_map/attend/pallas_call | solution.py:191
  46.9 4.1 %attend.5 = bf16[384,256]{1,0:T(8,128)(2,1)S(1)} custom-call(s32[3,128]{1,0:T(4,128)S(1)} %collective-permute-done.13.refs_0_, bf16[384,256]{1,0:T(8,128)(2,1)S(1)} %collective-permute-done.14.refs_1_, bf16[3072,512]{1,0:T(8,128)(2,1)S(1)} %assemble.1.refs_2_.refs_4_), custom_call_target="tpu_custom_call" | custom-call | flops 1207959552 | bytes 3145728 | tf_op jit(solution)/shard_map/attend/pallas_call | solution.py:191
  51.8 2.2 %attend.3.refs_0_ = bf16[384,256]{1,0:T(8,128)(2,1)S(1)} custom-call(s32[3,128]{1,0:T(4,128)S(1)} %bitcast.12, bf16[384,256]{1,0:T(8,128)(2,1)S(1)} %get-tuple-element.28.refs_1_, bf16[3072,512]{1,0:T(8,128)(2,1)S(1)} %assemble.1.refs_2_.refs_4_), custom_call_target="tpu_custom_call" | custom-call | flops 1207959552 | bytes 3145728 | tf_op jit(solution)/shard_map/attend/pallas_call | solution.py:191
  54.7 2.9 %collective-permute-done.15.refs_3_ = bf16[384,256]{1,0:T(8,128)(2,1)S(1)} collective-permute-done((bf16[384,256]{1,0:T(8,128)(2,1)S(1)}, bf16[384,256]{1,0:T(8,128)(2,1)S(1)}, u32[]{:S(2)}, u32[]{:S(2)}) %collective-permute-start.15) | collective-permute-done | bytes 196640 | tf_op jit(solution)/shard_map/ppermute | solution.py:384
  57.6 1.4 %collective-permute-done.19.refs_7_ = bf16[384,256]{1,0:T(8,128)(2,1)S(1)} collective-permute-done((bf16[384,256]{1,0:T(8,128)(2,1)S(1)}, bf16[384,256]{1,0:T(8,128)(2,1)S(1)}, u32[]{:S(2)}, u32[]{:S(2)}) %collective-permute-start.19) | collective-permute-done | bytes 196640 | tf_op jit(solution)/shard_map/ppermute | solution.py:384
  59.1 2.2 %weight_gradient.2 = (f32[128,1408]{1,0:T(8,128)S(1)}, bf16[128,1408]{1,0:T(8,128)(2,1)S(1)}, bf16[128,1408]{1,0:T(8,128)(2,1)S(1)}, bf16[128,1408]{1,0:T(8,128)(2,1)S(1)}, bf16[1024,768]{1,0:T(8,128)(2,1)S(1)}) custom-call(bf16[384,256]{1,0:T(8,128)(2,1)S(1)} %attend.3.refs_0_, bf16[384,256]{1,0:T(8,128)(2,1)S(1)} %collective-permute-done.11.refs_1_, ...), custom_call_target="tpu_custom_call" | custom-call | flops 1107296256 | bytes 2162688 | tf_op jit(solution)/shard_map/weight_gradient/pallas_call | solution.py:274
  62.2 1.8 %collective-permute-start.27 = (bf16[128,640]{1,0:T(8,128)(2,1)S(1)}, bf16[128,640]{1,0:T(8,128)(2,1)S(1)}, u32[]{:S(2)}, u32[]{:S(2)}) collective-permute-start(bf16[128,640]{1,0:T(8,128)(2,1)S(1)} %get-tuple-element.47), channel_id=1, source_target_pairs={{0,8},{8,0},{16,24},{24,16},{1,9},{9,1},{17,25},{25,17},{2,10},{10... | collective-permute-start | bytes 491528 | tf_op jit(solution)/shard_map/ppermute | solution.py:384
  64.0 1.0 %collective-permute-start.21 = (bf16[128,1408]{1,0:T(8,128)(2,1)S(1)}, bf16[128,1408]{1,0:T(8,128)(2,1)S(1)}, u32[]{:S(2)}, u32[]{:S(2)}) collective-permute-start(bf16[128,1408]{1,0:T(8,128)(2,1)S(1)} %get-tuple-element.38), channel_id=1, source_target_pairs={{0,2},{1,3},{2,0},{3,1},{4,6},{5,7},{6,4},{7,5},{8,10},{9,11},{10,... | collective-permute-start | bytes 1081352 | tf_op jit(solution)/shard_map/ppermute | solution.py:384
  65.0 0.9 collective-permute-start.22
  65.9 1.6 %collective-permute-start.23 = (bf16[128,1408]{1,0:T(8,128)(2,1)S(1)}, bf16[128,1408]{1,0:T(8,128)(2,1)S(1)}, u32[]{:S(2)}, u32[]{:S(2)}) collective-permute-start(bf16[128,1408]{1,0:T(8,128)(2,1)S(1)} %get-tuple-element.40), channel_id=1, source_target_pairs={{0,6},{1,7},{2,4},{3,5},{4,2},{5,3},{6,0},{7,1},{8,14},{9,15},{10,... | collective-permute-start | bytes 1081352 | tf_op jit(solution)/shard_map/ppermute | solution.py:384
  67.5 2.6 %collective-permute-start.28 = (bf16[128,640]{1,0:T(8,128)(2,1)S(1)}, bf16[128,640]{1,0:T(8,128)(2,1)S(1)}, u32[]{:S(2)}, u32[]{:S(2)}) collective-permute-start(bf16[128,640]{1,0:T(8,128)(2,1)S(1)} %get-tuple-element.48), channel_id=1, source_target_pairs={{0,16},{8,24},{16,0},{24,8},{1,17},{9,25},{17,1},{25,9},{2,18},{10... | collective-permute-start | bytes 491528 | tf_op jit(solution)/shard_map/ppermute | solution.py:384
  70.0 2.2 %collective-permute-start.29 = (bf16[128,640]{1,0:T(8,128)(2,1)S(1)}, bf16[128,640]{1,0:T(8,128)(2,1)S(1)}, u32[]{:S(2)}, u32[]{:S(2)}) collective-permute-start(bf16[128,640]{1,0:T(8,128)(2,1)S(1)} %get-tuple-element.49), channel_id=1, source_target_pairs={{0,24},{8,16},{16,8},{24,0},{1,25},{9,17},{17,9},{25,1},{2,26},{10... | collective-permute-start | bytes 491528 | tf_op jit(solution)/shard_map/ppermute | solution.py:384
  72.2 9.1 %collective-permute-done.28.refs_2_ = bf16[128,640]{1,0:T(8,128)(2,1)S(1)} collective-permute-done((bf16[128,640]{1,0:T(8,128)(2,1)S(1)}, bf16[128,640]{1,0:T(8,128)(2,1)S(1)}, u32[]{:S(2)}, u32[]{:S(2)}) %collective-permute-start.28) | collective-permute-done | bytes 163872 | tf_op jit(solution)/shard_map/ppermute | solution.py:384
  81.4 1.1 %collective-permute-start.30 = (bf16[32,640]{1,0:T(8,128)(2,1)S(1)}, bf16[32,640]{1,0:T(8,128)(2,1)S(1)}, u32[]{:S(2)}, u32[]{:S(2)}) collective-permute-start(bf16[32,640]{1,0:T(8,128)(2,1)S(1)} %get-tuple-element.51), channel_id=1, source_target_pairs={{0,2},{1,3},{2,0},{3,1},{4,6},{5,7},{6,4},{7,5},{8,10},{9,11},{10,... | collective-permute-start | bytes 122888 | tf_op jit(solution)/shard_map/ppermute | solution.py:384
  82.5 1.0 collective-permute-start.31
  83.5 1.5 %collective-permute-start.32 = (bf16[32,640]{1,0:T(8,128)(2,1)S(1)}, bf16[32,640]{1,0:T(8,128)(2,1)S(1)}, u32[]{:S(2)}, u32[]{:S(2)}) collective-permute-start(bf16[32,640]{1,0:T(8,128)(2,1)S(1)} %get-tuple-element.53), channel_id=1, source_target_pairs={{0,6},{1,7},{2,4},{3,5},{4,2},{5,3},{6,0},{7,1},{8,14},{9,15},{10,... | collective-permute-start | bytes 122888 | tf_op jit(solution)/shard_map/ppermute | solution.py:384
  85.1 3.3 %collective-permute-start.24 = (bf16[32,1408]{1,0:T(8,128)(2,1)S(1)}, bf16[32,1408]{1,0:T(8,128)(2,1)S(1)}, u32[]{:S(2)}, u32[]{:S(2)}) collective-permute-start(bf16[32,1408]{1,0:T(8,128)(2,1)S(1)} %get-tuple-element.42), channel_id=1, source_target_pairs={{0,8},{8,0},{16,24},{24,16},{1,9},{9,1},{17,25},{25,17},{2,10},{10... | collective-permute-start | bytes 270344 | tf_op jit(solution)/shard_map/ppermute | solution.py:384
  88.4 1.2 %collective-permute-start.25 = (bf16[32,1408]{1,0:T(8,128)(2,1)S(1)}, bf16[32,1408]{1,0:T(8,128)(2,1)S(1)}, u32[]{:S(2)}, u32[]{:S(2)}) collective-permute-start(bf16[32,1408]{1,0:T(8,128)(2,1)S(1)} %get-tuple-element.43), channel_id=1, source_target_pairs={{0,16},{8,24},{16,0},{24,8},{1,17},{9,25},{17,1},{25,9},{2,18},{10... | collective-permute-start | bytes 270344 | tf_op jit(solution)/shard_map/ppermute | solution.py:384
  89.6 1.4 %collective-permute-start.26 = (bf16[32,1408]{1,0:T(8,128)(2,1)S(1)}, bf16[32,1408]{1,0:T(8,128)(2,1)S(1)}, u32[]{:S(2)}, u32[]{:S(2)}) collective-permute-start(bf16[32,1408]{1,0:T(8,128)(2,1)S(1)} %get-tuple-element.44), channel_id=1, source_target_pairs={{0,24},{8,16},{16,8},{24,0},{1,25},{9,17},{17,9},{25,1},{2,26},{10... | collective-permute-start | bytes 270344 | tf_op jit(solution)/shard_map/ppermute | solution.py:384
  91.0 2.9 %project.1 = bf16[384,2048]{1,0:T(8,128)(2,1)} custom-call(bf16[384,256]{1,0:T(8,128)(2,1)S(1)} %attend.3.refs_0_, bf16[384,256]{1,0:T(8,128)(2,1)S(1)} %collective-permute-done.11.refs_1_, bf16[384,256]{1,0:T(8,128)(2,1)S(1)} %collective-permute-done.12.refs_2_, bf16[384,256]{1,0:T(8,128)(2,1)S(1)} %collective-permute-done.15.refs_3_, ...), custom_call_target="tpu_custom_call" | custom-call | flops 1610612736 | bytes 4194304 | tf_op jit(solution)/shard_map/project/pallas_call | solution.py:310
  93.9 2.9 %collective-permute-done.25.refs_2_ = bf16[32,1408]{1,0:T(8,128)(2,1)S(1)} collective-permute-done((bf16[32,1408]{1,0:T(8,128)(2,1)S(1)}, bf16[32,1408]{1,0:T(8,128)(2,1)S(1)}, u32[]{:S(2)}, u32[]{:S(2)}) %collective-permute-start.25) | collective-permute-done | bytes 90144 | tf_op jit(solution)/shard_map/ppermute | solution.py:384
  (53 shorter events, 6.9 us)
Async XLA Ops:
  2.2 13.0 %collective-permute-start = (bf16[384,512]{1,0:T(8,128)(2,1)S(1)}, bf16[384,512]{1,0:T(8,128)(2,1)S(1)}, u32[]{:S(2)}, u32[]{:S(2)}) collective-permute-start(bf16[384,512]{1,0:T(8,128)(2,1)S(1)} %get-tuple-element.30), channel_id=1, source_target_pairs={{0,2},{1,3},{2,0},{3,1},{4,6},{5,7},{6,4},{7,5},{8,10},{9,11},{10,... | collective-permute-start | bytes 1179656 | tf_op jit(solution)/shard_map/ppermute | solution.py:384
  5.2 53.8 %collective-permute-start.20 = (bf16[384,2048]{1,0:T(8,128)(2,1)S(1)}, bf16[384,2048]{1,0:T(8,128)(2,1)S(1)}, u32[]{:S(2)}, u32[]{:S(2)}) collective-permute-start(bf16[384,2048]{1,0:T(8,128)(2,1)S(1)} %bitcast.6), channel_id=1, source_target_pairs={{0,1},{1,0},{2,3},{3,2},{4,5},{5,4},{6,7},{7,6},{8,9},{9,8},{10,11... | collective-permute-start | bytes 4718600 | tf_op jit(solution)/shard_map/ppermute | solution.py:384
  5.2 20.0 %collective-permute-start.1 = (bf16[384,512]{1,0:T(8,128)(2,1)S(1)}, bf16[384,512]{1,0:T(8,128)(2,1)S(1)}, u32[]{:S(2)}, u32[]{:S(2)}) collective-permute-start(bf16[384,512]{1,0:T(8,128)(2,1)S(1)} %get-tuple-element.31), channel_id=1, source_target_pairs={{0,4},{1,5},{2,6},{3,7},{4,0},{5,1},{6,2},{7,3},{8,12},{9,13},{10,... | collective-permute-start | bytes 1179656 | tf_op jit(solution)/shard_map/ppermute | solution.py:384
  7.8 17.4 %collective-permute-start.2 = (bf16[384,512]{1,0:T(8,128)(2,1)S(1)}, bf16[384,512]{1,0:T(8,128)(2,1)S(1)}, u32[]{:S(2)}, u32[]{:S(2)}) collective-permute-start(bf16[384,512]{1,0:T(8,128)(2,1)S(1)} %cut.5), channel_id=1, source_target_pairs={{0,6},{1,7},{2,4},{3,5},{4,2},{5,3},{6,0},{7,1},{8,14},{9,15},{10,... | collective-permute-start | bytes 1179656 | tf_op jit(solution)/shard_map/ppermute | solution.py:384
  8.1 18.9 %collective-permute-start.3 = (bf16[384,512]{1,0:T(8,128)(2,1)S(1)}, bf16[384,512]{1,0:T(8,128)(2,1)S(1)}, u32[]{:S(2)}, u32[]{:S(2)}) collective-permute-start(bf16[384,512]{1,0:T(8,128)(2,1)S(1)} %get-tuple-element.29.refs_0_), channel_id=1, source_target_pairs={{0,1},{1,0},{2,3},{3,2},{4,5},{5,4},{6,7},{7,6},{8,9},{9,8},{10,11... | collective-permute-start | bytes 1179656 | tf_op jit(solution)/shard_map/ppermute | solution.py:384
  15.2 13.4 %collective-permute-start.4 = (bf16[384,512]{1,0:T(8,128)(2,1)S(1)}, bf16[384,512]{1,0:T(8,128)(2,1)S(1)}, u32[]{:S(2)}, u32[]{:S(2)}) collective-permute-start(bf16[384,512]{1,0:T(8,128)(2,1)S(1)} %collective-permute-done.refs_1_), channel_id=1, source_target_pairs={{0,1},{1,0},{2,3},{3,2},{4,5},{5,4},{6,7},{7,6},{8,9},{9,8},{10,11... | collective-permute-start | bytes 1179656 | tf_op jit(solution)/shard_map/ppermute | solution.py:384
  25.2 3.9 %collective-permute-start.5 = (bf16[384,512]{1,0:T(8,128)(2,1)S(1)}, bf16[384,512]{1,0:T(8,128)(2,1)S(1)}, u32[]{:S(2)}, u32[]{:S(2)}) collective-permute-start(bf16[384,512]{1,0:T(8,128)(2,1)S(1)} %collective-permute-done.1.refs_2_), channel_id=1, source_target_pairs={{0,1},{1,0},{2,3},{3,2},{4,5},{5,4},{6,7},{7,6},{8,9},{9,8},{10,11... | collective-permute-start | bytes 1179656 | tf_op jit(solution)/shard_map/ppermute | solution.py:384
  25.2 5.4 %collective-permute-start.6 = (bf16[384,512]{1,0:T(8,128)(2,1)S(1)}, bf16[384,512]{1,0:T(8,128)(2,1)S(1)}, u32[]{:S(2)}, u32[]{:S(2)}) collective-permute-start(bf16[384,512]{1,0:T(8,128)(2,1)S(1)} %collective-permute-done.2.refs_3_), channel_id=1, source_target_pairs={{0,1},{1,0},{2,3},{3,2},{4,5},{5,4},{6,7},{7,6},{8,9},{9,8},{10,11... | collective-permute-start | bytes 1179656 | tf_op jit(solution)/shard_map/ppermute | solution.py:384
  27.0 11.1 %collective-permute-start.10 = (bf16[384,256]{1,0:T(8,128)(2,1)S(1)}, bf16[384,256]{1,0:T(8,128)(2,1)S(1)}, u32[]{:S(2)}, u32[]{:S(2)}) collective-permute-start(bf16[384,256]{1,0:T(8,128)(2,1)S(1)} %get-tuple-element.33), channel_id=1, source_target_pairs={{0,4},{1,5},{2,6},{3,7},{4,0},{5,1},{6,2},{7,3},{8,12},{9,13},{10,... | collective-permute-start | bytes 589832 | tf_op jit(solution)/shard_map/ppermute | solution.py:384
  28.6 9.5 %collective-permute-start.9 = (bf16[384,256]{1,0:T(8,128)(2,1)S(1)}, bf16[384,256]{1,0:T(8,128)(2,1)S(1)}, u32[]{:S(2)}, u32[]{:S(2)}) collective-permute-start(bf16[384,256]{1,0:T(8,128)(2,1)S(1)} %get-tuple-element.32), channel_id=1, source_target_pairs={{0,2},{1,3},{2,0},{3,1},{4,6},{5,7},{6,4},{7,5},{8,10},{9,11},{10,... | collective-permute-start | bytes 589832 | tf_op jit(solution)/shard_map/ppermute | solution.py:384
  29.1 6.0 %collective-permute-start.7 = (s32[3,128]{1,0:T(4,128)S(1)}, s32[3,128]{1,0:T(4,128)S(1)}, u32[]{:S(2)}, u32[]{:S(2)}) collective-permute-start(s32[3,128]{1,0:T(4,128)S(1)} %bitcast.9), channel_id=1, source_target_pairs={{0,2},{1,3},{2,0},{3,1},{4,6},{5,7},{6,4},{7,5},{8,10},{9,11},{10,... | collective-permute-start | bytes 4616 | tf_op jit(solution)/shard_map/ppermute | solution.py:384
  30.6 4.9 %collective-permute-start.8 = (s32[3,128]{1,0:T(4,128)S(1)}, s32[3,128]{1,0:T(4,128)S(1)}, u32[]{:S(2)}, u32[]{:S(2)}) collective-permute-start(s32[3,128]{1,0:T(4,128)S(1)} %bitcast.10), channel_id=1, source_target_pairs={{0,4},{1,5},{2,6},{3,7},{4,0},{5,1},{6,2},{7,3},{8,12},{9,13},{10,... | collective-permute-start | bytes 4616 | tf_op jit(solution)/shard_map/ppermute | solution.py:384
  35.1 11.8 %collective-permute-start.13 = (s32[3,128]{1,0:T(4,128)S(1)}, s32[3,128]{1,0:T(4,128)S(1)}, u32[]{:S(2)}, u32[]{:S(2)}) collective-permute-start(s32[3,128]{1,0:T(4,128)S(1)} %bitcast.11), channel_id=1, source_target_pairs={{0,6},{1,7},{2,4},{3,5},{4,2},{5,3},{6,0},{7,1},{8,14},{9,15},{10,... | collective-permute-start | bytes 4616 | tf_op jit(solution)/shard_map/ppermute | solution.py:384
  35.5 11.4 %collective-permute-start.14 = (bf16[384,256]{1,0:T(8,128)(2,1)S(1)}, bf16[384,256]{1,0:T(8,128)(2,1)S(1)}, u32[]{:S(2)}, u32[]{:S(2)}) collective-permute-start(bf16[384,256]{1,0:T(8,128)(2,1)S(1)} %get-tuple-element.36), channel_id=1, source_target_pairs={{0,6},{1,7},{2,4},{3,5},{4,2},{5,3},{6,0},{7,1},{8,14},{9,15},{10,... | collective-permute-start | bytes 589832 | tf_op jit(solution)/shard_map/ppermute | solution.py:384
  45.9 8.2 %collective-permute-start.11 = (bf16[384,256]{1,0:T(8,128)(2,1)S(1)}, bf16[384,256]{1,0:T(8,128)(2,1)S(1)}, u32[]{:S(2)}, u32[]{:S(2)}) collective-permute-start(bf16[384,256]{1,0:T(8,128)(2,1)S(1)} %get-tuple-element.34), channel_id=1, source_target_pairs={{0,2},{1,3},{2,0},{3,1},{4,6},{5,7},{6,4},{7,5},{8,10},{9,11},{10,... | collective-permute-start | bytes 589832 | tf_op jit(solution)/shard_map/ppermute | solution.py:384
  46.0 8.6 %collective-permute-start.12 = (bf16[384,256]{1,0:T(8,128)(2,1)S(1)}, bf16[384,256]{1,0:T(8,128)(2,1)S(1)}, u32[]{:S(2)}, u32[]{:S(2)}) collective-permute-start(bf16[384,256]{1,0:T(8,128)(2,1)S(1)} %get-tuple-element.35), channel_id=1, source_target_pairs={{0,4},{1,5},{2,6},{3,7},{4,0},{5,1},{6,2},{7,3},{8,12},{9,13},{10,... | collective-permute-start | bytes 589832 | tf_op jit(solution)/shard_map/ppermute | solution.py:384
  51.0 6.6 %collective-permute-start.15 = (bf16[384,256]{1,0:T(8,128)(2,1)S(1)}, bf16[384,256]{1,0:T(8,128)(2,1)S(1)}, u32[]{:S(2)}, u32[]{:S(2)}) collective-permute-start(bf16[384,256]{1,0:T(8,128)(2,1)S(1)} %attend.5), channel_id=1, source_target_pairs={{0,6},{1,7},{2,4},{3,5},{4,2},{5,3},{6,0},{7,1},{8,14},{9,15},{10,... | collective-permute-start | bytes 589832 | tf_op jit(solution)/shard_map/ppermute | solution.py:384
  54.0 3.6 %collective-permute-start.16 = (bf16[384,256]{1,0:T(8,128)(2,1)S(1)}, bf16[384,256]{1,0:T(8,128)(2,1)S(1)}, u32[]{:S(2)}, u32[]{:S(2)}) collective-permute-start(bf16[384,256]{1,0:T(8,128)(2,1)S(1)} %attend.3.refs_0_), channel_id=1, source_target_pairs={{0,1},{1,0},{2,3},{3,2},{4,5},{5,4},{6,7},{7,6},{8,9},{9,8},{10,11... | collective-permute-start | bytes 589832 | tf_op jit(solution)/shard_map/ppermute | solution.py:384
  54.1 3.5 %collective-permute-start.17 = (bf16[384,256]{1,0:T(8,128)(2,1)S(1)}, bf16[384,256]{1,0:T(8,128)(2,1)S(1)}, u32[]{:S(2)}, u32[]{:S(2)}) collective-permute-start(bf16[384,256]{1,0:T(8,128)(2,1)S(1)} %collective-permute-done.11.refs_1_), channel_id=1, source_target_pairs={{0,1},{1,0},{2,3},{3,2},{4,5},{5,4},{6,7},{7,6},{8,9},{9,8},{10,11... | collective-permute-start | bytes 589832 | tf_op jit(solution)/shard_map/ppermute | solution.py:384
  54.6 3.0 %collective-permute-start.18 = (bf16[384,256]{1,0:T(8,128)(2,1)S(1)}, bf16[384,256]{1,0:T(8,128)(2,1)S(1)}, u32[]{:S(2)}, u32[]{:S(2)}) collective-permute-start(bf16[384,256]{1,0:T(8,128)(2,1)S(1)} %collective-permute-done.12.refs_2_), channel_id=1, source_target_pairs={{0,1},{1,0},{2,3},{3,2},{4,5},{5,4},{6,7},{7,6},{8,9},{9,8},{10,11... | collective-permute-start | bytes 589832 | tf_op jit(solution)/shard_map/ppermute | solution.py:384
  62.2 7.9 %collective-permute-start.27 = (bf16[128,640]{1,0:T(8,128)(2,1)S(1)}, bf16[128,640]{1,0:T(8,128)(2,1)S(1)}, u32[]{:S(2)}, u32[]{:S(2)}) collective-permute-start(bf16[128,640]{1,0:T(8,128)(2,1)S(1)} %get-tuple-element.47), channel_id=1, source_target_pairs={{0,8},{8,0},{16,24},{24,16},{1,9},{9,1},{17,25},{25,17},{2,10},{10... | collective-permute-start | bytes 491528 | tf_op jit(solution)/shard_map/ppermute | solution.py:384
  64.0 19.5 %collective-permute-start.21 = (bf16[128,1408]{1,0:T(8,128)(2,1)S(1)}, bf16[128,1408]{1,0:T(8,128)(2,1)S(1)}, u32[]{:S(2)}, u32[]{:S(2)}) collective-permute-start(bf16[128,1408]{1,0:T(8,128)(2,1)S(1)} %get-tuple-element.38), channel_id=1, source_target_pairs={{0,2},{1,3},{2,0},{3,1},{4,6},{5,7},{6,4},{7,5},{8,10},{9,11},{10,... | collective-permute-start | bytes 1081352 | tf_op jit(solution)/shard_map/ppermute | solution.py:384
  65.0 20.0 %collective-permute-start.22 = (bf16[128,1408]{1,0:T(8,128)(2,1)S(1)}, bf16[128,1408]{1,0:T(8,128)(2,1)S(1)}, u32[]{:S(2)}, u32[]{:S(2)}) collective-permute-start(bf16[128,1408]{1,0:T(8,128)(2,1)S(1)} %get-tuple-element.39), channel_id=1, source_target_pairs={{0,4},{1,5},{2,6},{3,7},{4,0},{5,1},{6,2},{7,3},{8,12},{9,13},{10,... | collective-permute-start | bytes 1081352 | tf_op jit(solution)/shard_map/ppermute | solution.py:384
  65.9 19.1 %collective-permute-start.23 = (bf16[128,1408]{1,0:T(8,128)(2,1)S(1)}, bf16[128,1408]{1,0:T(8,128)(2,1)S(1)}, u32[]{:S(2)}, u32[]{:S(2)}) collective-permute-start(bf16[128,1408]{1,0:T(8,128)(2,1)S(1)} %get-tuple-element.40), channel_id=1, source_target_pairs={{0,6},{1,7},{2,4},{3,5},{4,2},{5,3},{6,0},{7,1},{8,14},{9,15},{10,... | collective-permute-start | bytes 1081352 | tf_op jit(solution)/shard_map/ppermute | solution.py:384
  67.5 13.9 %collective-permute-start.28 = (bf16[128,640]{1,0:T(8,128)(2,1)S(1)}, bf16[128,640]{1,0:T(8,128)(2,1)S(1)}, u32[]{:S(2)}, u32[]{:S(2)}) collective-permute-start(bf16[128,640]{1,0:T(8,128)(2,1)S(1)} %get-tuple-element.48), channel_id=1, source_target_pairs={{0,16},{8,24},{16,0},{24,8},{1,17},{9,25},{17,1},{25,9},{2,18},{10... | collective-permute-start | bytes 491528 | tf_op jit(solution)/shard_map/ppermute | solution.py:384
  70.0 11.3 %collective-permute-start.29 = (bf16[128,640]{1,0:T(8,128)(2,1)S(1)}, bf16[128,640]{1,0:T(8,128)(2,1)S(1)}, u32[]{:S(2)}, u32[]{:S(2)}) collective-permute-start(bf16[128,640]{1,0:T(8,128)(2,1)S(1)} %get-tuple-element.49), channel_id=1, source_target_pairs={{0,24},{8,16},{16,8},{24,0},{1,25},{9,17},{17,9},{25,1},{2,26},{10... | collective-permute-start | bytes 491528 | tf_op jit(solution)/shard_map/ppermute | solution.py:384
  81.4 8.2 %collective-permute-start.30 = (bf16[32,640]{1,0:T(8,128)(2,1)S(1)}, bf16[32,640]{1,0:T(8,128)(2,1)S(1)}, u32[]{:S(2)}, u32[]{:S(2)}) collective-permute-start(bf16[32,640]{1,0:T(8,128)(2,1)S(1)} %get-tuple-element.51), channel_id=1, source_target_pairs={{0,2},{1,3},{2,0},{3,1},{4,6},{5,7},{6,4},{7,5},{8,10},{9,11},{10,... | collective-permute-start | bytes 122888 | tf_op jit(solution)/shard_map/ppermute | solution.py:384
  82.5 11.4 %collective-permute-start.31 = (bf16[32,640]{1,0:T(8,128)(2,1)S(1)}, bf16[32,640]{1,0:T(8,128)(2,1)S(1)}, u32[]{:S(2)}, u32[]{:S(2)}) collective-permute-start(bf16[32,640]{1,0:T(8,128)(2,1)S(1)} %get-tuple-element.52), channel_id=1, source_target_pairs={{0,4},{1,5},{2,6},{3,7},{4,0},{5,1},{6,2},{7,3},{8,12},{9,13},{10,... | collective-permute-start | bytes 122888 | tf_op jit(solution)/shard_map/ppermute | solution.py:384
  83.5 10.4 %collective-permute-start.32 = (bf16[32,640]{1,0:T(8,128)(2,1)S(1)}, bf16[32,640]{1,0:T(8,128)(2,1)S(1)}, u32[]{:S(2)}, u32[]{:S(2)}) collective-permute-start(bf16[32,640]{1,0:T(8,128)(2,1)S(1)} %get-tuple-element.53), channel_id=1, source_target_pairs={{0,6},{1,7},{2,4},{3,5},{4,2},{5,3},{6,0},{7,1},{8,14},{9,15},{10,... | collective-permute-start | bytes 122888 | tf_op jit(solution)/shard_map/ppermute | solution.py:384
  85.1 8.8 %collective-permute-start.24 = (bf16[32,1408]{1,0:T(8,128)(2,1)S(1)}, bf16[32,1408]{1,0:T(8,128)(2,1)S(1)}, u32[]{:S(2)}, u32[]{:S(2)}) collective-permute-start(bf16[32,1408]{1,0:T(8,128)(2,1)S(1)} %get-tuple-element.42), channel_id=1, source_target_pairs={{0,8},{8,0},{16,24},{24,16},{1,9},{9,1},{17,25},{25,17},{2,10},{10... | collective-permute-start | bytes 270344 | tf_op jit(solution)/shard_map/ppermute | solution.py:384
  88.4 8.4 %collective-permute-start.25 = (bf16[32,1408]{1,0:T(8,128)(2,1)S(1)}, bf16[32,1408]{1,0:T(8,128)(2,1)S(1)}, u32[]{:S(2)}, u32[]{:S(2)}) collective-permute-start(bf16[32,1408]{1,0:T(8,128)(2,1)S(1)} %get-tuple-element.43), channel_id=1, source_target_pairs={{0,16},{8,24},{16,0},{24,8},{1,17},{9,25},{17,1},{25,9},{2,18},{10... | collective-permute-start | bytes 270344 | tf_op jit(solution)/shard_map/ppermute | solution.py:384
  89.6 7.2 %collective-permute-start.26 = (bf16[32,1408]{1,0:T(8,128)(2,1)S(1)}, bf16[32,1408]{1,0:T(8,128)(2,1)S(1)}, u32[]{:S(2)}, u32[]{:S(2)}) collective-permute-start(bf16[32,1408]{1,0:T(8,128)(2,1)S(1)} %get-tuple-element.44), channel_id=1, source_target_pairs={{0,24},{8,16},{16,8},{24,0},{1,25},{9,17},{17,9},{25,1},{2,26},{10... | collective-permute-start | bytes 270344 | tf_op jit(solution)/shard_map/ppermute | solution.py:384
  (4 other events, 62.7 us)

commit v5 on v4

--- a/solution.py
+++ b/solution.py
@@ -211,40 +211,49 @@
     )(*ends, *queries, both)
 
 
-def turn_over(near, far, chips, width):
-    row_count = near[0].shape[0]
-
-    def kernel(*refs):
-        pieces, out = (refs[:chips], refs[chips : 2 * chips]), refs[2 * chips]
+def turning(pieces, chips, width):
+    row_count = pieces[0].shape[0]
+
+    def kernel(*refs):
+        ins, out = refs[:chips], refs[chips]
         chip, _ = place()
-        for side in range(2):
-            for away in range(chips):
-                start = pl.multiple_of((chip ^ away) * width, width)
-                out[pl.ds(start, width), side * row_count : (side + 1) * row_count] = (
-                    pieces[side][away][...].T
-                )
-
-    return kernel, jax.ShapeDtypeStruct((chips * width, 2 * row_count), near[0].dtype)
-
-
-def weight_gradient(turned, grad_near, grad_far, columns, axis, chips, planes, pieces=None):
+        for away in range(chips):
+            start = pl.multiple_of((chip ^ away) * width, width)
+            out[pl.ds(start, width), :] = ins[away][...].T
+
+    return kernel, jax.ShapeDtypeStruct((chips * width, row_count), pieces[0].dtype)
+
+
+def turn_over(pieces, chips, width):
+    kernel, shape = turning(pieces, chips, width)
+    return pl.pallas_call(
+        kernel,
+        out_shape=shape,
+        in_specs=[VMEM] * chips,
+        out_specs=VMEM,
+        compiler_params=params(16),
+        name="turn_over",
+    )(*pieces)
+
+
+def weight_gradient(near, far, grad_near, grad_far, columns, axis, chips, planes, pieces=None):
     row_count = grad_near.shape[0]
     if pieces is None:
-        turn, shape, sources = None, turned.shape, [turned]
+        turn, sources = None, [near, far]
     else:
-        turn, target = turn_over(*pieces)
-        shape, sources = target.shape, [*pieces[0], *pieces[1]]
-    group = shape[0] // (planes * chips * 2)
+        turn, target = turning(*pieces)
+        sources = [near, *pieces[0]]
+    group = near.shape[0] // (planes * chips * 2)
     size = planes if axis == "dp" else chips
     other = chips if axis == "dp" else planes
 
     def kernel(*refs):
         ins, rest = refs[: len(sources)], refs[len(sources) :]
         grads, outs, left = rest[:2], rest[2 : 2 + size], rest[-1]
-        flat = ins[0]
+        flat = ins[:2]
         if turn is not None:
-            flat = rest[2 + size]
-            turn(*ins, flat)
+            flat = (ins[0], rest[2 + size])
+            turn(*ins[1:], flat[1])
         chip, core = place()
         plane = lax.axis_index("dp")
         for away in range(size):
@@ -252,7 +261,10 @@
                 start = (plane ^ away) * chips + at if axis == "dp" else at * chips + (chip ^ away)
                 rows = pl.ds(pl.multiple_of((start * 2 + core) * group, group), group)
                 target = (away * other + at) * group
-                left[target : target + group, :] = flat[rows, :]
+                for side in range(2):
+                    left[
+                        target : target + group, side * row_count : (side + 1) * row_count
+                    ] = flat[side][rows, :]
         for first in range(columns.start, columns.stop, 512):
             part = slice(first, min(first + 512, columns.stop))
             value = jnp.dot(
@@ -279,7 +291,7 @@
         scratch_shapes=[pltpu.VMEM((size * other * group, 2 * row_count), jnp.bfloat16)],
         compiler_params=params(32),
         cost_estimate=pl.CostEstimate(
-            flops=2 * shape[0] * row_count * width,
+            flops=2 * near.shape[0] * row_count * width,
             bytes_accessed=4 * row_count * width,
             transcendentals=0,
         ),
@@ -403,7 +415,7 @@
     grad_far = other_core(grad_near)
     both = assemble(near, far, chips)
     mine = [None] * chips
-    for aways in ([0], [chips - 1], list(range(1, chips - 1))):
+    for aways in ([chips - 1], list(range(1, chips - 1)), [0]):
         results = attend(
             [queries[i] for i in aways], [ends[i] for i in aways], both, width
         )
@@ -413,12 +425,13 @@
     out_width = out_weight.shape[1]
     split = out_width * 11 // 16
     grads = (grad_near, grad_far)
-    *by_chip, turned = weight_gradient(
-        None, *grads, slice(0, split), "seq", chips, planes, (mine, others, chips, width)
+    turned = turn_over(mine, chips, width)
+    *by_chip, far_turned = weight_gradient(
+        turned, None, *grads, slice(0, split), "seq", chips, planes, (others, chips, width)
     )
     gathered = spread(by_chip)
     by_plane = weight_gradient(
-        turned, *grads, slice(split, out_width), "dp", chips, planes
+        turned, far_turned, *grads, slice(split, out_width), "dp", chips, planes
     )
     met = meet(by_plane)
     mixed_out = project(mine, out_weight, chips, width)[None]

time: 97.7 us -> 97.6 us (level)
  transfers between devices with their start and end apart: 33 -> 33, of which waited for: 7 -> 7; matrix products, arithmetic and copies ran while one was open for 0% -> 0% of each run, Pallas kernels for 20% -> 21%
where the time goes in v5:
time: 97.6 us; the launch traced here: 97.4 us
  waiting for transfers between devices  36.9 us (38%)
  starting transfers between devices  34.3 us (35%)
  Pallas kernels  25.3 us (26%)
    ppermute x33, waiting for transfers between devices, over(): return lax.ppermute(value, axis, [(i, i ^ mask) for i in range(size)])  36.9 us
    ppermute x33, starting transfers between devices, over(): return lax.ppermute(value, axis, [(i, i ^ mask) for i in range(size)])  34.3 us
    pallas_call x3, Pallas kernels, attend(): pl.pallas_call(kernel, out_shape=[jax.ShapeDtypeStruct((row_count, width)...  14.1 us
    pallas_call x3, Pallas kernels, cut(): pl.pallas_call(kernel, out_shape=[shape] * len(aways), in_specs=[HBM] * c...  3.82 us
    pallas_call x1, Pallas kernels, project(): pl.pallas_call(kernel, out_shape=jax.ShapeDtypeStruct((row_count, out_wid...  2.93 us
    pallas_call x2, Pallas kernels, weight_gradient(): pl.pallas_call(kernel, out_shape=shapes, in_specs=[VMEM] * (len(sources)...  2.9 us
  transfers between devices with their start and end apart: 33, of which 7 were waited for; matrix products, arithmetic and copies ran while one was open for 0% of the time, Pallas kernels for 21%

profile of v5, /device:TPU:0, one launch (start us, length us, event | category | flops | bytes accessed | tf_op | source)
XLA Modules:
  0.0 97.4 jit_solution(10465294249284385410)
XLA Ops:
  0.6 1.5 %cut.4 = (bf16[384,512]{1,0:T(8,128)(2,1)S(1)}, bf16[384,512]{1,0:T(8,128)(2,1)S(1)}, bf16[384,512]{1,0:T(8,128)(2,1)S(1)}) custom-call(bf16[384,1024]{1,0:T(8,128)(2,1)} %bitcast.13, bf16[384,1024]{1,0:T(8,128)(2,1)} %bitcast.15), custom_call_target="tpu_custom_call" | custom-call | tf_op jit(solution)/shard_map/cut/pallas_call | solution.py:53
  2.2 3.0 %collective-permute-start = (bf16[384,512]{1,0:T(8,128)(2,1)S(1)}, bf16[384,512]{1,0:T(8,128)(2,1)S(1)}, u32[]{:S(2)}, u32[]{:S(2)}) collective-permute-start(bf16[384,512]{1,0:T(8,128)(2,1)S(1)} %get-tuple-element.30), channel_id=1, source_target_pairs={{0,2},{1,3},{2,0},{3,1},{4,6},{5,7},{6,4},{7,5},{8,10},{9,11},{10,... | collective-permute-start | bytes 1179656 | tf_op jit(solution)/shard_map/ppermute | solution.py:396
  5.2 1.5 %collective-permute-start.1 = (bf16[384,512]{1,0:T(8,128)(2,1)S(1)}, bf16[384,512]{1,0:T(8,128)(2,1)S(1)}, u32[]{:S(2)}, u32[]{:S(2)}) collective-permute-start(bf16[384,512]{1,0:T(8,128)(2,1)S(1)} %get-tuple-element.31), channel_id=1, source_target_pairs={{0,4},{1,5},{2,6},{3,7},{4,0},{5,1},{6,2},{7,3},{8,12},{9,13},{10,... | collective-permute-start | bytes 1179656 | tf_op jit(solution)/shard_map/ppermute | solution.py:396
  6.7 1.0 %cut.5 = bf16[384,512]{1,0:T(8,128)(2,1)S(1)} custom-call(bf16[384,1024]{1,0:T(8,128)(2,1)} %bitcast.14, bf16[384,1024]{1,0:T(8,128)(2,1)} %bitcast.16), custom_call_target="tpu_custom_call" | custom-call | tf_op jit(solution)/shard_map/cut/pallas_call | solution.py:53
  8.2 7.0 %collective-permute-done.refs_1_ = bf16[384,512]{1,0:T(8,128)(2,1)S(1)} collective-permute-done((bf16[384,512]{1,0:T(8,128)(2,1)S(1)}, bf16[384,512]{1,0:T(8,128)(2,1)S(1)}, u32[]{:S(2)}, u32[]{:S(2)}) %collective-permute-start) | collective-permute-done | bytes 393248 | tf_op jit(solution)/shard_map/ppermute | solution.py:396
  15.2 10.0 %collective-permute-done.1.refs_2_ = bf16[384,512]{1,0:T(8,128)(2,1)S(1)} collective-permute-done((bf16[384,512]{1,0:T(8,128)(2,1)S(1)}, bf16[384,512]{1,0:T(8,128)(2,1)S(1)}, u32[]{:S(2)}, u32[]{:S(2)}) %collective-permute-start.1) | collective-permute-done | bytes 393248 | tf_op jit(solution)/shard_map/ppermute | solution.py:396
  25.7 1.3 %cut.3 = (bf16[384,256]{1,0:T(8,128)(2,1)S(1)}, bf16[384,256]{1,0:T(8,128)(2,1)S(1)}, bf16[384,256]{1,0:T(8,128)(2,1)S(1)}, bf16[384,256]{1,0:T(8,128)(2,1)S(1)}) custom-call(bf16[384,1024]{1,0:T(8,128)(2,1)} %bitcast.18), custom_call_target="tpu_custom_call" | custom-call | tf_op jit(solution)/shard_map/cut/pallas_call | solution.py:53
  27.0 1.6 %collective-permute-start.10 = (bf16[384,256]{1,0:T(8,128)(2,1)S(1)}, bf16[384,256]{1,0:T(8,128)(2,1)S(1)}, u32[]{:S(2)}, u32[]{:S(2)}) collective-permute-start(bf16[384,256]{1,0:T(8,128)(2,1)S(1)} %get-tuple-element.33), channel_id=1, source_target_pairs={{0,4},{1,5},{2,6},{3,7},{4,0},{5,1},{6,2},{7,3},{8,12},{9,13},{10,... | collective-permute-start | bytes 589832 | tf_op jit(solution)/shard_map/ppermute | solution.py:396
  29.1 1.5 %collective-permute-start.7 = (s32[3,128]{1,0:T(4,128)S(1)}, s32[3,128]{1,0:T(4,128)S(1)}, u32[]{:S(2)}, u32[]{:S(2)}) collective-permute-start(s32[3,128]{1,0:T(4,128)S(1)} %bitcast.9), channel_id=1, source_target_pairs={{0,2},{1,3},{2,0},{3,1},{4,6},{5,7},{6,4},{7,5},{8,10},{9,11},{10,... | collective-permute-start | bytes 4616 | tf_op jit(solution)/shard_map/ppermute | solution.py:396
  31.3 3.8 %collective-permute-done.7.refs_0_ = s32[3,128]{1,0:T(4,128)S(1)} collective-permute-done((s32[3,128]{1,0:T(4,128)S(1)}, s32[3,128]{1,0:T(4,128)S(1)}, u32[]{:S(2)}, u32[]{:S(2)}) %collective-permute-start.7) | collective-permute-done | bytes 1568 | tf_op jit(solution)/shard_map/ppermute | solution.py:396
  35.5 2.6 %collective-permute-start.14 = (bf16[384,256]{1,0:T(8,128)(2,1)S(1)}, bf16[384,256]{1,0:T(8,128)(2,1)S(1)}, u32[]{:S(2)}, u32[]{:S(2)}) collective-permute-start(bf16[384,256]{1,0:T(8,128)(2,1)S(1)} %get-tuple-element.36), channel_id=1, source_target_pairs={{0,6},{1,7},{2,4},{3,5},{4,2},{5,3},{6,0},{7,1},{8,14},{9,15},{10,... | collective-permute-start | bytes 589832 | tf_op jit(solution)/shard_map/ppermute | solution.py:396
  38.1 7.8 %attend.4 = (bf16[384,256]{1,0:T(8,128)(2,1)S(1)}, bf16[384,256]{1,0:T(8,128)(2,1)S(1)}) custom-call(s32[3,128]{1,0:T(4,128)S(1)} %collective-permute-done.7.refs_0_, s32[3,128]{1,0:T(4,128)S(1)} %collective-permute-done.8.refs_1_, bf16[384,256]{1,0:T(8,128)(2,1)S(1)} %collective-permute-done.9.refs_2_, ...), custom_call_target="tpu_custom_call" | custom-call | flops 2415919104 | bytes 3145728 | tf_op jit(solution)/shard_map/attend/pallas_call | solution.py:191
  46.9 4.1 %attend.5 = bf16[384,256]{1,0:T(8,128)(2,1)S(1)} custom-call(s32[3,128]{1,0:T(4,128)S(1)} %collective-permute-done.13.refs_0_, bf16[384,256]{1,0:T(8,128)(2,1)S(1)} %collective-permute-done.14.refs_1_, bf16[3072,512]{1,0:T(8,128)(2,1)S(1)} %assemble.1.refs_2_.refs_4_), custom_call_target="tpu_custom_call" | custom-call | flops 1207959552 | bytes 3145728 | tf_op jit(solution)/shard_map/attend/pallas_call | solution.py:191
  51.8 2.3 %attend.3.refs_0_ = bf16[384,256]{1,0:T(8,128)(2,1)S(1)} custom-call(s32[3,128]{1,0:T(4,128)S(1)} %bitcast.12, bf16[384,256]{1,0:T(8,128)(2,1)S(1)} %get-tuple-element.28.refs_1_, bf16[3072,512]{1,0:T(8,128)(2,1)S(1)} %assemble.1.refs_2_.refs_4_), custom_call_target="tpu_custom_call" | custom-call | flops 1207959552 | bytes 3145728 | tf_op jit(solution)/shard_map/attend/pallas_call | solution.py:191
  54.7 2.9 %collective-permute-done.15.refs_3_ = bf16[384,256]{1,0:T(8,128)(2,1)S(1)} collective-permute-done((bf16[384,256]{1,0:T(8,128)(2,1)S(1)}, bf16[384,256]{1,0:T(8,128)(2,1)S(1)}, u32[]{:S(2)}, u32[]{:S(2)}) %collective-permute-start.15) | collective-permute-done | bytes 196640 | tf_op jit(solution)/shard_map/ppermute | solution.py:396
  57.9 1.1 %collective-permute-done.19.refs_4_ = bf16[384,256]{1,0:T(8,128)(2,1)S(1)} collective-permute-done((bf16[384,256]{1,0:T(8,128)(2,1)S(1)}, bf16[384,256]{1,0:T(8,128)(2,1)S(1)}, u32[]{:S(2)}, u32[]{:S(2)}) %collective-permute-start.19) | collective-permute-done | bytes 196640 | tf_op jit(solution)/shard_map/ppermute | solution.py:396
  59.0 2.0 %weight_gradient.2 = (f32[128,1408]{1,0:T(8,128)S(1)}, bf16[128,1408]{1,0:T(8,128)(2,1)S(1)}, bf16[128,1408]{1,0:T(8,128)(2,1)S(1)}, bf16[128,1408]{1,0:T(8,128)(2,1)S(1)}, bf16[1024,384]{1,0:T(8,128)(2,1)S(1)}) custom-call(bf16[1024,384]{1,0:T(8,128)(2,1)S(1)} %turn_over.1.refs_0_, bf16[384,256]{1,0:T(8,128)(2,1)S(1)} %collective-permute-done.16.refs_1_, ...), custom_call_target="tpu_custom_call" | custom-call | flops 1107296256 | bytes 2162688 | tf_op jit(solution)/shard_map/weight_gradient/pallas_call | solution.py:286
  62.0 1.8 %collective-permute-start.27 = (bf16[128,640]{1,0:T(8,128)(2,1)S(1)}, bf16[128,640]{1,0:T(8,128)(2,1)S(1)}, u32[]{:S(2)}, u32[]{:S(2)}) collective-permute-start(bf16[128,640]{1,0:T(8,128)(2,1)S(1)} %get-tuple-element.47), channel_id=1, source_target_pairs={{0,8},{8,0},{16,24},{24,16},{1,9},{9,1},{17,25},{25,17},{2,10},{10... | collective-permute-start | bytes 491528 | tf_op jit(solution)/shard_map/ppermute | solution.py:396
  63.8 1.0 %collective-permute-start.21 = (bf16[128,1408]{1,0:T(8,128)(2,1)S(1)}, bf16[128,1408]{1,0:T(8,128)(2,1)S(1)}, u32[]{:S(2)}, u32[]{:S(2)}) collective-permute-start(bf16[128,1408]{1,0:T(8,128)(2,1)S(1)} %get-tuple-element.38), channel_id=1, source_target_pairs={{0,2},{1,3},{2,0},{3,1},{4,6},{5,7},{6,4},{7,5},{8,10},{9,11},{10,... | collective-permute-start | bytes 1081352 | tf_op jit(solution)/shard_map/ppermute | solution.py:396
  64.7 1.0 collective-permute-start.22
  65.7 1.6 %collective-permute-start.23 = (bf16[128,1408]{1,0:T(8,128)(2,1)S(1)}, bf16[128,1408]{1,0:T(8,128)(2,1)S(1)}, u32[]{:S(2)}, u32[]{:S(2)}) collective-permute-start(bf16[128,1408]{1,0:T(8,128)(2,1)S(1)} %get-tuple-element.40), channel_id=1, source_target_pairs={{0,6},{1,7},{2,4},{3,5},{4,2},{5,3},{6,0},{7,1},{8,14},{9,15},{10,... | collective-permute-start | bytes 1081352 | tf_op jit(solution)/shard_map/ppermute | solution.py:396
  67.2 2.6 %collective-permute-start.28 = (bf16[128,640]{1,0:T(8,128)(2,1)S(1)}, bf16[128,640]{1,0:T(8,128)(2,1)S(1)}, u32[]{:S(2)}, u32[]{:S(2)}) collective-permute-start(bf16[128,640]{1,0:T(8,128)(2,1)S(1)} %get-tuple-element.48), channel_id=1, source_target_pairs={{0,16},{8,24},{16,0},{24,8},{1,17},{9,25},{17,1},{25,9},{2,18},{10... | collective-permute-start | bytes 491528 | tf_op jit(solution)/shard_map/ppermute | solution.py:396
  69.8 2.2 %collective-permute-start.29 = (bf16[128,640]{1,0:T(8,128)(2,1)S(1)}, bf16[128,640]{1,0:T(8,128)(2,1)S(1)}, u32[]{:S(2)}, u32[]{:S(2)}) collective-permute-start(bf16[128,640]{1,0:T(8,128)(2,1)S(1)} %get-tuple-element.49), channel_id=1, source_target_pairs={{0,24},{8,16},{16,8},{24,0},{1,25},{9,17},{17,9},{25,1},{2,26},{10... | collective-permute-start | bytes 491528 | tf_op jit(solution)/shard_map/ppermute | solution.py:396
  72.0 9.1 %collective-permute-done.28.refs_2_ = bf16[128,640]{1,0:T(8,128)(2,1)S(1)} collective-permute-done((bf16[128,640]{1,0:T(8,128)(2,1)S(1)}, bf16[128,640]{1,0:T(8,128)(2,1)S(1)}, u32[]{:S(2)}, u32[]{:S(2)}) %collective-permute-start.28) | collective-permute-done | bytes 163872 | tf_op jit(solution)/shard_map/ppermute | solution.py:396
  81.2 1.1 %collective-permute-start.30 = (bf16[32,640]{1,0:T(8,128)(2,1)S(1)}, bf16[32,640]{1,0:T(8,128)(2,1)S(1)}, u32[]{:S(2)}, u32[]{:S(2)}) collective-permute-start(bf16[32,640]{1,0:T(8,128)(2,1)S(1)} %get-tuple-element.51), channel_id=1, source_target_pairs={{0,2},{1,3},{2,0},{3,1},{4,6},{5,7},{6,4},{7,5},{8,10},{9,11},{10,... | collective-permute-start | bytes 122888 | tf_op jit(solution)/shard_map/ppermute | solution.py:396
  82.3 1.0 collective-permute-start.31
  83.3 1.5 %collective-permute-start.32 = (bf16[32,640]{1,0:T(8,128)(2,1)S(1)}, bf16[32,640]{1,0:T(8,128)(2,1)S(1)}, u32[]{:S(2)}, u32[]{:S(2)}) collective-permute-start(bf16[32,640]{1,0:T(8,128)(2,1)S(1)} %get-tuple-element.53), channel_id=1, source_target_pairs={{0,6},{1,7},{2,4},{3,5},{4,2},{5,3},{6,0},{7,1},{8,14},{9,15},{10,... | collective-permute-start | bytes 122888 | tf_op jit(solution)/shard_map/ppermute | solution.py:396
  84.9 3.3 %collective-permute-start.24 = (bf16[32,1408]{1,0:T(8,128)(2,1)S(1)}, bf16[32,1408]{1,0:T(8,128)(2,1)S(1)}, u32[]{:S(2)}, u32[]{:S(2)}) collective-permute-start(bf16[32,1408]{1,0:T(8,128)(2,1)S(1)} %get-tuple-element.42), channel_id=1, source_target_pairs={{0,8},{8,0},{16,24},{24,16},{1,9},{9,1},{17,25},{25,17},{2,10},{10... | collective-permute-start | bytes 270344 | tf_op jit(solution)/shard_map/ppermute | solution.py:396
  88.2 1.1 %collective-permute-start.25 = (bf16[32,1408]{1,0:T(8,128)(2,1)S(1)}, bf16[32,1408]{1,0:T(8,128)(2,1)S(1)}, u32[]{:S(2)}, u32[]{:S(2)}) collective-permute-start(bf16[32,1408]{1,0:T(8,128)(2,1)S(1)} %get-tuple-element.43), channel_id=1, source_target_pairs={{0,16},{8,24},{16,0},{24,8},{1,17},{9,25},{17,1},{25,9},{2,18},{10... | collective-permute-start | bytes 270344 | tf_op jit(solution)/shard_map/ppermute | solution.py:396
  89.4 1.4 %collective-permute-start.26 = (bf16[32,1408]{1,0:T(8,128)(2,1)S(1)}, bf16[32,1408]{1,0:T(8,128)(2,1)S(1)}, u32[]{:S(2)}, u32[]{:S(2)}) collective-permute-start(bf16[32,1408]{1,0:T(8,128)(2,1)S(1)} %get-tuple-element.44), channel_id=1, source_target_pairs={{0,24},{8,16},{16,8},{24,0},{1,25},{9,17},{17,9},{25,1},{2,26},{10... | collective-permute-start | bytes 270344 | tf_op jit(solution)/shard_map/ppermute | solution.py:396
  90.8 2.9 %project.1 = bf16[384,2048]{1,0:T(8,128)(2,1)} custom-call(bf16[384,256]{1,0:T(8,128)(2,1)S(1)} %attend.3.refs_0_, bf16[384,256]{1,0:T(8,128)(2,1)S(1)} %collective-permute-done.11.refs_1_, bf16[384,256]{1,0:T(8,128)(2,1)S(1)} %collective-permute-done.12.refs_2_, bf16[384,256]{1,0:T(8,128)(2,1)S(1)} %collective-permute-done.15.refs_3_, ...), custom_call_target="tpu_custom_call" | custom-call | flops 1610612736 | bytes 4194304 | tf_op jit(solution)/shard_map/project/pallas_call | solution.py:322
  93.7 2.9 %collective-permute-done.25.refs_2_ = bf16[32,1408]{1,0:T(8,128)(2,1)S(1)} collective-permute-done((bf16[32,1408]{1,0:T(8,128)(2,1)S(1)}, bf16[32,1408]{1,0:T(8,128)(2,1)S(1)}, u32[]{:S(2)}, u32[]{:S(2)}) %collective-permute-start.25) | collective-permute-done | bytes 90144 | tf_op jit(solution)/shard_map/ppermute | solution.py:396
  (54 shorter events, 7.2 us)
Async XLA Ops:
  2.2 13.0 %collective-permute-start = (bf16[384,512]{1,0:T(8,128)(2,1)S(1)}, bf16[384,512]{1,0:T(8,128)(2,1)S(1)}, u32[]{:S(2)}, u32[]{:S(2)}) collective-permute-start(bf16[384,512]{1,0:T(8,128)(2,1)S(1)} %get-tuple-element.30), channel_id=1, source_target_pairs={{0,2},{1,3},{2,0},{3,1},{4,6},{5,7},{6,4},{7,5},{8,10},{9,11},{10,... | collective-permute-start | bytes 1179656 | tf_op jit(solution)/shard_map/ppermute | solution.py:396
  5.2 53.8 %collective-permute-start.20 = (bf16[384,2048]{1,0:T(8,128)(2,1)S(1)}, bf16[384,2048]{1,0:T(8,128)(2,1)S(1)}, u32[]{:S(2)}, u32[]{:S(2)}) collective-permute-start(bf16[384,2048]{1,0:T(8,128)(2,1)S(1)} %bitcast.6), channel_id=1, source_target_pairs={{0,1},{1,0},{2,3},{3,2},{4,5},{5,4},{6,7},{7,6},{8,9},{9,8},{10,11... | collective-permute-start | bytes 4718600 | tf_op jit(solution)/shard_map/ppermute | solution.py:396
  5.2 20.0 %collective-permute-start.1 = (bf16[384,512]{1,0:T(8,128)(2,1)S(1)}, bf16[384,512]{1,0:T(8,128)(2,1)S(1)}, u32[]{:S(2)}, u32[]{:S(2)}) collective-permute-start(bf16[384,512]{1,0:T(8,128)(2,1)S(1)} %get-tuple-element.31), channel_id=1, source_target_pairs={{0,4},{1,5},{2,6},{3,7},{4,0},{5,1},{6,2},{7,3},{8,12},{9,13},{10,... | collective-permute-start | bytes 1179656 | tf_op jit(solution)/shard_map/ppermute | solution.py:396
  7.8 17.4 %collective-permute-start.2 = (bf16[384,512]{1,0:T(8,128)(2,1)S(1)}, bf16[384,512]{1,0:T(8,128)(2,1)S(1)}, u32[]{:S(2)}, u32[]{:S(2)}) collective-permute-start(bf16[384,512]{1,0:T(8,128)(2,1)S(1)} %cut.5), channel_id=1, source_target_pairs={{0,6},{1,7},{2,4},{3,5},{4,2},{5,3},{6,0},{7,1},{8,14},{9,15},{10,... | collective-permute-start | bytes 1179656 | tf_op jit(solution)/shard_map/ppermute | solution.py:396
  8.1 18.9 %collective-permute-start.3 = (bf16[384,512]{1,0:T(8,128)(2,1)S(1)}, bf16[384,512]{1,0:T(8,128)(2,1)S(1)}, u32[]{:S(2)}, u32[]{:S(2)}) collective-permute-start(bf16[384,512]{1,0:T(8,128)(2,1)S(1)} %get-tuple-element.29.refs_0_), channel_id=1, source_target_pairs={{0,1},{1,0},{2,3},{3,2},{4,5},{5,4},{6,7},{7,6},{8,9},{9,8},{10,11... | collective-permute-start | bytes 1179656 | tf_op jit(solution)/shard_map/ppermute | solution.py:396
  15.2 13.4 %collective-permute-start.4 = (bf16[384,512]{1,0:T(8,128)(2,1)S(1)}, bf16[384,512]{1,0:T(8,128)(2,1)S(1)}, u32[]{:S(2)}, u32[]{:S(2)}) collective-permute-start(bf16[384,512]{1,0:T(8,128)(2,1)S(1)} %collective-permute-done.refs_1_), channel_id=1, source_target_pairs={{0,1},{1,0},{2,3},{3,2},{4,5},{5,4},{6,7},{7,6},{8,9},{9,8},{10,11... | collective-permute-start | bytes 1179656 | tf_op jit(solution)/shard_map/ppermute | solution.py:396
  25.2 3.9 %collective-permute-start.5 = (bf16[384,512]{1,0:T(8,128)(2,1)S(1)}, bf16[384,512]{1,0:T(8,128)(2,1)S(1)}, u32[]{:S(2)}, u32[]{:S(2)}) collective-permute-start(bf16[384,512]{1,0:T(8,128)(2,1)S(1)} %collective-permute-done.1.refs_2_), channel_id=1, source_target_pairs={{0,1},{1,0},{2,3},{3,2},{4,5},{5,4},{6,7},{7,6},{8,9},{9,8},{10,11... | collective-permute-start | bytes 1179656 | tf_op jit(solution)/shard_map/ppermute | solution.py:396
  25.2 5.4 %collective-permute-start.6 = (bf16[384,512]{1,0:T(8,128)(2,1)S(1)}, bf16[384,512]{1,0:T(8,128)(2,1)S(1)}, u32[]{:S(2)}, u32[]{:S(2)}) collective-permute-start(bf16[384,512]{1,0:T(8,128)(2,1)S(1)} %collective-permute-done.2.refs_3_), channel_id=1, source_target_pairs={{0,1},{1,0},{2,3},{3,2},{4,5},{5,4},{6,7},{7,6},{8,9},{9,8},{10,11... | collective-permute-start | bytes 1179656 | tf_op jit(solution)/shard_map/ppermute | solution.py:396
  27.0 11.1 %collective-permute-start.10 = (bf16[384,256]{1,0:T(8,128)(2,1)S(1)}, bf16[384,256]{1,0:T(8,128)(2,1)S(1)}, u32[]{:S(2)}, u32[]{:S(2)}) collective-permute-start(bf16[384,256]{1,0:T(8,128)(2,1)S(1)} %get-tuple-element.33), channel_id=1, source_target_pairs={{0,4},{1,5},{2,6},{3,7},{4,0},{5,1},{6,2},{7,3},{8,12},{9,13},{10,... | collective-permute-start | bytes 589832 | tf_op jit(solution)/shard_map/ppermute | solution.py:396
  28.6 9.5 %collective-permute-start.9 = (bf16[384,256]{1,0:T(8,128)(2,1)S(1)}, bf16[384,256]{1,0:T(8,128)(2,1)S(1)}, u32[]{:S(2)}, u32[]{:S(2)}) collective-permute-start(bf16[384,256]{1,0:T(8,128)(2,1)S(1)} %get-tuple-element.32), channel_id=1, source_target_pairs={{0,2},{1,3},{2,0},{3,1},{4,6},{5,7},{6,4},{7,5},{8,10},{9,11},{10,... | collective-permute-start | bytes 589832 | tf_op jit(solution)/shard_map/ppermute | solution.py:396
  29.1 6.0 %collective-permute-start.7 = (s32[3,128]{1,0:T(4,128)S(1)}, s32[3,128]{1,0:T(4,128)S(1)}, u32[]{:S(2)}, u32[]{:S(2)}) collective-permute-start(s32[3,128]{1,0:T(4,128)S(1)} %bitcast.9), channel_id=1, source_target_pairs={{0,2},{1,3},{2,0},{3,1},{4,6},{5,7},{6,4},{7,5},{8,10},{9,11},{10,... | collective-permute-start | bytes 4616 | tf_op jit(solution)/shard_map/ppermute | solution.py:396
  30.6 4.9 %collective-permute-start.8 = (s32[3,128]{1,0:T(4,128)S(1)}, s32[3,128]{1,0:T(4,128)S(1)}, u32[]{:S(2)}, u32[]{:S(2)}) collective-permute-start(s32[3,128]{1,0:T(4,128)S(1)} %bitcast.10), channel_id=1, source_target_pairs={{0,4},{1,5},{2,6},{3,7},{4,0},{5,1},{6,2},{7,3},{8,12},{9,13},{10,... | collective-permute-start | bytes 4616 | tf_op jit(solution)/shard_map/ppermute | solution.py:396
  35.1 11.8 %collective-permute-start.13 = (s32[3,128]{1,0:T(4,128)S(1)}, s32[3,128]{1,0:T(4,128)S(1)}, u32[]{:S(2)}, u32[]{:S(2)}) collective-permute-start(s32[3,128]{1,0:T(4,128)S(1)} %bitcast.11), channel_id=1, source_target_pairs={{0,6},{1,7},{2,4},{3,5},{4,2},{5,3},{6,0},{7,1},{8,14},{9,15},{10,... | collective-permute-start | bytes 4616 | tf_op jit(solution)/shard_map/ppermute | solution.py:396
  35.5 11.4 %collective-permute-start.14 = (bf16[384,256]{1,0:T(8,128)(2,1)S(1)}, bf16[384,256]{1,0:T(8,128)(2,1)S(1)}, u32[]{:S(2)}, u32[]{:S(2)}) collective-permute-start(bf16[384,256]{1,0:T(8,128)(2,1)S(1)} %get-tuple-element.36), channel_id=1, source_target_pairs={{0,6},{1,7},{2,4},{3,5},{4,2},{5,3},{6,0},{7,1},{8,14},{9,15},{10,... | collective-permute-start | bytes 589832 | tf_op jit(solution)/shard_map/ppermute | solution.py:396
  45.9 8.2 %collective-permute-start.11 = (bf16[384,256]{1,0:T(8,128)(2,1)S(1)}, bf16[384,256]{1,0:T(8,128)(2,1)S(1)}, u32[]{:S(2)}, u32[]{:S(2)}) collective-permute-start(bf16[384,256]{1,0:T(8,128)(2,1)S(1)} %get-tuple-element.34), channel_id=1, source_target_pairs={{0,2},{1,3},{2,0},{3,1},{4,6},{5,7},{6,4},{7,5},{8,10},{9,11},{10,... | collective-permute-start | bytes 589832 | tf_op jit(solution)/shard_map/ppermute | solution.py:396
  46.0 8.6 %collective-permute-start.12 = (bf16[384,256]{1,0:T(8,128)(2,1)S(1)}, bf16[384,256]{1,0:T(8,128)(2,1)S(1)}, u32[]{:S(2)}, u32[]{:S(2)}) collective-permute-start(bf16[384,256]{1,0:T(8,128)(2,1)S(1)} %get-tuple-element.35), channel_id=1, source_target_pairs={{0,4},{1,5},{2,6},{3,7},{4,0},{5,1},{6,2},{7,3},{8,12},{9,13},{10,... | collective-permute-start | bytes 589832 | tf_op jit(solution)/shard_map/ppermute | solution.py:396
  51.0 6.6 %collective-permute-start.15 = (bf16[384,256]{1,0:T(8,128)(2,1)S(1)}, bf16[384,256]{1,0:T(8,128)(2,1)S(1)}, u32[]{:S(2)}, u32[]{:S(2)}) collective-permute-start(bf16[384,256]{1,0:T(8,128)(2,1)S(1)} %attend.5), channel_id=1, source_target_pairs={{0,6},{1,7},{2,4},{3,5},{4,2},{5,3},{6,0},{7,1},{8,14},{9,15},{10,... | collective-permute-start | bytes 589832 | tf_op jit(solution)/shard_map/ppermute | solution.py:396
  54.0 3.8 %collective-permute-start.16 = (bf16[384,256]{1,0:T(8,128)(2,1)S(1)}, bf16[384,256]{1,0:T(8,128)(2,1)S(1)}, u32[]{:S(2)}, u32[]{:S(2)}) collective-permute-start(bf16[384,256]{1,0:T(8,128)(2,1)S(1)} %attend.3.refs_0_), channel_id=1, source_target_pairs={{0,1},{1,0},{2,3},{3,2},{4,5},{5,4},{6,7},{7,6},{8,9},{9,8},{10,11... | collective-permute-start | bytes 589832 | tf_op jit(solution)/shard_map/ppermute | solution.py:396
  54.1 3.8 %collective-permute-start.17 = (bf16[384,256]{1,0:T(8,128)(2,1)S(1)}, bf16[384,256]{1,0:T(8,128)(2,1)S(1)}, u32[]{:S(2)}, u32[]{:S(2)}) collective-permute-start(bf16[384,256]{1,0:T(8,128)(2,1)S(1)} %collective-permute-done.11.refs_1_), channel_id=1, source_target_pairs={{0,1},{1,0},{2,3},{3,2},{4,5},{5,4},{6,7},{7,6},{8,9},{9,8},{10,11... | collective-permute-start | bytes 589832 | tf_op jit(solution)/shard_map/ppermute | solution.py:396
  54.6 3.3 %collective-permute-start.18 = (bf16[384,256]{1,0:T(8,128)(2,1)S(1)}, bf16[384,256]{1,0:T(8,128)(2,1)S(1)}, u32[]{:S(2)}, u32[]{:S(2)}) collective-permute-start(bf16[384,256]{1,0:T(8,128)(2,1)S(1)} %collective-permute-done.12.refs_2_), channel_id=1, source_target_pairs={{0,1},{1,0},{2,3},{3,2},{4,5},{5,4},{6,7},{7,6},{8,9},{9,8},{10,11... | collective-permute-start | bytes 589832 | tf_op jit(solution)/shard_map/ppermute | solution.py:396
  62.0 7.9 %collective-permute-start.27 = (bf16[128,640]{1,0:T(8,128)(2,1)S(1)}, bf16[128,640]{1,0:T(8,128)(2,1)S(1)}, u32[]{:S(2)}, u32[]{:S(2)}) collective-permute-start(bf16[128,640]{1,0:T(8,128)(2,1)S(1)} %get-tuple-element.47), channel_id=1, source_target_pairs={{0,8},{8,0},{16,24},{24,16},{1,9},{9,1},{17,25},{25,17},{2,10},{10... | collective-permute-start | bytes 491528 | tf_op jit(solution)/shard_map/ppermute | solution.py:396
  63.8 19.5 %collective-permute-start.21 = (bf16[128,1408]{1,0:T(8,128)(2,1)S(1)}, bf16[128,1408]{1,0:T(8,128)(2,1)S(1)}, u32[]{:S(2)}, u32[]{:S(2)}) collective-permute-start(bf16[128,1408]{1,0:T(8,128)(2,1)S(1)} %get-tuple-element.38), channel_id=1, source_target_pairs={{0,2},{1,3},{2,0},{3,1},{4,6},{5,7},{6,4},{7,5},{8,10},{9,11},{10,... | collective-permute-start | bytes 1081352 | tf_op jit(solution)/shard_map/ppermute | solution.py:396
  64.7 20.0 %collective-permute-start.22 = (bf16[128,1408]{1,0:T(8,128)(2,1)S(1)}, bf16[128,1408]{1,0:T(8,128)(2,1)S(1)}, u32[]{:S(2)}, u32[]{:S(2)}) collective-permute-start(bf16[128,1408]{1,0:T(8,128)(2,1)S(1)} %get-tuple-element.39), channel_id=1, source_target_pairs={{0,4},{1,5},{2,6},{3,7},{4,0},{5,1},{6,2},{7,3},{8,12},{9,13},{10,... | collective-permute-start | bytes 1081352 | tf_op jit(solution)/shard_map/ppermute | solution.py:396
  65.7 19.1 %collective-permute-start.23 = (bf16[128,1408]{1,0:T(8,128)(2,1)S(1)}, bf16[128,1408]{1,0:T(8,128)(2,1)S(1)}, u32[]{:S(2)}, u32[]{:S(2)}) collective-permute-start(bf16[128,1408]{1,0:T(8,128)(2,1)S(1)} %get-tuple-element.40), channel_id=1, source_target_pairs={{0,6},{1,7},{2,4},{3,5},{4,2},{5,3},{6,0},{7,1},{8,14},{9,15},{10,... | collective-permute-start | bytes 1081352 | tf_op jit(solution)/shard_map/ppermute | solution.py:396
  67.2 13.9 %collective-permute-start.28 = (bf16[128,640]{1,0:T(8,128)(2,1)S(1)}, bf16[128,640]{1,0:T(8,128)(2,1)S(1)}, u32[]{:S(2)}, u32[]{:S(2)}) collective-permute-start(bf16[128,640]{1,0:T(8,128)(2,1)S(1)} %get-tuple-element.48), channel_id=1, source_target_pairs={{0,16},{8,24},{16,0},{24,8},{1,17},{9,25},{17,1},{25,9},{2,18},{10... | collective-permute-start | bytes 491528 | tf_op jit(solution)/shard_map/ppermute | solution.py:396
  69.8 11.3 %collective-permute-start.29 = (bf16[128,640]{1,0:T(8,128)(2,1)S(1)}, bf16[128,640]{1,0:T(8,128)(2,1)S(1)}, u32[]{:S(2)}, u32[]{:S(2)}) collective-permute-start(bf16[128,640]{1,0:T(8,128)(2,1)S(1)} %get-tuple-element.49), channel_id=1, source_target_pairs={{0,24},{8,16},{16,8},{24,0},{1,25},{9,17},{17,9},{25,1},{2,26},{10... | collective-permute-start | bytes 491528 | tf_op jit(solution)/shard_map/ppermute | solution.py:396
  81.2 8.2 %collective-permute-start.30 = (bf16[32,640]{1,0:T(8,128)(2,1)S(1)}, bf16[32,640]{1,0:T(8,128)(2,1)S(1)}, u32[]{:S(2)}, u32[]{:S(2)}) collective-permute-start(bf16[32,640]{1,0:T(8,128)(2,1)S(1)} %get-tuple-element.51), channel_id=1, source_target_pairs={{0,2},{1,3},{2,0},{3,1},{4,6},{5,7},{6,4},{7,5},{8,10},{9,11},{10,... | collective-permute-start | bytes 122888 | tf_op jit(solution)/shard_map/ppermute | solution.py:396
  82.3 11.4 %collective-permute-start.31 = (bf16[32,640]{1,0:T(8,128)(2,1)S(1)}, bf16[32,640]{1,0:T(8,128)(2,1)S(1)}, u32[]{:S(2)}, u32[]{:S(2)}) collective-permute-start(bf16[32,640]{1,0:T(8,128)(2,1)S(1)} %get-tuple-element.52), channel_id=1, source_target_pairs={{0,4},{1,5},{2,6},{3,7},{4,0},{5,1},{6,2},{7,3},{8,12},{9,13},{10,... | collective-permute-start | bytes 122888 | tf_op jit(solution)/shard_map/ppermute | solution.py:396
  83.3 10.4 %collective-permute-start.32 = (bf16[32,640]{1,0:T(8,128)(2,1)S(1)}, bf16[32,640]{1,0:T(8,128)(2,1)S(1)}, u32[]{:S(2)}, u32[]{:S(2)}) collective-permute-start(bf16[32,640]{1,0:T(8,128)(2,1)S(1)} %get-tuple-element.53), channel_id=1, source_target_pairs={{0,6},{1,7},{2,4},{3,5},{4,2},{5,3},{6,0},{7,1},{8,14},{9,15},{10,... | collective-permute-start | bytes 122888 | tf_op jit(solution)/shard_map/ppermute | solution.py:396
  84.9 8.8 %collective-permute-start.24 = (bf16[32,1408]{1,0:T(8,128)(2,1)S(1)}, bf16[32,1408]{1,0:T(8,128)(2,1)S(1)}, u32[]{:S(2)}, u32[]{:S(2)}) collective-permute-start(bf16[32,1408]{1,0:T(8,128)(2,1)S(1)} %get-tuple-element.42), channel_id=1, source_target_pairs={{0,8},{8,0},{16,24},{24,16},{1,9},{9,1},{17,25},{25,17},{2,10},{10... | collective-permute-start | bytes 270344 | tf_op jit(solution)/shard_map/ppermute | solution.py:396
  88.2 8.4 %collective-permute-start.25 = (bf16[32,1408]{1,0:T(8,128)(2,1)S(1)}, bf16[32,1408]{1,0:T(8,128)(2,1)S(1)}, u32[]{:S(2)}, u32[]{:S(2)}) collective-permute-start(bf16[32,1408]{1,0:T(8,128)(2,1)S(1)} %get-tuple-element.43), channel_id=1, source_target_pairs={{0,16},{8,24},{16,0},{24,8},{1,17},{9,25},{17,1},{25,9},{2,18},{10... | collective-permute-start | bytes 270344 | tf_op jit(solution)/shard_map/ppermute | solution.py:396
  89.4 7.3 %collective-permute-start.26 = (bf16[32,1408]{1,0:T(8,128)(2,1)S(1)}, bf16[32,1408]{1,0:T(8,128)(2,1)S(1)}, u32[]{:S(2)}, u32[]{:S(2)}) collective-permute-start(bf16[32,1408]{1,0:T(8,128)(2,1)S(1)} %get-tuple-element.44), channel_id=1, source_target_pairs={{0,24},{8,16},{16,8},{24,0},{1,25},{9,17},{17,9},{25,1},{2,26},{10... | collective-permute-start | bytes 270344 | tf_op jit(solution)/shard_map/ppermute | solution.py:396
  (4 other events, 62.7 us)
